TPU v7x, 32 devices: a whole 2x2x4 slice. The times are simulated.
32 devices in a mesh: freq: 4 (over z), cell: 8 (over y, x, core).
Axes of the slice: x: 2, y: 2, z: 4, core: 2. Of those that a mesh axis runs over, the one named last changes fastest.
Arguments:
- green: bfloat16 [2, 8, 1024, 4096], P(None, 'freq', None, 'cell'), may hold values from -0.25 to 0.25
- coeffs: float32 [8, 4096], P('freq', 'cell'), may hold values from -6 to 6
- basis: float32 [8, 8], P('freq'), may hold values from -2 to 2
- amplitude: float32 [8, 1024], P('freq'), may hold values from 0.5 to 2
- block_mask: int32 [16, 16], replicated, may hold values 0 or 1
Outputs:
- hess_vec: float32 [8, 4096], P('freq', 'cell')
All inputs are finite; a program needn't handle non-finite values.
Results may differ from a plain program's by a relative error of at most 0.0024.
Values may be sent and summed in bfloat16 or wider, within the bound.
No kernel may reach another device: no remote copies, remote signals or barrier semaphores. Data moves between devices by JAX's collectives and lax.ppermute only.
A program may use at most 192 MiB of HBM per device.

v0:
```python
import jax
import jax.numpy as jnp
from jax import lax
from jax.sharding import PartitionSpec as P

NS = 1024


def whiten(corr, amplitude, expanded):
    weight = amplitude.T[:, :, None] * amplitude[None, :, :] * expanded[:, None, :]
    return (weight[:, :, None, :] * corr).astype(jnp.bfloat16)


def on_device(green, coeffs, basis, amplitude, block_mask):
    highest = lax.Precision.HIGHEST
    full = lax.all_gather(coeffs, "freq", axis=0, tiled=True)
    source = jnp.dot(basis, full, precision=highest)
    scaled = (green * source[None, :, None, :]).astype(jnp.bfloat16)
    right = jnp.stack((jnp.stack((green[0], green[1])), jnp.stack((-green[1], green[0]))))
    blocks = block_mask.shape[0]
    width = NS // blocks
    expanded = (
        jnp.broadcast_to(block_mask[:, None, :, None], (blocks, width, blocks, width))
        .reshape(NS, NS)
        .astype(jnp.float32)
    )
    total = lax.psum(
        jnp.einsum("pfic,qpfjc->ifqj", scaled, right, preferred_element_type=jnp.float32).astype(
            jnp.bfloat16
        ),
        "cell",
    ).astype(jnp.float32)
    resid = whiten(total, amplitude, expanded)
    yre = jnp.einsum("ifj,fjc->fic", resid[:, :, 0], green[0], preferred_element_type=jnp.float32)
    yre = yre - jnp.einsum(
        "ifj,fjc->fic", resid[:, :, 1], green[1], preferred_element_type=jnp.float32
    )
    yim = jnp.einsum("ifj,fjc->fic", resid[:, :, 0], green[1], preferred_element_type=jnp.float32)
    yim = yim + jnp.einsum(
        "ifj,fjc->fic", resid[:, :, 1], green[0], preferred_element_type=jnp.float32
    )
    sens = jnp.sum(green[0] * yre + green[1] * yim, axis=1)
    partial_value = jnp.dot(basis.T, sens, precision=highest)
    return lax.psum_scatter(partial_value, "freq", scatter_dimension=0, tiled=True)


def solution(mesh):
    placed = (
        P(None, "freq", None, "cell"),
        P("freq", "cell"),
        P("freq", None),
        P("freq", None),
        P(),
    )
    return jax.shard_map(
        on_device, mesh=mesh, in_specs=placed, out_specs=P("freq", "cell"), check_vma=False
    )
```

profile of v0, /device:TPU:0, one launch (start us, length us, event | category | flops | bytes accessed | tf_op | source)
XLA Modules:
  0.0 226.7 jit_solution(2647136355200068773)
XLA Ops:
  6.5 0.0 copy-start
  6.5 0.0 all-reduce.3.cloned.1.call-start
  6.5 0.0 copy-start.1
  6.5 2.6 %copy.24 = bf16[2,2,1024,512]{3,2,0,1:T(8,128)(2,1)S(1)} copy(bf16[2,2,1024,512]{3,2,1,0:T(8,128)(2,1)} %param.5) | data formatting | bytes 8388608 | tf_op args[0]
  9.2 0.8 copy-done.1
  10.0 0.0 copy-start.4
  10.0 0.0 copy-start.10
  10.0 0.1 negate_bitcast_fusion
  10.1 1.7 slice.13
  11.8 0.9 copy-done.4
  12.7 0.0 copy-done.10
  12.7 14.9 %all-gather = f32[4,2,512]{2,1,0:T(2,128)S(1)} all-gather(f32[1,2,512]{2,1,0:T(2,128)S(1)} %bitcast.57), channel_id=1, replica_groups=mesh['freq'=4,'cell'=8] {'freq'}, dimensions={0}, use_global_device_ids=true | all-gather | bytes 20480 | tf_op jit(solution)/shard_map/all_gather | solution.py:16
  27.6 0.0 copy-start.2
  27.6 0.0 copy-start.5
  27.6 4.3 %maximum_bitcast_fusion = bf16[1,2,2,1024,512]{4,3,1,0,2:T(8,128)(2,1)} fusion(bf16[1,2,1024,512]{3,2,0,1:T(8,128)(2,1)} %slice.13, bf16[1,2,1024,512]{3,2,0,1:T(8,128)(2,1)S(1)} %negate_bitcast_fusion), kind=kLoop, calls=%fused_computation.12 | loop fusion | flops 2097152 | bytes 8388608 | tf_op jit(solution)/shard_map/stack | solution.py:19
  31.9 0.0 copy-done
  31.9 0.1 fusion.24
  32.0 0.0 copy-done.2
  32.0 1.2 copy-done.5
  33.2 13.5 %fusion = bf16[1024,2,2,1024]{0,3,2,1:T(8,128)(2,1)} fusion(bf16[1,2,2,1024,512]{4,3,1,0,2:T(8,128)(2,1)} %maximum_bitcast_fusion, bf16[1,2,2,1024,512]{4,3,1,0,2:T(8,128)(2,1)S(1)} %bitcast.55, bf16[2,2,1024,512]{3,2,1,0:T(8,128)(2,1)S(1)} %copy-done.2, f32[2,512]{1,0:T(2,128)S(1)} %fusion.24), kind=kOutput, calls=%fused_computation.2 | convolution fusion | flops 8604614656 | bytes 20975616 | tf_op jit(solution)/shard_map/pfic,qpfjc->ifqj/dot_general | solution.py:28
  46.7 0.0 copy-start.9
  46.7 0.0 all-reduce.3.cloned.1.call-update
  46.8 0.7 copy-done.9
  47.4 0.1 copy.12
  47.5 3.8 %broadcast_in_dim.2 = f32[16,64,16,64]{1,0,3,2:T(8,128)} broadcast(f32[16,16]{0,1:T(8,128)S(1)} %copy.12), dimensions={0,2} | broadcast | bytes 4195328 | tf_op jit(solution)/shard_map/broadcast_in_dim | solution.py:23
  51.3 0.0 copy-start.11
  51.3 0.0 copy-start.8
  51.3 7.7 %convert_element_type.37 = f32[1024,1024]{0,1:T(8,128)} reshape(f32[16,64,16,64]{1,0,3,2:T(8,128)} %broadcast_in_dim.2) | data formatting | bytes 8388608 | tf_op jit(solution)/shard_map/convert_element_type | solution.py:25
  59.0 0.0 copy-done.11
  59.0 0.6 dynamic-slice
  60.3 0.0 copy-done.8
  60.3 5.4 %multiply_multiply_fusion = f32[1024,2,1024]{0,2,1:T(8,128)} fusion(f32[1024,1024]{0,1:T(8,128)} %convert_element_type.37, f32[2,1024]{1,0:T(2,128)S(1)} %copy-done.8, f32[1024,2]{0,1:T(2,128)S(1)} %bitcast.56), kind=kLoop, calls=%fused_computation.8 | loop fusion | flops 4194304 | bytes 12599296 | tf_op jit(solution)/shard_map/mul | solution.py:10
  65.6 108.5 %all-reduce.3.cloned.1.call-done = bf16[1024,2,2,1024]{0,3,2,1:T(8,128)(2,1)} async-done(((bf16[1024,2,2,1024]{0,3,2,1:T(8,128)(2,1)}), bf16[1024,2,2,1024]{0,3,2,1:T(8,128)(2,1)}) %all-reduce.3.cloned.1.call-update) | async-done | bytes 8388624 | tf_op jit(solution)/shard_map/psum | solution.py:27
  174.1 0.0 copy-start.6
  174.1 7.6 %multiply_convert_fusion = bf16[1024,2,2,1024]{0,3,2,1:T(8,128)(2,1)S(1)} fusion(bf16[1024,2,2,1024]{0,3,2,1:T(8,128)(2,1)} %all-reduce.3.cloned.1.call-done, f32[1024,2,1024]{0,2,1:T(8,128)} %multiply_multiply_fusion), kind=kLoop, calls=%fused_computation.1 | loop fusion | flops 12582912 | bytes 25165824 | tf_op jit(solution)/shard_map/convert_element_type | solution.py:11
  181.7 0.0 copy-done.6
  181.7 0.0 copy-start.7
  181.7 2.4 %fusion.10 = f32[2,1024,512]{2,1,0:T(8,128)S(1)} fusion(bf16[1024,2,2,1024]{0,3,2,1:T(8,128)(2,1)S(1)} %multiply_convert_fusion, bf16[2,2,1024,512]{3,2,0,1:T(8,128)(2,1)S(1)} %copy-done.6), kind=kOutput, calls=%fused_computation.16 | convolution fusion | flops 2147483648 | bytes 10485760 | tf_op jit(solution)/shard_map/ifj,fjc->fic/dot_general | solution.py:34
  184.1 0.0 copy-start.3
  184.1 4.3 %fusion.11 = f32[2,1024,512]{2,1,0:T(8,128)} fusion(bf16[1024,2,2,1024]{0,3,2,1:T(8,128)(2,1)S(1)} %multiply_convert_fusion, bf16[2,2,1024,512]{3,2,0,1:T(8,128)(2,1)S(1)} %copy-done.6), kind=kOutput, calls=%fused_computation.17 | convolution fusion | flops 2147483648 | bytes 10485760 | tf_op jit(solution)/shard_map/ifj,fjc->fic/dot_general | solution.py:39
  188.4 0.0 copy-done.7
  188.4 0.0 copy-done.3
  188.4 4.3 %fusion.9 = f32[2,1024,512]{2,1,0:T(8,128)} fusion(bf16[1024,2,2,1024]{0,3,2,1:T(8,128)(2,1)S(1)} %multiply_convert_fusion, bf16[2,2,1024,512]{3,2,1,0:T(8,128)(2,1)S(1)} %copy-done.3), kind=kOutput, calls=%fused_computation.15 | convolution fusion | flops 2147483648 | bytes 10485760 | tf_op jit(solution)/shard_map/ifj,fjc->fic/dot_general | solution.py:38
  192.8 7.6 %add_reduce_fusion = f32[2,512]{1,0:T(2,128)S(1)} fusion(f32[2,1024,512]{2,1,0:T(8,128)} %fusion.9, f32[2,1024,512]{2,1,0:T(8,128)} %fusion.11, f32[2,1024,512]{2,1,0:T(8,128)S(1)} %fusion.10, bf16[1024,2,2,1024]{0,3,2,1:T(8,128)(2,1)} %copy-done.7, bf16[2,2,1024,512]{3,2,1,0:T(8,128)(2,1)S(1)} %copy-done.3, bf16[2,2,1024,512]{3,2,0,1:T(8,128)(2,1)S(1)} %copy-done.6), kind=kOutput, calls=%fused_computation.14 | convolution fusion | flops 2155871232 | bytes 23072768 | tf_op jit(solution)/shard_map/ifj,fjc->fic/dot_general | solution.py:35
  200.3 0.2 convolution_bitcast_fusion
  200.5 18.7 %all-reduce = f32[8,512]{1,0:T(8,128)S(1)} all-reduce(f32[8,512]{1,0:T(8,128)S(1)} %convolution_bitcast_fusion), channel_id=2, replica_groups=mesh['freq'=4,'cell'=8] {'freq'}, use_global_device_ids=true, to_apply=%region_2.0.clone | all-reduce | flops 4096 | bytes 32768
  219.3 0.6 constant_dynamic-slice_fusion
  (2 shorter events, 0.0 us)
Async XLA Ops:
  6.5 25.4 %copy-start = (f32[2,8]{1,0:T(2,128)S(1)}, f32[2,8]{1,0:T(2,128)}, u32[]{:S(2)}) copy-start(f32[2,8]{1,0:T(2,128)} %param.7) | copy-start | bytes 196
  6.5 167.6 %all-reduce.3.cloned.1.call-start = ((), (), s32[]{:S(2)}) async-start(), calls=%async_computation | async-start | bytes 16777216 | tf_op jit(solution)/shard_map/psum | solution.py:27
  6.5 3.5 %copy-start.1 = (bf16[2,2,1024,512]{3,2,1,0:T(8,128)(2,1)S(1)}, bf16[2,2,1024,512]{3,2,1,0:T(8,128)(2,1)}, u32[]{:S(2)}) copy-start(bf16[2,2,1024,512]{3,2,1,0:T(8,128)(2,1)} %param.5) | copy-start | bytes 12582916
  10.0 2.7 %copy-start.4 = (bf16[2,2,1024,512]{3,2,0,1:T(8,128)(2,1)}, bf16[2,2,1024,512]{3,2,0,1:T(8,128)(2,1)S(1)}, u32[]{:S(2)}) copy-start(bf16[2,2,1024,512]{3,2,0,1:T(8,128)(2,1)S(1)} %copy.24) | copy-start | bytes 12582916
  10.0 2.7 %copy-start.10 = (f32[2,512]{1,0:T(2,128)S(1)}, f32[2,512]{1,0:T(2,128)}, u32[]{:S(2)}) copy-start(f32[2,512]{1,0:T(2,128)} %param.6) | copy-start | bytes 12292
  27.6 4.4 %copy-start.2 = (bf16[2,2,1024,512]{3,2,1,0:T(8,128)(2,1)S(1)}, bf16[2,2,1024,512]{3,2,1,0:T(8,128)(2,1)}, u32[]{:S(2)}) copy-start(bf16[2,2,1024,512]{3,2,1,0:T(8,128)(2,1)} %param.5) | copy-start | bytes 12582916
  27.6 5.6 %copy-start.5 = (bf16[2,2,1024,512]{3,2,0,1:T(8,128)(2,1)S(1)}, bf16[2,2,1024,512]{3,2,0,1:T(8,128)(2,1)}, u32[]{:S(2)}) copy-start(bf16[2,2,1024,512]{3,2,0,1:T(8,128)(2,1)} %copy-done.4) | copy-start | bytes 12582916
  46.7 0.7 copy-start.9
  51.3 7.7 %copy-start.11 = (u32[32]{0:T(128)S(1)}, u32[32]{0:T(128)}, u32[]{:S(2)}) copy-start(u32[32]{0:T(128)} %constant.8) | copy-start | bytes 388
  51.3 8.9 %copy-start.8 = (f32[2,1024]{1,0:T(2,128)S(1)}, f32[2,1024]{1,0:T(2,128)}, u32[]{:S(2)}) copy-start(f32[2,1024]{1,0:T(2,128)} %param.8) | copy-start | bytes 24580
  174.1 7.6 %copy-start.6 = (bf16[2,2,1024,512]{3,2,0,1:T(8,128)(2,1)S(1)}, bf16[2,2,1024,512]{3,2,0,1:T(8,128)(2,1)}, u32[]{:S(2)}) copy-start(bf16[2,2,1024,512]{3,2,0,1:T(8,128)(2,1)} %copy-done.4) | copy-start | bytes 12582916
  181.7 6.7 %copy-start.7 = (bf16[1024,2,2,1024]{0,3,2,1:T(8,128)(2,1)}, bf16[1024,2,2,1024]{0,3,2,1:T(8,128)(2,1)S(1)}, u32[]{:S(2)}) copy-start(bf16[1024,2,2,1024]{0,3,2,1:T(8,128)(2,1)S(1)} %multiply_convert_fusion) | copy-start | bytes 25165828
  184.1 4.3 %copy-start.3 = (bf16[2,2,1024,512]{3,2,1,0:T(8,128)(2,1)S(1)}, bf16[2,2,1024,512]{3,2,1,0:T(8,128)(2,1)}, u32[]{:S(2)}) copy-start(bf16[2,2,1024,512]{3,2,1,0:T(8,128)(2,1)} %param.5) | copy-start | bytes 12582916
Sparse Core Ops, SparseCore 0:
  46.9 127.1 all-reduce.2
where the time goes:
time: 227 us
  waiting for transfers between devices  108 us (48%)
  blocking collectives  33.6 us (15%)
  matrix products  32.4 us (14%)
  local copies, waits for them, and re-layouts  20.7 us (9%)
  other arithmetic  17.3 us (8%)
  between operations  14.1 us (6%)
    psum x1, waiting for transfers between devices, on_device(): lax.psum(jnp.einsum('pfic,qpfjc->ifqj', scaled, right, preferred_element_...  108 us
    unnamed x1, blocking collectives  18.7 us
    all_gather x1, blocking collectives, on_device(): full = lax.all_gather(coeffs, 'freq', axis=0, tiled=True)  14.9 us
    dot_general x1, matrix products, on_device(): jnp.einsum('pfic,qpfjc->ifqj', scaled, right, preferred_element_type=jnp....  13.5 us
    convert_element_type x2, local copies, waits for them, and re-layouts, on_device(): expanded = jnp.broadcast_to(block_mask[:, None, :, None], (blocks, width,...  7.77 us
    convert_element_type x1, other arithmetic, whiten(): return (weight[:, :, None, :] * corr).astype(jnp.bfloat16)  7.57 us
    dot_general x1, matrix products, on_device(): jnp.einsum('ifj,fjc->fic', resid[:, :, 1], green[1], preferred_element_ty...  7.55 us
    unnamed x28, local copies, waits for them, and re-layouts  7.42 us
  transfers between devices with their start and end apart: 1, of which 1 were waited for; matrix products, arithmetic and copies ran while one was open for 8% of the time, Pallas kernels for 0%

commit v1 on v0

v1 whole, which is shorter than its diff:
```python
import functools

import jax
import jax.numpy as jnp
from jax import lax
from jax.experimental import pallas as pl
from jax.experimental.pallas import tpu as pltpu
from jax.sharding import PartitionSpec as P

F32 = jnp.float32
BF16 = jnp.bfloat16
MIB = 1 << 20


def across(left, right):
    return lax.dot_general(left, right, (((1,), (1,)), ((), ())), preferred_element_type=F32)


def along(left, right):
    return jnp.dot(left, right, preferred_element_type=F32)


def corr_kernel(n, piece_ref, source_ref, green_ref, out_ref):
    stations, width = green_ref.shape
    tile, half = stations // n, width // 2
    piece = piece_ref[0]

    def block(d):
        start = lax.rem(piece + d, n) * tile
        return green_ref[pl.ds(pl.multiple_of(start, tile), tile), :]

    scaled = (block(0).astype(F32) * source_ref[...]).astype(BF16)
    turned = jnp.concatenate((scaled[:, half:], -scaled[:, :half]), axis=1)
    both = jnp.concatenate((scaled, turned), axis=0)
    pair = across(both, block(0))
    row = lax.broadcasted_iota(jnp.int32, (tile, tile), 0)
    col = lax.broadcasted_iota(jnp.int32, (tile, tile), 1)
    out_ref[:, :tile] = jnp.where(row >= col, pair[:tile], pair[tile:]).astype(out_ref.dtype)
    for d in range(1, n // 2):
        pair = across(both, block(d)).astype(out_ref.dtype)
        out_ref[:, (2 * d - 1) * tile : 2 * d * tile] = pair[:tile]
        out_ref[:, 2 * d * tile : (2 * d + 1) * tile] = pair[tile:]
    last = across(jnp.where(piece < n // 2, scaled, turned), block(n // 2))
    out_ref[:, (n - 1) * tile :] = last.astype(out_ref.dtype)


def sens_kernel(n, step, piece_ref, resid_ref, green_ref, out_ref):
    stations, width = green_ref.shape
    tile, half = stations // n, width // 2
    piece = piece_ref[0]
    starts = [pl.multiple_of(lax.rem(piece + d, n) * tile, tile) for d in range(n // 2 + 1)]
    row = lax.broadcasted_iota(jnp.int32, (tile, tile), 0)
    col = lax.broadcasted_iota(jnp.int32, (tile, tile), 1)
    diag = resid_ref[:, :tile].astype(F32)
    lower = jnp.where(row > col, diag, jnp.where(row == col, 0.5 * diag, 0.0)).astype(BF16)
    upper = jnp.where(row < col, diag, 0.0).astype(BF16)
    last = resid_ref[:, (n - 1) * tile :]
    real = piece < n // 2
    for at in range(0, half, step):

        def fields(d):
            rows = pl.ds(starts[d], tile)
            return green_ref[rows, at : at + step], green_ref[rows, half + at : half + at + step]

        re_here, im_here = fields(0)
        pu, pv = along(lower, re_here), along(lower, im_here)
        qu, qv = along(upper, re_here), along(upper, im_here)
        for d in range(1, n // 2):
            re, im = fields(d)
            p = resid_ref[:, (2 * d - 1) * tile : 2 * d * tile]
            q = resid_ref[:, 2 * d * tile : (2 * d + 1) * tile]
            pu, pv = pu + along(p, re), pv + along(p, im)
            qu, qv = qu + along(q, re), qv + along(q, im)
        re, im = fields(n // 2)
        hu, hv = along(last, re), along(last, im)
        yre = pu - qv + jnp.where(real, hu, -hv)
        yim = pv + qu + jnp.where(real, hv, hu)
        share = re_here.astype(F32) * yre + im_here.astype(F32) * yim
        out_ref[:, at : at + step] = 2.0 * jnp.sum(share, axis=0, keepdims=True)


SMEM = pl.BlockSpec(memory_space=pltpu.SMEM)
VMEM = pl.BlockSpec(memory_space=pltpu.VMEM)


def corr_piece(n, piece, source, green, dtype):
    stations, width = green.shape
    tile = stations // n
    return pl.pallas_call(
        functools.partial(corr_kernel, n),
        out_shape=jax.ShapeDtypeStruct((tile, stations), dtype),
        in_specs=[SMEM, VMEM, VMEM],
        out_specs=VMEM,
        compiler_params=pltpu.CompilerParams(vmem_limit_bytes=24 * MIB),
        cost_estimate=pl.CostEstimate(
            flops=2 * tile * stations * width * 5 // 4,
            bytes_accessed=2 * stations * width + 4 * tile * stations,
            transcendentals=0,
        ),
        name="corr_piece",
    )(piece, source, green)


def sens_piece(n, piece, resid, green):
    stations, width = green.shape
    tile = stations // n
    return pl.pallas_call(
        functools.partial(sens_kernel, n, min(512, width // 2)),
        out_shape=jax.ShapeDtypeStruct((1, width // 2), F32),
        in_specs=[SMEM, VMEM, VMEM],
        out_specs=VMEM,
        compiler_params=pltpu.CompilerParams(vmem_limit_bytes=24 * MIB),
        cost_estimate=pl.CostEstimate(
            flops=2 * tile * stations * width * 5 // 4,
            bytes_accessed=2 * stations * width + 2 * tile * stations,
            transcendentals=0,
        ),
        name="sens_piece",
    )(piece, resid, green)


def on_device(n_freq, n_cell, green, coeffs, basis, amplitude, block_mask):
    n = n_cell // 2
    bits, z_bits = n.bit_length() - 1, n_freq.bit_length() - 1
    stations, cells = green.shape[2], green.shape[3]
    tile = stations // n
    here = lax.axis_index("cell")
    core, chip, plane = here % 2, here // 2, lax.axis_index("freq")

    def dims(which):
        return [(which + j) % bits for j in range(bits)]

    swap_core = [(i, i ^ 1) for i in range(n_cell)]

    def swap_chip(value, j):
        pairs = [(i, i ^ (2 << dims(i % 2)[j])) for i in range(n_cell)]
        return lax.ppermute(value, "cell", pairs)

    def swap_plane(value, j):
        return lax.ppermute(value, "freq", [(i, i ^ (1 << j)) for i in range(n_freq)])

    def piece_of(q):
        flips = [sum(((q >> j) & 1) << dims(which)[j] for j in range(bits)) for which in (0, 1)]
        return (chip ^ jnp.where(core == 0, flips[0], flips[1])).astype(jnp.int32).reshape(1)

    known = jnp.concatenate((coeffs, lax.ppermute(coeffs, "cell", swap_core)), axis=1)
    for j in range(z_bits):
        known = jnp.concatenate((known, swap_plane(known, j)), axis=0)
    order = plane ^ jnp.arange(n_freq)
    basis_near = basis.reshape(2, n_freq, -1)[:, order].reshape(2, -1)
    basis_mine = lax.dynamic_index_in_dim(basis_near, core, 0, keepdims=False)
    basis_other = lax.dynamic_index_in_dim(basis_near, 1 - core, 0, keepdims=False)
    source = jnp.sum(basis_mine[:, None] * known, axis=0, keepdims=True)
    source = jnp.concatenate((source, source), axis=1)

    mine = lax.dynamic_index_in_dim(green, core, 1, keepdims=False)
    theirs = lax.ppermute(
        lax.dynamic_index_in_dim(green, 1 - core, 1, keepdims=False), "cell", swap_core
    )
    field = jnp.concatenate((mine[0], theirs[0], mine[1], theirs[1]), axis=1)

    own = piece_of(0)[0]
    columns = [0] + [d for d in range(1, n // 2) for _ in (0, 1)] + [n // 2]
    amp = lax.dynamic_index_in_dim(amplitude, core, 0, keepdims=False).reshape(n, tile)
    col_blocks = (own + jnp.array(columns)) % n
    amp_rows, amp_cols = amp[own], amp[col_blocks].reshape(-1)
    n_blocks = block_mask.shape[0]
    size = stations // n_blocks
    symmetric = (0.5 * (block_mask + block_mask.T)).astype(BF16)
    inside = jnp.arange(tile)
    row_block = (own * tile + inside) // size
    col_block = ((col_blocks * tile)[:, None] + inside[None, :]).reshape(-1) // size
    numbers = jnp.arange(n_blocks)
    pick_rows = (row_block[:, None] == numbers[None, :]).astype(BF16)
    pick_cols = (numbers[:, None] == col_block[None, :]).astype(BF16)
    spread = along(along(pick_rows, symmetric).astype(BF16), pick_cols)
    weight = amp_rows[:, None] * amp_cols[None, :] * spread

    held = {}
    first = sorted((q for q in range(n) if q & 1), reverse=True)
    for q in first + sorted((q for q in range(n) if not q & 1), reverse=True):
        held[q] = corr_piece(n, piece_of(q), source, field, BF16 if q & 1 else F32)
    for j in range(bits):
        for q in sorted((q for q in held if (q >> j) & 1), reverse=True):
            got = swap_chip(held.pop(q).astype(BF16), j)
            rest = q ^ (1 << j)
            held[rest] = held[rest] + got.astype(F32)
    resid = {0: (held[0] * weight).astype(BF16)}

    for j in reversed(range(bits)):
        for q in sorted(resid):
            resid[q | (1 << j)] = swap_chip(resid[q], j)
    sens = sum(sens_piece(n, piece_of(q), resid[q], field) for q in resid)

    other = lax.ppermute(sens[:, cells:], "cell", swap_core)
    partial = basis_mine[:, None] * sens[:, :cells] + basis_other[:, None] * other
    for j in reversed(range(z_bits)):
        middle = partial.shape[0] // 2
        partial = partial[:middle] + swap_plane(partial[middle:], j)
    return partial


def solution(mesh):
    placed = (
        P(None, "freq", None, "cell"),
        P("freq", "cell"),
        P("freq", None),
        P("freq", None),
        P(),
    )
    n_freq, n_cell = mesh.shape["freq"], mesh.shape["cell"]
    return jax.shard_map(
        functools.partial(on_device, n_freq, n_cell),
        mesh=mesh,
        in_specs=placed,
        out_specs=P("freq", "cell"),
        check_vma=False,
    )
```

time: 227 us -> 79.1 us (0.35)
  waiting for transfers between devices: 108 us -> 25.7 us
  blocking collectives: 33.6 us -> 0 us
  matrix products: 32.4 us -> 0.45 us
  starting transfers between devices: 0.01 us -> 21 us
  other arithmetic: 17.3 us -> 2.84 us
  Pallas kernels: 0 us -> 14 us
  between operations: 14.1 us -> 0.25 us
  local copies, waits for them, and re-layouts: 20.7 us -> 14.5 us
    psum x1 -> x0, waiting for transfers between devices: 108 us -> none  [on_device(): lax.psum(jnp.einsum('pfic,qpfjc->ifqj', scaled, right, preferred_element_...]
    dot_general x7 -> x1, matrix products: 32.4 us -> 0.45 us  [along(): return jnp.dot(left, right, preferred_element_type=F32)]
    ppermute x0 -> x13, waiting for transfers between devices: none -> 25.7 us  [the longest x6 15.9 us: swap_chip(): return lax.ppermute(value, 'cell', pairs)]
    ppermute x0 -> x13, starting transfers between devices: none -> 21 us  [the longest x4 10.6 us: swap_plane(): return lax.ppermute(value, 'freq', [(i, i ^ 1 << j) for i in range(n_freq)])]
    unnamed x1 -> x0, blocking collectives: 18.7 us -> none
    all_gather x1 -> x0, blocking collectives: 14.9 us -> none  [on_device(): full = lax.all_gather(coeffs, 'freq', axis=0, tiled=True)]
    pallas_call x0 -> x8, Pallas kernels: none -> 14 us  [the longest x4 7.71 us: sens_piece(): pl.pallas_call(functools.partial(sens_kernel, n, min(512, width // 2)), o...]
    convert_element_type x2 -> x0, local copies, waits for them, and re-layouts: 7.77 us -> none  [on_device(): expanded = jnp.broadcast_to(block_mask[:, None, :, None], (blocks, width,...]
  transfers between devices with their start and end apart: 1 -> 13, of which waited for: 1 -> 10; matrix products, arithmetic and copies ran while one was open for 8% -> 6% of each run, Pallas kernels for 0% -> 13%
where the time goes in v1:
time: 79.1 us; the launch traced here: 78.8 us
  waiting for transfers between devices  25.7 us (32%)
  starting transfers between devices  21 us (27%)
  local copies, waits for them, and re-layouts  14.5 us (18%)
  Pallas kernels  14 us (18%)
  other arithmetic  2.84 us (4%)
    ppermute x6, waiting for transfers between devices, swap_chip(): return lax.ppermute(value, 'cell', pairs)  15.9 us
    ppermute x4, starting transfers between devices, swap_plane(): return lax.ppermute(value, 'freq', [(i, i ^ 1 << j) for i in range(n_freq)])  10.6 us
    ppermute x6, starting transfers between devices, swap_chip(): return lax.ppermute(value, 'cell', pairs)  9.82 us
    pallas_call x4, Pallas kernels, sens_piece(): pl.pallas_call(functools.partial(sens_kernel, n, min(512, width // 2)), o...  7.71 us
    unnamed x24, local copies, waits for them, and re-layouts  6.69 us
    pallas_call x4, Pallas kernels, corr_piece(): pl.pallas_call(functools.partial(corr_kernel, n), out_shape=jax.ShapeDtyp...  6.33 us
    ppermute x4, waiting for transfers between devices, swap_plane(): return lax.ppermute(value, 'freq', [(i, i ^ 1 << j) for i in range(n_freq)])  6.27 us
    squeeze x2, local copies, waits for them, and re-layouts, on_device(): field = jnp.concatenate((mine[0], theirs[0], mine[1], theirs[1]), axis=1)  3.35 us
  transfers between devices with their start and end apart: 13, of which 10 were waited for; matrix products, arithmetic and copies ran while one was open for 6% of the time, Pallas kernels for 13%

profile of v1, /device:TPU:0, one launch (start us, length us, event | category | flops | bytes accessed | tf_op | source)
XLA Modules:
  0.0 78.8 jit_solution(10996512700662731007)
XLA Ops:
  0.0 3.1 %dynamic-slice_bitcast_fusion = bf16[2,1024,512]{2,1,0:T(8,128)(2,1)} fusion(bf16[2,2,1024,512]{3,2,1,0:T(8,128)(2,1)} %param.6, s32[]{:T(128)S(6)} %select_n.81), kind=kLoop, calls=%fused_computation.3 | loop fusion | bytes 4194308 | tf_op jit(solution)/shard_map/jit(dynamic_index_in_dim)/squeeze | solution.py:158
  3.1 0.5 collective-permute-start.3
  3.6 1.7 %dynamic-slice_bitcast_fusion.2 = (bf16[1024,512]{1,0:T(8,128)(2,1)S(1)}, bf16[1024,512]{1,0:T(8,128)(2,1)S(1)}) fusion(bf16[2,2,1024,512]{3,2,1,0:T(8,128)(2,1)} %param.6, s32[]{:T(128)S(6)} %select_n.79, s32[]{:T(128)S(6)} %add.144), kind=kLoop, calls=%fused_computation.9 | loop fusion | bytes 4194312 | tf_op jit(solution)/shard_map/squeeze | solution.py:160
  5.4 2.4 %collective-permute-done = f32[2,512]{1,0:T(2,128)S(1)} collective-permute-done((f32[2,512]{1,0:T(2,128)S(1)}, f32[2,512]{1,0:T(2,128)S(1)}, u32[]{:S(2)}, u32[]{:S(2)}) %collective-permute-start) | collective-permute-done | bytes 4128 | tf_op jit(solution)/shard_map/ppermute | solution.py:146
  7.7 2.9 %collective-permute-start.1 = (f32[2,1024]{1,0:T(2,128)S(1)}, f32[2,1024]{1,0:T(2,128)S(1)}, u32[]{:S(2)}, u32[]{:S(2)}) collective-permute-start(f32[2,1024]{1,0:T(2,128)S(1)} %constant_dynamic-update-slice_fusion), channel_id=1, source_target_pairs={{0,8},{8,0},{16,24},{24,16},{1,9},{9,1},{17,25},{25,17},{2,10},{10... | collective-permute-start | bytes 24584 | tf_op jit(solution)/shard_map/ppermute | solution.py:140
  10.7 0.1 reshape.100
  10.8 0.6 gather_fusion
  11.4 0.1 reshape.101
  11.4 0.9 %collective-permute-done.1 = f32[2,1024]{1,0:T(2,128)S(1)} collective-permute-done((f32[2,1024]{1,0:T(2,128)S(1)}, f32[2,1024]{1,0:T(2,128)S(1)}, u32[]{:S(2)}, u32[]{:S(2)}) %collective-permute-start.1) | collective-permute-done | bytes 8224 | tf_op jit(solution)/shard_map/ppermute | solution.py:140
  12.3 3.1 %collective-permute-start.2 = (f32[4,1024]{1,0:T(4,128)S(1)}, f32[4,1024]{1,0:T(4,128)S(1)}, u32[]{:S(2)}, u32[]{:S(2)}) collective-permute-start(f32[4,1024]{1,0:T(4,128)S(1)} %pad_maximum_fusion.1), channel_id=1, source_target_pairs={{0,16},{8,24},{16,0},{24,8},{1,17},{9,25},{17,1},{25,9},{2,18},{10... | collective-permute-start | bytes 49160 | tf_op jit(solution)/shard_map/ppermute | solution.py:140
  15.4 1.7 %collective-permute-done.2 = f32[4,1024]{1,0:T(4,128)S(1)} collective-permute-done((f32[4,1024]{1,0:T(4,128)S(1)}, f32[4,1024]{1,0:T(4,128)S(1)}, u32[]{:S(2)}, u32[]{:S(2)}) %collective-permute-start.2) | collective-permute-done | bytes 16416 | tf_op jit(solution)/shard_map/ppermute | solution.py:140
  17.1 0.1 fusion.2
  17.3 1.7 %slice_bitcast_fusion.1 = (bf16[1024,512]{1,0:T(8,128)(2,1)S(1)}, bf16[1024,512]{1,0:T(8,128)(2,1)S(1)}) fusion(bf16[2,1024,512]{2,1,0:T(8,128)(2,1)} %collective-permute-done.3), kind=kLoop, calls=%fused_computation.8 | loop fusion | bytes 4194304 | tf_op jit(solution)/shard_map/squeeze | solution.py:160
  18.9 0.6 pad_maximum_fusion.green_ref
  19.6 1.6 %corr_piece.7 = bf16[256,1024]{1,0:T(8,128)(2,1)S(1)} custom-call(s32[1]{0:T(128)} %bitcast.12.piece_ref, f32[1,2048]{1,0:T(1,128)S(1)} %pad_maximum_fusion.2.source_ref, bf16[1024,2048]{1,0:T(8,128)(2,1)S(1)} %pad_maximum_fusion.green_ref), custom_call_target="tpu_custom_call" | custom-call | flops 1342177280 | bytes 5242880 | tf_op jit(solution)/shard_map/corr_piece/pallas_call | solution.py:89
  21.2 1.9 %copy-done.1 = bf16[1024,2048]{1,0:T(8,128)(2,1)} copy-done((bf16[1024,2048]{1,0:T(8,128)(2,1)}, bf16[1024,2048]{1,0:T(8,128)(2,1)S(1)}, u32[]{:S(2)}) %copy-start.1) | copy-done | bytes 4194328
  23.1 1.8 %collective-permute-start.5 = (bf16[256,1024]{1,0:T(8,128)(2,1)S(1)}, bf16[256,1024]{1,0:T(8,128)(2,1)S(1)}, u32[]{:S(2)}, u32[]{:S(2)}) collective-permute-start(bf16[256,1024]{1,0:T(8,128)(2,1)S(1)} %corr_piece.7), channel_id=1, source_target_pairs={{0,2},{1,5},{2,0},{3,7},{4,6},{5,1},{6,4},{7,3},{8,10},{9,13},{10,... | collective-permute-start | bytes 1572872 | tf_op jit(solution)/shard_map/ppermute | solution.py:137
  25.1 2.2 %copy-done.2 = bf16[1024,2048]{1,0:T(8,128)(2,1)S(1)} copy-done((bf16[1024,2048]{1,0:T(8,128)(2,1)S(1)}, bf16[1024,2048]{1,0:T(8,128)(2,1)}, u32[]{:S(2)}) %copy-start.2) | copy-done | bytes 4194328
  27.3 1.6 %corr_piece.5 = bf16[256,1024]{1,0:T(8,128)(2,1)S(1)} custom-call(s32[1]{0:T(128)} %bitcast.10.piece_ref, f32[1,2048]{1,0:T(1,128)S(1)} %pad_maximum_fusion.2.source_ref, bf16[1024,2048]{1,0:T(8,128)(2,1)S(1)} %copy-done.2), custom_call_target="tpu_custom_call" | custom-call | flops 1342177280 | bytes 5242880 | tf_op jit(solution)/shard_map/corr_piece/pallas_call | solution.py:89
  28.8 0.3 collective-permute-start.4
  29.1 0.3 copy-done.3
  29.4 1.6 %corr_piece.6 = f32[256,1024]{1,0:T(8,128)S(1)} custom-call(s32[1]{0:T(128)} %bitcast.11.piece_ref, f32[1,2048]{1,0:T(1,128)S(1)} %pad_maximum_fusion.2.source_ref, bf16[1024,2048]{1,0:T(8,128)(2,1)S(1)} %copy-done.3), custom_call_target="tpu_custom_call" | custom-call | flops 1342177280 | bytes 5242880 | tf_op jit(solution)/shard_map/corr_piece/pallas_call | solution.py:89
  31.0 1.3 %collective-permute-done.5 = bf16[256,1024]{1,0:T(8,128)(2,1)S(1)} collective-permute-done((bf16[256,1024]{1,0:T(8,128)(2,1)S(1)}, bf16[256,1024]{1,0:T(8,128)(2,1)S(1)}, u32[]{:S(2)}, u32[]{:S(2)}) %collective-permute-start.5) | collective-permute-done | bytes 524320 | tf_op jit(solution)/shard_map/ppermute | solution.py:137
  32.3 1.0 %add_convert_fusion = bf16[256,1024]{1,0:T(8,128)(2,1)} fusion(f32[256,1024]{1,0:T(8,128)S(1)} %corr_piece.6, bf16[256,1024]{1,0:T(8,128)(2,1)S(1)} %collective-permute-done.5), kind=kLoop, calls=%fused_computation.11 | loop fusion | flops 786432 | bytes 2097152 | tf_op jit(solution)/shard_map/convert_element_type | solution.py:185
  33.3 1.8 %collective-permute-start.6 = (bf16[256,1024]{1,0:T(8,128)(2,1)}, bf16[256,1024]{1,0:T(8,128)(2,1)S(1)}, u32[]{:S(2)}, u32[]{:S(2)}) collective-permute-start(bf16[256,1024]{1,0:T(8,128)(2,1)} %add_convert_fusion), channel_id=1, source_target_pairs={{0,4},{1,3},{2,6},{3,1},{4,0},{5,7},{6,2},{7,5},{8,12},{9,11},{10,... | collective-permute-start | bytes 1572872 | tf_op jit(solution)/shard_map/ppermute | solution.py:137
  35.1 0.6 gather_fusion.1
  35.8 0.4 convolution_multiply_fusion
  36.2 2.2 %copy-done.4 = bf16[1024,2048]{1,0:T(8,128)(2,1)S(1)} copy-done((bf16[1024,2048]{1,0:T(8,128)(2,1)S(1)}, bf16[1024,2048]{1,0:T(8,128)(2,1)}, u32[]{:S(2)}) %copy-start.4) | copy-done | bytes 4194328
  38.4 1.6 %corr_piece.4 = f32[256,1024]{1,0:T(8,128)S(1)} custom-call(s32[1]{0:T(128)} %bitcast.3.piece_ref, f32[1,2048]{1,0:T(1,128)S(1)} %pad_maximum_fusion.2.source_ref, bf16[1024,2048]{1,0:T(8,128)(2,1)S(1)} %copy-done.4), custom_call_target="tpu_custom_call" | custom-call | flops 1342177280 | bytes 5242880 | tf_op jit(solution)/shard_map/corr_piece/pallas_call | solution.py:89
  40.0 2.8 %collective-permute-done.4 = bf16[256,1024]{1,0:T(8,128)(2,1)S(1)} collective-permute-done((bf16[256,1024]{1,0:T(8,128)(2,1)S(1)}, bf16[256,1024]{1,0:T(8,128)(2,1)S(1)}, u32[]{:S(2)}, u32[]{:S(2)}) %collective-permute-start.4) | collective-permute-done | bytes 524320 | tf_op jit(solution)/shard_map/ppermute | solution.py:137
  42.8 0.3 multiply_convert_fusion.resid_ref
  43.2 1.8 %collective-permute-start.7 = (bf16[256,1024]{1,0:T(8,128)(2,1)S(1)}, bf16[256,1024]{1,0:T(8,128)(2,1)S(1)}, u32[]{:S(2)}, u32[]{:S(2)}) collective-permute-start(bf16[256,1024]{1,0:T(8,128)(2,1)S(1)} %multiply_convert_fusion.resid_ref), channel_id=1, source_target_pairs={{0,4},{1,3},{2,6},{3,1},{4,0},{5,7},{6,2},{7,5},{8,12},{9,11},{10,... | collective-permute-start | bytes 1572872 | tf_op jit(solution)/shard_map/ppermute | solution.py:137
  45.0 1.5 %collective-permute-start.8 = (bf16[256,1024]{1,0:T(8,128)(2,1)S(1)}, bf16[256,1024]{1,0:T(8,128)(2,1)S(1)}, u32[]{:S(2)}, u32[]{:S(2)}) collective-permute-start(bf16[256,1024]{1,0:T(8,128)(2,1)S(1)} %multiply_convert_fusion.resid_ref), channel_id=1, source_target_pairs={{0,2},{1,5},{2,0},{3,7},{4,6},{5,1},{6,4},{7,3},{8,10},{9,13},{10,... | collective-permute-start | bytes 1572872 | tf_op jit(solution)/shard_map/ppermute | solution.py:137
  46.5 10.5 %collective-permute-done.7.resid_ref = bf16[256,1024]{1,0:T(8,128)(2,1)S(1)} collective-permute-done((bf16[256,1024]{1,0:T(8,128)(2,1)S(1)}, bf16[256,1024]{1,0:T(8,128)(2,1)S(1)}, u32[]{:S(2)}, u32[]{:S(2)}) %collective-permute-start.7) | collective-permute-done | bytes 524320 | tf_op jit(solution)/shard_map/ppermute | solution.py:137
  56.9 2.6 %collective-permute-start.9 = (bf16[256,1024]{1,0:T(8,128)(2,1)S(1)}, bf16[256,1024]{1,0:T(8,128)(2,1)S(1)}, u32[]{:S(2)}, u32[]{:S(2)}) collective-permute-start(bf16[256,1024]{1,0:T(8,128)(2,1)S(1)} %collective-permute-done.7.resid_ref), channel_id=1, source_target_pairs={{0,2},{1,5},{2,0},{3,7},{4,6},{5,1},{6,4},{7,3},{8,10},{9,13},{10,... | collective-permute-start | bytes 1572872 | tf_op jit(solution)/shard_map/ppermute | solution.py:137
  59.5 1.9 %sens_piece.4 = f32[1,1024]{1,0:T(1,128)S(1)} custom-call(s32[1]{0:T(128)} %bitcast.3.piece_ref, bf16[256,1024]{1,0:T(8,128)(2,1)S(1)} %multiply_convert_fusion.resid_ref, bf16[1024,2048]{1,0:T(8,128)(2,1)S(1)} %copy-done.5), custom_call_target="tpu_custom_call" | custom-call | flops 1342177280 | bytes 4718592 | tf_op jit(solution)/shard_map/sens_piece/pallas_call | solution.py:107
  61.4 1.9 %sens_piece.5 = f32[1,1024]{1,0:T(1,128)S(1)} custom-call(s32[1]{0:T(128)} %bitcast.11.piece_ref, bf16[256,1024]{1,0:T(8,128)(2,1)S(1)} %collective-permute-done.7.resid_ref, bf16[1024,2048]{1,0:T(8,128)(2,1)S(1)} %copy-done.5), custom_call_target="tpu_custom_call" | custom-call | flops 1342177280 | bytes 4718592 | tf_op jit(solution)/shard_map/sens_piece/pallas_call | solution.py:107
  63.4 1.9 %sens_piece.6 = f32[1,1024]{1,0:T(1,128)S(1)} custom-call(s32[1]{0:T(128)} %bitcast.10.piece_ref, bf16[256,1024]{1,0:T(8,128)(2,1)S(1)} %collective-permute-done.8.resid_ref, bf16[1024,2048]{1,0:T(8,128)(2,1)S(1)} %copy-done.5), custom_call_target="tpu_custom_call" | custom-call | flops 1342177280 | bytes 4718592 | tf_op jit(solution)/shard_map/sens_piece/pallas_call | solution.py:107
  65.3 1.3 %collective-permute-done.9.resid_ref = bf16[256,1024]{1,0:T(8,128)(2,1)S(1)} collective-permute-done((bf16[256,1024]{1,0:T(8,128)(2,1)S(1)}, bf16[256,1024]{1,0:T(8,128)(2,1)S(1)}, u32[]{:S(2)}, u32[]{:S(2)}) %collective-permute-start.9) | collective-permute-done | bytes 524320 | tf_op jit(solution)/shard_map/ppermute | solution.py:137
  66.7 1.9 %sens_piece.7 = f32[1,1024]{1,0:T(1,128)S(1)} custom-call(s32[1]{0:T(128)} %bitcast.12.piece_ref, bf16[256,1024]{1,0:T(8,128)(2,1)S(1)} %collective-permute-done.9.resid_ref, bf16[1024,2048]{1,0:T(8,128)(2,1)S(1)} %copy-done.5), custom_call_target="tpu_custom_call" | custom-call | flops 1342177280 | bytes 4718592 | tf_op jit(solution)/shard_map/sens_piece/pallas_call | solution.py:107
  68.6 0.1 collective-permute-start.10
  68.7 1.1 %collective-permute-done.10 = f32[1,512]{1,0:T(1,128)S(1)} collective-permute-done((f32[1,512]{1,0:T(1,128)S(1)}, f32[1,512]{1,0:T(1,128)S(1)}, u32[]{:S(2)}, u32[]{:S(2)}) %collective-permute-start.10) | collective-permute-done | bytes 2080 | tf_op jit(solution)/shard_map/ppermute | solution.py:195
  69.8 0.1 multiply_add_fusion
  69.9 2.8 %collective-permute-start.11 = (f32[4,512]{1,0:T(4,128)S(1)}, f32[4,512]{1,0:T(4,128)S(1)}, u32[]{:S(2)}, u32[]{:S(2)}) collective-permute-start(f32[4,512]{1,0:T(4,128)S(1)} %slice.51), channel_id=1, source_target_pairs={{0,16},{8,24},{16,0},{24,8},{1,17},{9,25},{17,1},{25,9},{2,18},{10... | collective-permute-start | bytes 24584 | tf_op jit(solution)/shard_map/ppermute | solution.py:140
  72.7 1.8 %collective-permute-done.11 = f32[4,512]{1,0:T(4,128)S(1)} collective-permute-done((f32[4,512]{1,0:T(4,128)S(1)}, f32[4,512]{1,0:T(4,128)S(1)}, u32[]{:S(2)}, u32[]{:S(2)}) %collective-permute-start.11) | collective-permute-done | bytes 8224 | tf_op jit(solution)/shard_map/ppermute | solution.py:140
  74.5 1.8 %collective-permute-start.12 = (f32[2,512]{1,0:T(2,128)S(1)}, f32[2,512]{1,0:T(2,128)S(1)}, u32[]{:S(2)}, u32[]{:S(2)}) collective-permute-start(f32[2,512]{1,0:T(2,128)S(1)} %slice.53), channel_id=1, source_target_pairs={{0,8},{8,0},{16,24},{24,16},{1,9},{9,1},{17,25},{25,17},{2,10},{10... | collective-permute-start | bytes 12296 | tf_op jit(solution)/shard_map/ppermute | solution.py:140
  76.3 1.9 %collective-permute-done.12 = f32[2,512]{1,0:T(2,128)S(1)} collective-permute-done((f32[2,512]{1,0:T(2,128)S(1)}, f32[2,512]{1,0:T(2,128)S(1)}, u32[]{:S(2)}, u32[]{:S(2)}) %collective-permute-start.12) | collective-permute-done | bytes 4128 | tf_op jit(solution)/shard_map/ppermute | solution.py:140
  78.2 0.6 slice_add_fusion.1
  (45 shorter events, 0.4 us)
Async XLA Ops:
  0.0 25.0 %copy-start = (f32[2,1024]{1,0:T(2,128)S(1)}, f32[2,1024]{1,0:T(2,128)}, u32[]{:S(2)}) copy-start(f32[2,1024]{1,0:T(2,128)} %param.9) | copy-start | bytes 24580
  0.0 3.6 %copy-start.7 = (f32[2,512]{1,0:T(2,128)S(1)}, f32[2,512]{1,0:T(2,128)}, u32[]{:S(2)}) copy-start(f32[2,512]{1,0:T(2,128)} %param.7) | copy-start | bytes 12292
  0.0 5.3 %copy-start.9 = (s32[4]{0:T(128)S(1)}, s32[4]{0:T(128)}, u32[]{:S(2)}) copy-start(s32[4]{0:T(128)} %constant.99.clone) | copy-start | bytes 52
  0.0 10.7 %copy-start.8 = (f32[2,8]{1,0:T(2,128)S(1)}, f32[2,8]{1,0:T(2,128)}, u32[]{:S(2)}) copy-start(f32[2,8]{1,0:T(2,128)} %param.8) | copy-start | bytes 196
  3.1 14.1 %collective-permute-start.3 = (bf16[2,1024,512]{2,1,0:T(8,128)(2,1)}, bf16[2,1024,512]{2,1,0:T(8,128)(2,1)}, u32[]{:S(2)}, u32[]{:S(2)}) collective-permute-start(bf16[2,1024,512]{2,1,0:T(8,128)(2,1)} %dynamic-slice_bitcast_fusion), channel_id=1, source_target_pairs={{0,1},{1,0},{2,3},{3,2},{4,5},{5,4},{6,7},{7,6},{8,9},{9,8},{10,11... | collective-permute-start | bytes 6291464 | tf_op jit(solution)/shard_map/ppermute | solution.py:157
  3.6 4.1 %collective-permute-start = (f32[2,512]{1,0:T(2,128)S(1)}, f32[2,512]{1,0:T(2,128)S(1)}, u32[]{:S(2)}, u32[]{:S(2)}) collective-permute-start(f32[2,512]{1,0:T(2,128)S(1)} %copy-done.7), channel_id=1, source_target_pairs={{0,1},{1,0},{2,3},{3,2},{4,5},{5,4},{6,7},{7,6},{8,9},{9,8},{10,11... | collective-permute-start | bytes 12296 | tf_op jit(solution)/shard_map/ppermute | solution.py:146
  7.7 4.6 %collective-permute-start.1 = (f32[2,1024]{1,0:T(2,128)S(1)}, f32[2,1024]{1,0:T(2,128)S(1)}, u32[]{:S(2)}, u32[]{:S(2)}) collective-permute-start(f32[2,1024]{1,0:T(2,128)S(1)} %constant_dynamic-update-slice_fusion), channel_id=1, source_target_pairs={{0,8},{8,0},{16,24},{24,16},{1,9},{9,1},{17,25},{25,17},{2,10},{10... | collective-permute-start | bytes 24584 | tf_op jit(solution)/shard_map/ppermute | solution.py:140
  12.3 4.8 %collective-permute-start.2 = (f32[4,1024]{1,0:T(4,128)S(1)}, f32[4,1024]{1,0:T(4,128)S(1)}, u32[]{:S(2)}, u32[]{:S(2)}) collective-permute-start(f32[4,1024]{1,0:T(4,128)S(1)} %pad_maximum_fusion.1), channel_id=1, source_target_pairs={{0,16},{8,24},{16,0},{24,8},{1,17},{9,25},{17,1},{25,9},{2,18},{10... | collective-permute-start | bytes 49160 | tf_op jit(solution)/shard_map/ppermute | solution.py:140
  21.2 1.9 %copy-start.1 = (bf16[1024,2048]{1,0:T(8,128)(2,1)}, bf16[1024,2048]{1,0:T(8,128)(2,1)S(1)}, u32[]{:S(2)}) copy-start(bf16[1024,2048]{1,0:T(8,128)(2,1)S(1)} %pad_maximum_fusion.green_ref) | copy-start | bytes 12582916
  23.1 9.2 %collective-permute-start.5 = (bf16[256,1024]{1,0:T(8,128)(2,1)S(1)}, bf16[256,1024]{1,0:T(8,128)(2,1)S(1)}, u32[]{:S(2)}, u32[]{:S(2)}) collective-permute-start(bf16[256,1024]{1,0:T(8,128)(2,1)S(1)} %corr_piece.7), channel_id=1, source_target_pairs={{0,2},{1,5},{2,0},{3,7},{4,6},{5,1},{6,4},{7,3},{8,10},{9,13},{10,... | collective-permute-start | bytes 1572872 | tf_op jit(solution)/shard_map/ppermute | solution.py:137
  25.1 2.2 %copy-start.2 = (bf16[1024,2048]{1,0:T(8,128)(2,1)S(1)}, bf16[1024,2048]{1,0:T(8,128)(2,1)}, u32[]{:S(2)}) copy-start(bf16[1024,2048]{1,0:T(8,128)(2,1)} %copy-done.1) | copy-start | bytes 12582916
  27.2 2.2 %copy-start.3 = (bf16[1024,2048]{1,0:T(8,128)(2,1)S(1)}, bf16[1024,2048]{1,0:T(8,128)(2,1)}, u32[]{:S(2)}) copy-start(bf16[1024,2048]{1,0:T(8,128)(2,1)} %copy-done.1) | copy-start | bytes 12582916
  28.8 6.9 %copy-start.6 = (s32[16,16]{1,0:T(8,128)S(1)}, s32[16,16]{1,0:T(8,128)}, u32[]{:S(2)}) copy-start(s32[16,16]{1,0:T(8,128)} %param.10) | copy-start | bytes 3076
  28.8 14.0 %collective-permute-start.4 = (bf16[256,1024]{1,0:T(8,128)(2,1)S(1)}, bf16[256,1024]{1,0:T(8,128)(2,1)S(1)}, u32[]{:S(2)}, u32[]{:S(2)}) collective-permute-start(bf16[256,1024]{1,0:T(8,128)(2,1)S(1)} %corr_piece.5), channel_id=1, source_target_pairs={{0,2},{1,5},{2,0},{3,7},{4,6},{5,1},{6,4},{7,3},{8,10},{9,13},{10,... | collective-permute-start | bytes 1572872 | tf_op jit(solution)/shard_map/ppermute | solution.py:137
  33.3 9.6 %collective-permute-start.6 = (bf16[256,1024]{1,0:T(8,128)(2,1)}, bf16[256,1024]{1,0:T(8,128)(2,1)S(1)}, u32[]{:S(2)}, u32[]{:S(2)}) collective-permute-start(bf16[256,1024]{1,0:T(8,128)(2,1)} %add_convert_fusion), channel_id=1, source_target_pairs={{0,4},{1,3},{2,6},{3,1},{4,0},{5,7},{6,2},{7,5},{8,12},{9,11},{10,... | collective-permute-start | bytes 1572872 | tf_op jit(solution)/shard_map/ppermute | solution.py:137
  36.2 2.2 %copy-start.4 = (bf16[1024,2048]{1,0:T(8,128)(2,1)S(1)}, bf16[1024,2048]{1,0:T(8,128)(2,1)}, u32[]{:S(2)}) copy-start(bf16[1024,2048]{1,0:T(8,128)(2,1)} %copy-done.1) | copy-start | bytes 12582916
  38.4 21.1 %copy-start.5 = (bf16[1024,2048]{1,0:T(8,128)(2,1)S(1)}, bf16[1024,2048]{1,0:T(8,128)(2,1)}, u32[]{:S(2)}) copy-start(bf16[1024,2048]{1,0:T(8,128)(2,1)} %copy-done.1) | copy-start | bytes 12582916
  43.2 13.8 %collective-permute-start.7 = (bf16[256,1024]{1,0:T(8,128)(2,1)S(1)}, bf16[256,1024]{1,0:T(8,128)(2,1)S(1)}, u32[]{:S(2)}, u32[]{:S(2)}) collective-permute-start(bf16[256,1024]{1,0:T(8,128)(2,1)S(1)} %multiply_convert_fusion.resid_ref), channel_id=1, source_target_pairs={{0,4},{1,3},{2,6},{3,1},{4,0},{5,7},{6,2},{7,5},{8,12},{9,11},{10,... | collective-permute-start | bytes 1572872 | tf_op jit(solution)/shard_map/ppermute | solution.py:137
  45.0 18.4 %collective-permute-start.8 = (bf16[256,1024]{1,0:T(8,128)(2,1)S(1)}, bf16[256,1024]{1,0:T(8,128)(2,1)S(1)}, u32[]{:S(2)}, u32[]{:S(2)}) collective-permute-start(bf16[256,1024]{1,0:T(8,128)(2,1)S(1)} %multiply_convert_fusion.resid_ref), channel_id=1, source_target_pairs={{0,2},{1,5},{2,0},{3,7},{4,6},{5,1},{6,4},{7,3},{8,10},{9,13},{10,... | collective-permute-start | bytes 1572872 | tf_op jit(solution)/shard_map/ppermute | solution.py:137
  56.9 9.7 %collective-permute-start.9 = (bf16[256,1024]{1,0:T(8,128)(2,1)S(1)}, bf16[256,1024]{1,0:T(8,128)(2,1)S(1)}, u32[]{:S(2)}, u32[]{:S(2)}) collective-permute-start(bf16[256,1024]{1,0:T(8,128)(2,1)S(1)} %collective-permute-done.7.resid_ref), channel_id=1, source_target_pairs={{0,2},{1,5},{2,0},{3,7},{4,6},{5,1},{6,4},{7,3},{8,10},{9,13},{10,... | collective-permute-start | bytes 1572872 | tf_op jit(solution)/shard_map/ppermute | solution.py:137
  68.6 1.2 %collective-permute-start.10 = (f32[1,512]{1,0:T(1,128)S(1)}, f32[1,512]{1,0:T(1,128)S(1)}, u32[]{:S(2)}, u32[]{:S(2)}) collective-permute-start(f32[1,512]{1,0:T(1,128)S(1)} %get-tuple-element.12), channel_id=1, source_target_pairs={{0,1},{1,0},{2,3},{3,2},{4,5},{5,4},{6,7},{7,6},{8,9},{9,8},{10,11... | collective-permute-start | bytes 6152 | tf_op jit(solution)/shard_map/ppermute | solution.py:195
  69.9 4.6 %collective-permute-start.11 = (f32[4,512]{1,0:T(4,128)S(1)}, f32[4,512]{1,0:T(4,128)S(1)}, u32[]{:S(2)}, u32[]{:S(2)}) collective-permute-start(f32[4,512]{1,0:T(4,128)S(1)} %slice.51), channel_id=1, source_target_pairs={{0,16},{8,24},{16,0},{24,8},{1,17},{9,25},{17,1},{25,9},{2,18},{10... | collective-permute-start | bytes 24584 | tf_op jit(solution)/shard_map/ppermute | solution.py:140
  74.5 3.7 %collective-permute-start.12 = (f32[2,512]{1,0:T(2,128)S(1)}, f32[2,512]{1,0:T(2,128)S(1)}, u32[]{:S(2)}, u32[]{:S(2)}) collective-permute-start(f32[2,512]{1,0:T(2,128)S(1)} %slice.53), channel_id=1, source_target_pairs={{0,8},{8,0},{16,24},{24,16},{1,9},{9,1},{17,25},{25,17},{2,10},{10... | collective-permute-start | bytes 12296 | tf_op jit(solution)/shard_map/ppermute | solution.py:140

commit v2 on v1

v2 whole, which is shorter than its diff:
```python
import functools

import jax
import jax.numpy as jnp
from jax import lax
from jax.experimental import pallas as pl
from jax.experimental.pallas import tpu as pltpu
from jax.sharding import PartitionSpec as P

F32 = jnp.float32
BF16 = jnp.bfloat16
MIB = 1 << 20


def across(left, right):
    return lax.dot_general(left, right, (((1,), (1,)), ((), ())), preferred_element_type=F32)


def along(left, right):
    return jnp.dot(left, right, preferred_element_type=F32)


def copy_all(sems, pairs):
    copies = [pltpu.make_async_copy(src, dst, sems.at[i]) for i, (src, dst) in enumerate(pairs)]
    for copy in copies:
        copy.start()
    for copy in copies:
        copy.wait()


def take_kernel(core_ref, green_ref, out_ref, sems):
    other = 1 - core_ref[0]
    copy_all(sems, [(green_ref.at[p, other], out_ref.at[p]) for p in (0, 1)])


def field_kernel(core_ref, green_ref, theirs_ref, out_ref, sems):
    core, cells = core_ref[0], green_ref.shape[3]
    pairs = []
    for p in (0, 1):
        pairs.append((green_ref.at[p, core], out_ref.at[:, pl.ds(2 * p * cells, cells)]))
        pairs.append((theirs_ref.at[p], out_ref.at[:, pl.ds((2 * p + 1) * cells, cells)]))
    copy_all(sems, pairs)


def weight_kernel(n, place_ref, amp_ref, mask_ref, out_ref):
    core, piece = place_ref[0], place_ref[1]
    tile, stations = out_ref.shape
    blocks = mask_ref.shape[0]
    size = stations // blocks

    def amp(start):
        both = amp_ref[:, pl.ds(pl.multiple_of(start, tile), tile)]
        return jnp.where(core == 0, both[0:1], both[1:2])

    here = piece * tile
    row = lax.broadcasted_iota(jnp.int32, (tile, tile), 0)
    col = lax.broadcasted_iota(jnp.int32, (tile, tile), 1)
    down = jnp.sum(jnp.where(row == col, amp(here), 0.0), axis=1, keepdims=True)
    mask = mask_ref[...].astype(BF16)
    low = lax.broadcasted_iota(jnp.int32, (tile, blocks), 1) * size
    at = here + lax.broadcasted_iota(jnp.int32, (tile, blocks), 0)
    pick = ((at >= low) & (at < low + size)).astype(BF16)
    rows = (0.5 * (along(pick, mask) + across(pick, mask))).astype(BF16)
    low = lax.broadcasted_iota(jnp.int32, (blocks, tile), 0) * size
    for d in range(n // 2 + 1):
        start = lax.rem(piece + d, n) * tile
        at = start + lax.broadcasted_iota(jnp.int32, (blocks, tile), 1)
        pick = ((at >= low) & (at < low + size)).astype(BF16)
        weight = down * amp(start) * along(rows, pick)
        for i in ([0] if d == 0 else [2 * d - 1] if d == n // 2 else [2 * d - 1, 2 * d]):
            out_ref[:, i * tile : (i + 1) * tile] = weight


def corr_kernel(n, place_ref, basis_ref, known_ref, green_ref, out_ref):
    stations, width = green_ref.shape
    tile, half = stations // n, width // 2
    core, plane, piece = place_ref[0], place_ref[1], place_ref[2]

    def block(d):
        start = lax.rem(piece + d, n) * tile
        return green_ref[pl.ds(pl.multiple_of(start, tile), tile), :]

    planes, each = known_ref.shape[0], known_ref.shape[1]
    source = jnp.zeros((1, half), F32)
    for r in range(planes):
        for k in range(each):
            source = source + basis_ref[core, (plane ^ r) * each + k] * known_ref[r, k : k + 1, :]
    source = jnp.concatenate((source, source), axis=1)
    scaled = (block(0).astype(F32) * source).astype(BF16)
    turned = jnp.concatenate((scaled[:, half:], -scaled[:, :half]), axis=1)
    both = jnp.concatenate((scaled, turned), axis=0)
    pair = across(both, block(0))
    row = lax.broadcasted_iota(jnp.int32, (tile, tile), 0)
    col = lax.broadcasted_iota(jnp.int32, (tile, tile), 1)
    out_ref[:, :tile] = jnp.where(row >= col, pair[:tile], pair[tile:]).astype(out_ref.dtype)
    for d in range(1, n // 2):
        pair = across(both, block(d)).astype(out_ref.dtype)
        out_ref[:, (2 * d - 1) * tile : 2 * d * tile] = pair[:tile]
        out_ref[:, 2 * d * tile : (2 * d + 1) * tile] = pair[tile:]
    last = across(jnp.where(piece < n // 2, scaled, turned), block(n // 2))
    out_ref[:, (n - 1) * tile :] = last.astype(out_ref.dtype)


def sens_kernel(n, step, piece_ref, resid_ref, green_ref, out_ref):
    stations, width = green_ref.shape
    tile, half = stations // n, width // 2
    piece = piece_ref[0]
    starts = [pl.multiple_of(lax.rem(piece + d, n) * tile, tile) for d in range(n // 2 + 1)]
    row = lax.broadcasted_iota(jnp.int32, (tile, tile), 0)
    col = lax.broadcasted_iota(jnp.int32, (tile, tile), 1)
    diag = resid_ref[:, :tile].astype(F32)
    lower = jnp.where(row > col, diag, jnp.where(row == col, 0.5 * diag, 0.0)).astype(BF16)
    upper = jnp.where(row < col, diag, 0.0).astype(BF16)
    last = resid_ref[:, (n - 1) * tile :]
    real = piece < n // 2
    for at in range(0, half, step):

        def fields(d):
            rows = pl.ds(starts[d], tile)
            return green_ref[rows, at : at + step], green_ref[rows, half + at : half + at + step]

        re_here, im_here = fields(0)
        pu, pv = along(lower, re_here), along(lower, im_here)
        qu, qv = along(upper, re_here), along(upper, im_here)
        for d in range(1, n // 2):
            re, im = fields(d)
            p = resid_ref[:, (2 * d - 1) * tile : 2 * d * tile]
            q = resid_ref[:, 2 * d * tile : (2 * d + 1) * tile]
            pu, pv = pu + along(p, re), pv + along(p, im)
            qu, qv = qu + along(q, re), qv + along(q, im)
        re, im = fields(n // 2)
        hu, hv = along(last, re), along(last, im)
        yre = pu - qv + jnp.where(real, hu, -hv)
        yim = pv + qu + jnp.where(real, hv, hu)
        share = re_here.astype(F32) * yre + im_here.astype(F32) * yim
        out_ref[:, at : at + step] = 2.0 * jnp.sum(share, axis=0, keepdims=True)


def hess_kernel(planes, place_ref, basis_ref, sens_ref, other_ref, out_ref):
    core, plane = place_ref[0], place_ref[1]
    each = out_ref.shape[0] // planes
    mine, other = sens_ref[:, : out_ref.shape[1]], other_ref[...]
    for r in range(planes):
        for k in range(each):
            b, i = (plane ^ r) * each + k, r * each + k
            out_ref[i : i + 1, :] = basis_ref[core, b] * mine + basis_ref[1 - core, b] * other


SMEM = pl.BlockSpec(memory_space=pltpu.SMEM)
VMEM = pl.BlockSpec(memory_space=pltpu.VMEM)
HBM = pl.BlockSpec(memory_space=pltpu.HBM)


def call(kernel, name, shape, dtype, specs, flops, moved, grant, *args, scratch=()):
    return pl.pallas_call(
        kernel,
        out_shape=jax.ShapeDtypeStruct(shape, dtype),
        in_specs=specs,
        out_specs=VMEM,
        scratch_shapes=scratch,
        compiler_params=pltpu.CompilerParams(vmem_limit_bytes=grant * MIB),
        cost_estimate=pl.CostEstimate(flops=flops, bytes_accessed=moved, transcendentals=0),
        name=name,
    )(*args)


def on_device(n_freq, n_cell, green, coeffs, basis, amplitude, block_mask):
    n = n_cell // 2
    bits, z_bits = n.bit_length() - 1, n_freq.bit_length() - 1
    stations, cells = green.shape[2], green.shape[3]
    tile, width, each = stations // n, 4 * cells, coeffs.shape[0]
    here = lax.axis_index("cell").astype(jnp.int32)
    plane = lax.axis_index("freq").astype(jnp.int32)
    core, chip = here % 2, here // 2
    flops = 2 * tile * stations * width * 5 // 4
    moved = 2 * stations * width + 2 * tile * stations

    def dims(which):
        return [(which + j) % bits for j in range(bits)]

    swap_core = [(i, i ^ 1) for i in range(n_cell)]

    def swap_chip(value, j):
        pairs = [(i, i ^ (2 << dims(i % 2)[j])) for i in range(n_cell)]
        return lax.ppermute(value, "cell", pairs)

    def swap_plane(value, j):
        return lax.ppermute(value, "freq", [(i, i ^ (1 << j)) for i in range(n_freq)])

    def piece_of(q):
        flips = [sum(((q >> j) & 1) << dims(which)[j] for j in range(bits)) for which in (0, 1)]
        return chip ^ jnp.where(core == 0, flips[0], flips[1])

    beside = lax.ppermute(coeffs, "cell", swap_core)
    core_only = core.reshape(1)
    two = [pltpu.SemaphoreType.DMA((2,))]
    theirs = call(
        take_kernel, "take", (2, stations, cells), BF16, [SMEM, HBM], 0,
        8 * stations * cells, 59, core_only, green, scratch=two,
    )
    theirs = lax.ppermute(theirs, "cell", swap_core)
    known = jnp.concatenate((coeffs, beside), axis=1)[None]
    for j in range(z_bits):
        known = jnp.concatenate((known, swap_plane(known, j)), axis=0)

    field = call(
        field_kernel, "field", (stations, width), BF16, [SMEM, HBM, HBM], 0,
        4 * stations * width, 56, core_only, green, theirs, scratch=[pltpu.SemaphoreType.DMA((4,))],
    )

    def corr_piece(q):
        return call(
            functools.partial(corr_kernel, n), "corr", (tile, stations), F32 if q % 2 == 0 else BF16,
            [SMEM, SMEM, VMEM, VMEM], flops, moved, 24,
            jnp.stack((core, plane, piece_of(q))), basis, known, field,
        )

    held = {}
    for q in sorted(range(n), key=lambda q: (q % 2 == 0, -q)):
        held[q] = corr_piece(q)
    weight = call(
        functools.partial(weight_kernel, n), "weight", (tile, stations), F32, [SMEM, VMEM, VMEM],
        0, 4 * tile * stations, 8, jnp.stack((core, piece_of(0))), amplitude, block_mask,
    )
    for j in range(bits):
        for q in sorted((q for q in held if (q >> j) & 1), reverse=True):
            got = swap_chip(held.pop(q).astype(BF16), j)
            rest = q ^ (1 << j)
            held[rest] = held[rest] + got.astype(F32)
    resid = {0: (held[0] * weight).astype(BF16)}

    def sens_piece(q):
        return call(
            functools.partial(sens_kernel, n, min(512, width // 2)), "sens", (1, width // 2), F32,
            [SMEM, VMEM, VMEM], flops, moved, 24, piece_of(q).reshape(1), resid[q], field,
        )

    sens = {}
    for j in reversed(range(bits)):
        for q in sorted(resid):
            if q == 0 and 0 in sens:
                sent, sens[0] = lax.optimization_barrier((resid[0], sens[0]))
            else:
                sent = resid[q]
            resid[q | (1 << j)] = swap_chip(sent, j)
            if 0 not in sens:
                sens[0] = sens_piece(0)
    for q in sorted(resid):
        if q not in sens:
            sens[q] = sens_piece(q)
    total = sum(sens.values())

    other = lax.ppermute(total[:, cells:], "cell", swap_core)
    partial = call(
        functools.partial(hess_kernel, n_freq), "hess", (n_freq * each, cells), F32,
        [SMEM, SMEM, VMEM, VMEM], 0, 4 * n_freq * each * cells, 4,
        jnp.stack((core, plane)), basis, total, other,
    )
    for j in reversed(range(z_bits)):
        middle = partial.shape[0] // 2
        partial = partial[:middle] + swap_plane(partial[middle:], j)
    return partial


def solution(mesh):
    placed = (
        P(None, "freq", None, "cell"),
        P("freq", "cell"),
        P("freq", None),
        P("freq", None),
        P(),
    )
    n_freq, n_cell = mesh.shape["freq"], mesh.shape["cell"]
    return jax.shard_map(
        functools.partial(on_device, n_freq, n_cell),
        mesh=mesh,
        in_specs=placed,
        out_specs=P("freq", "cell"),
        check_vma=False,
    )
```

time: 79.1 us -> 83.3 us (1.053)
  local copies, waits for them, and re-layouts: 14.5 us -> 3.56 us
  Pallas kernels: 14 us -> 24.7 us
  waiting for transfers between devices: 25.7 us -> 31.3 us
  other arithmetic: 2.84 us -> 1.42 us
  starting transfers between devices: 21 us -> 21.9 us
    pallas_call x8 -> x12, Pallas kernels: 14 us -> 24.7 us  [call(): pl.pallas_call(kernel, out_shape=jax.ShapeDtypeStruct(shape, dtype), in_s...]
    squeeze x3 -> x0, local copies, waits for them, and re-layouts: 6.46 us -> none  [the longest x2 3.35 us: on_device(): field = jnp.concatenate((mine[0], theirs[0], mine[1], theirs[1]), axis=1)]
    unnamed x24 -> x12, local copies, waits for them, and re-layouts: 6.69 us -> 3.55 us
    ppermute x6, waiting for transfers between devices: 15.9 us -> 18.7 us  [swap_chip(): return lax.ppermute(value, 'cell', pairs)]
    ppermute x6, starting transfers between devices: 9.82 us -> 11.3 us  [swap_chip(): return lax.ppermute(value, 'cell', pairs)]
    ppermute x3, waiting for transfers between devices: 3.53 us -> 4.99 us  [the longest x1 3.91 us: on_device(): beside = lax.ppermute(coeffs, 'cell', swap_core)]
    ppermute x4, waiting for transfers between devices: 6.27 us -> 7.61 us  [swap_plane(): return lax.ppermute(value, 'freq', [(i, i ^ 1 << j) for i in range(n_freq)])]
    gather x3 -> x0, local copies, waits for them, and re-layouts: 1.14 us -> none  [the longest x2 0.58 us: on_device(): basis_near = basis.reshape(2, n_freq, -1)[:, order].reshape(2, -1)]
  transfers between devices with their start and end apart: 13 -> 13, of which waited for: 10 -> 10; matrix products, arithmetic and copies ran while one was open for 6% -> 1% of each run, Pallas kernels for 13% -> 16%
where the time goes in v2:
time: 83.3 us; the launch traced here: 83.1 us
  waiting for transfers between devices  31.3 us (38%)
  Pallas kernels  24.7 us (30%)
  starting transfers between devices  21.9 us (26%)
  local copies, waits for them, and re-layouts  3.56 us (4%)
  other arithmetic  1.42 us (2%)
    pallas_call x12, Pallas kernels, call(): pl.pallas_call(kernel, out_shape=jax.ShapeDtypeStruct(shape, dtype), in_s...  24.7 us
    ppermute x6, waiting for transfers between devices, swap_chip(): return lax.ppermute(value, 'cell', pairs)  18.7 us
    ppermute x6, starting transfers between devices, swap_chip(): return lax.ppermute(value, 'cell', pairs)  11.3 us
    ppermute x4, starting transfers between devices, swap_plane(): return lax.ppermute(value, 'freq', [(i, i ^ 1 << j) for i in range(n_freq)])  9.91 us
    ppermute x4, waiting for transfers between devices, swap_plane(): return lax.ppermute(value, 'freq', [(i, i ^ 1 << j) for i in range(n_freq)])  7.61 us
    ppermute x1, waiting for transfers between devices, on_device(): beside = lax.ppermute(coeffs, 'cell', swap_core)  3.91 us
    unnamed x12, local copies, waits for them, and re-layouts  3.55 us
  transfers between devices with their start and end apart: 13, of which 10 were waited for; matrix products, arithmetic and copies ran while one was open for 1% of the time, Pallas kernels for 16%

profile of v2, /device:TPU:0, one launch (start us, length us, event | category | flops | bytes accessed | tf_op | source)
XLA Modules:
  0.0 83.1 jit_solution(17100228282842961135)
XLA Ops:
  0.0 2.9 %take.1 = bf16[2,1024,512]{2,1,0:T(8,128)(2,1)} custom-call(s32[1]{0:T(128)} %bitcast.core_ref, bf16[2,2,1024,512]{3,2,1,0:T(8,128)(2,1)} %green_ref.3), custom_call_target="tpu_custom_call" | custom-call | bytes 4194304 | tf_op jit(solution)/shard_map/take/pallas_call | solution.py:155
  2.9 0.6 collective-permute-start.3
  3.5 0.1 collective-permute-start
  3.6 3.9 %collective-permute-done = f32[2,512]{1,0:T(2,128)S(1)} collective-permute-done((f32[2,512]{1,0:T(2,128)S(1)}, f32[2,512]{1,0:T(2,128)S(1)}, u32[]{:S(2)}, u32[]{:S(2)}) %collective-permute-start) | collective-permute-done | bytes 4128 | tf_op jit(solution)/shard_map/ppermute | solution.py:194
  7.5 2.9 %collective-permute-start.1 = (f32[1,2,1024]{2,1,0:T(2,128)S(1)}, f32[1,2,1024]{2,1,0:T(2,128)S(1)}, u32[]{:S(2)}, u32[]{:S(2)}) collective-permute-start(f32[1,2,1024]{2,1,0:T(2,128)S(1)} %maximum_bitcast_fusion), channel_id=1, source_target_pairs={{0,8},{8,0},{16,24},{24,16},{1,9},{9,1},{17,25},{25,17},{2,10},{10... | collective-permute-start | bytes 24584 | tf_op jit(solution)/shard_map/ppermute | solution.py:188
  10.4 0.1 pad_add_fusion.3
  10.5 1.6 %collective-permute-done.1 = f32[1,2,1024]{2,1,0:T(2,128)S(1)} collective-permute-done((f32[1,2,1024]{2,1,0:T(2,128)S(1)}, f32[1,2,1024]{2,1,0:T(2,128)S(1)}, u32[]{:S(2)}, u32[]{:S(2)}) %collective-permute-start.1) | collective-permute-done | bytes 8224 | tf_op jit(solution)/shard_map/ppermute | solution.py:188
  12.1 3.1 %collective-permute-start.2 = (f32[2,2,1024]{2,1,0:T(2,128)S(1)}, f32[2,2,1024]{2,1,0:T(2,128)S(1)}, u32[]{:S(2)}, u32[]{:S(2)}) collective-permute-start(f32[2,2,1024]{2,1,0:T(2,128)S(1)} %pad_maximum_fusion.1), channel_id=1, source_target_pairs={{0,16},{8,24},{16,0},{24,8},{1,17},{9,25},{17,1},{25,9},{2,18},{10... | collective-permute-start | bytes 49160 | tf_op jit(solution)/shard_map/ppermute | solution.py:188
  15.2 0.1 pad_add_fusion.1
  15.2 1.6 %collective-permute-done.2 = f32[2,2,1024]{2,1,0:T(2,128)S(1)} collective-permute-done((f32[2,2,1024]{2,1,0:T(2,128)S(1)}, f32[2,2,1024]{2,1,0:T(2,128)S(1)}, u32[]{:S(2)}, u32[]{:S(2)}) %collective-permute-start.2) | collective-permute-done | bytes 16416 | tf_op jit(solution)/shard_map/ppermute | solution.py:188
  16.9 0.0 copy-start.1
  16.9 1.3 %copy-done.4 = bf16[2,1024,512]{2,1,0:T(8,128)(2,1)} copy-done((bf16[2,1024,512]{2,1,0:T(8,128)(2,1)}, bf16[2,1024,512]{2,1,0:T(8,128)(2,1)S(1)}, u32[]{:S(2)}) %copy-start.4) | copy-done | bytes 2097176
  18.3 4.2 %field.1.green_ref = bf16[1024,2048]{1,0:T(8,128)(2,1)} custom-call(s32[1]{0:T(128)} %bitcast.core_ref, bf16[2,2,1024,512]{3,2,1,0:T(8,128)(2,1)} %green_ref.3, bf16[2,1024,512]{2,1,0:T(8,128)(2,1)} %copy-done.4), custom_call_target="tpu_custom_call" | custom-call | bytes 8388608 | tf_op jit(solution)/shard_map/field/pallas_call | solution.py:155
  22.5 2.2 %copy-done = bf16[1024,2048]{1,0:T(8,128)(2,1)S(1)} copy-done((bf16[1024,2048]{1,0:T(8,128)(2,1)S(1)}, bf16[1024,2048]{1,0:T(8,128)(2,1)}, u32[]{:S(2)}) %copy-start) | copy-done | bytes 4194328
  24.6 2.1 %corr.7 = bf16[256,1024]{1,0:T(8,128)(2,1)S(1)} custom-call(s32[3]{0:T(128)S(1)} %get-tuple-element.13.place_ref, f32[2,8]{1,0:T(2,128)S(1)} %copy-done.1, f32[4,2,1024]{2,1,0:T(2,128)S(1)} %pad_maximum_fusion.known_ref, bf16[1024,2048]{1,0:T(8,128)(2,1)S(1)} %copy-done), custom_call_target="tpu_custom_call" | custom-call | flops 1342177280 | bytes 4718592 | tf_op jit(solution)/shard_map/corr/pallas_call | solution.py:155
  26.8 1.9 %collective-permute-start.5 = (bf16[256,1024]{1,0:T(8,128)(2,1)S(1)}, bf16[256,1024]{1,0:T(8,128)(2,1)S(1)}, u32[]{:S(2)}, u32[]{:S(2)}) collective-permute-start(bf16[256,1024]{1,0:T(8,128)(2,1)S(1)} %corr.7), channel_id=1, source_target_pairs={{0,2},{1,5},{2,0},{3,7},{4,6},{5,1},{6,4},{7,3},{8,10},{9,13},{10,... | collective-permute-start | bytes 1572872 | tf_op jit(solution)/shard_map/ppermute | solution.py:185
  28.6 2.1 %corr.5 = bf16[256,1024]{1,0:T(8,128)(2,1)S(1)} custom-call(s32[3]{0:T(128)S(1)} %get-tuple-element.9.place_ref, f32[2,8]{1,0:T(2,128)S(1)} %copy-done.1, f32[4,2,1024]{2,1,0:T(2,128)S(1)} %pad_maximum_fusion.known_ref, bf16[1024,2048]{1,0:T(8,128)(2,1)S(1)} %copy-done), custom_call_target="tpu_custom_call" | custom-call | flops 1342177280 | bytes 4718592 | tf_op jit(solution)/shard_map/corr/pallas_call | solution.py:155
  30.8 0.0 copy-start.2
  30.8 0.0 copy-start.3
  30.8 0.3 collective-permute-start.4
  31.1 2.1 %corr.6 = f32[256,1024]{1,0:T(8,128)S(1)} custom-call(s32[3]{0:T(128)S(1)} %get-tuple-element.12.place_ref, f32[2,8]{1,0:T(2,128)S(1)} %copy-done.1, f32[4,2,1024]{2,1,0:T(2,128)S(1)} %pad_maximum_fusion.known_ref, bf16[1024,2048]{1,0:T(8,128)(2,1)S(1)} %copy-done), custom_call_target="tpu_custom_call" | custom-call | flops 1342177280 | bytes 4718592 | tf_op jit(solution)/shard_map/corr/pallas_call | solution.py:155
  33.2 2.8 %collective-permute-done.5 = bf16[256,1024]{1,0:T(8,128)(2,1)S(1)} collective-permute-done((bf16[256,1024]{1,0:T(8,128)(2,1)S(1)}, bf16[256,1024]{1,0:T(8,128)(2,1)S(1)}, u32[]{:S(2)}, u32[]{:S(2)}) %collective-permute-start.5) | collective-permute-done | bytes 524320 | tf_op jit(solution)/shard_map/ppermute | solution.py:185
  36.0 0.2 add_convert_fusion
  36.2 2.1 %collective-permute-start.6 = (bf16[256,1024]{1,0:T(8,128)(2,1)S(1)}, bf16[256,1024]{1,0:T(8,128)(2,1)S(1)}, u32[]{:S(2)}, u32[]{:S(2)}) collective-permute-start(bf16[256,1024]{1,0:T(8,128)(2,1)S(1)} %add_convert_fusion), channel_id=1, source_target_pairs={{0,4},{1,3},{2,6},{3,1},{4,0},{5,7},{6,2},{7,5},{8,12},{9,11},{10,... | collective-permute-start | bytes 1572872 | tf_op jit(solution)/shard_map/ppermute | solution.py:185
  38.3 0.1 pad_add_fusion.6.place_ref
  38.4 1.0 %weight.1 = f32[256,1024]{1,0:T(8,128)S(1)} custom-call(s32[2]{0:T(128)S(1)} %pad_add_fusion.6.place_ref, f32[2,1024]{1,0:T(2,128)S(1)} %copy-done.2, s32[16,16]{1,0:T(8,128)S(1)} %copy-done.3), custom_call_target="tpu_custom_call" | custom-call | bytes 1048576 | tf_op jit(solution)/shard_map/weight/pallas_call | solution.py:155
  39.3 2.1 %corr.4 = f32[256,1024]{1,0:T(8,128)S(1)} custom-call(s32[3]{0:T(128)S(1)} %get-tuple-element.11.place_ref, f32[2,8]{1,0:T(2,128)S(1)} %copy-done.1, f32[4,2,1024]{2,1,0:T(2,128)S(1)} %pad_maximum_fusion.known_ref, bf16[1024,2048]{1,0:T(8,128)(2,1)S(1)} %copy-done), custom_call_target="tpu_custom_call" | custom-call | flops 1342177280 | bytes 4718592 | tf_op jit(solution)/shard_map/corr/pallas_call | solution.py:155
  41.4 5.7 %collective-permute-done.4 = bf16[256,1024]{1,0:T(8,128)(2,1)S(1)} collective-permute-done((bf16[256,1024]{1,0:T(8,128)(2,1)S(1)}, bf16[256,1024]{1,0:T(8,128)(2,1)S(1)}, u32[]{:S(2)}, u32[]{:S(2)}) %collective-permute-start.4) | collective-permute-done | bytes 524320 | tf_op jit(solution)/shard_map/ppermute | solution.py:185
  47.2 0.0 collective-permute-done.6
  47.2 0.3 multiply_convert_fusion.resid_ref
  47.5 2.0 %collective-permute-start.8 = (bf16[256,1024]{1,0:T(8,128)(2,1)S(1)}, bf16[256,1024]{1,0:T(8,128)(2,1)S(1)}, u32[]{:S(2)}, u32[]{:S(2)}) collective-permute-start(bf16[256,1024]{1,0:T(8,128)(2,1)S(1)} %multiply_convert_fusion.resid_ref), channel_id=1, source_target_pairs={{0,4},{1,3},{2,6},{3,1},{4,0},{5,7},{6,2},{7,5},{8,12},{9,11},{10,... | collective-permute-start | bytes 1572872 | tf_op jit(solution)/shard_map/ppermute | solution.py:185
  49.5 1.9 %sens.4 = f32[1,1024]{1,0:T(1,128)S(1)} custom-call(s32[1]{0:T(128)} %bitcast.2.piece_ref, bf16[256,1024]{1,0:T(8,128)(2,1)S(1)} %multiply_convert_fusion.resid_ref, bf16[1024,2048]{1,0:T(8,128)(2,1)S(1)} %copy-done), custom_call_target="tpu_custom_call" | custom-call | flops 1342177280 | bytes 4718592 | tf_op jit(solution)/shard_map/sens/pallas_call | solution.py:155
  51.4 1.6 %collective-permute-start.7 = (bf16[256,1024]{1,0:T(8,128)(2,1)S(1)}, bf16[256,1024]{1,0:T(8,128)(2,1)S(1)}, u32[]{:S(2)}, u32[]{:S(2)}) collective-permute-start(bf16[256,1024]{1,0:T(8,128)(2,1)S(1)} %multiply_convert_fusion.resid_ref), channel_id=1, source_target_pairs={{0,2},{1,5},{2,0},{3,7},{4,6},{5,1},{6,4},{7,3},{8,10},{9,13},{10,... | collective-permute-start | bytes 1572872 | tf_op jit(solution)/shard_map/ppermute | solution.py:185
  53.0 6.9 %collective-permute-done.8.resid_ref = bf16[256,1024]{1,0:T(8,128)(2,1)S(1)} collective-permute-done((bf16[256,1024]{1,0:T(8,128)(2,1)S(1)}, bf16[256,1024]{1,0:T(8,128)(2,1)S(1)}, u32[]{:S(2)}, u32[]{:S(2)}) %collective-permute-start.8) | collective-permute-done | bytes 524320 | tf_op jit(solution)/shard_map/ppermute | solution.py:185
  59.8 3.5 %collective-permute-start.9 = (bf16[256,1024]{1,0:T(8,128)(2,1)S(1)}, bf16[256,1024]{1,0:T(8,128)(2,1)S(1)}, u32[]{:S(2)}, u32[]{:S(2)}) collective-permute-start(bf16[256,1024]{1,0:T(8,128)(2,1)S(1)} %collective-permute-done.8.resid_ref), channel_id=1, source_target_pairs={{0,2},{1,5},{2,0},{3,7},{4,6},{5,1},{6,4},{7,3},{8,10},{9,13},{10,... | collective-permute-start | bytes 1572872 | tf_op jit(solution)/shard_map/ppermute | solution.py:185
  63.3 1.9 %sens.6 = f32[1,1024]{1,0:T(1,128)S(1)} custom-call(s32[1]{0:T(128)} %bitcast.5.piece_ref, bf16[256,1024]{1,0:T(8,128)(2,1)S(1)} %collective-permute-done.8.resid_ref, bf16[1024,2048]{1,0:T(8,128)(2,1)S(1)} %copy-done), custom_call_target="tpu_custom_call" | custom-call | flops 1342177280 | bytes 4718592 | tf_op jit(solution)/shard_map/sens/pallas_call | solution.py:155
  65.2 1.9 %sens.5 = f32[1,1024]{1,0:T(1,128)S(1)} custom-call(s32[1]{0:T(128)} %bitcast.4.piece_ref, bf16[256,1024]{1,0:T(8,128)(2,1)S(1)} %collective-permute-done.7.resid_ref, bf16[1024,2048]{1,0:T(8,128)(2,1)S(1)} %copy-done), custom_call_target="tpu_custom_call" | custom-call | flops 1342177280 | bytes 4718592 | tf_op jit(solution)/shard_map/sens/pallas_call | solution.py:155
  67.1 3.3 %collective-permute-done.9.resid_ref = bf16[256,1024]{1,0:T(8,128)(2,1)S(1)} collective-permute-done((bf16[256,1024]{1,0:T(8,128)(2,1)S(1)}, bf16[256,1024]{1,0:T(8,128)(2,1)S(1)}, u32[]{:S(2)}, u32[]{:S(2)}) %collective-permute-start.9) | collective-permute-done | bytes 524320 | tf_op jit(solution)/shard_map/ppermute | solution.py:185
  70.5 1.9 %sens.7 = f32[1,1024]{1,0:T(1,128)S(1)} custom-call(s32[1]{0:T(128)} %bitcast.6.piece_ref, bf16[256,1024]{1,0:T(8,128)(2,1)S(1)} %collective-permute-done.9.resid_ref, bf16[1024,2048]{1,0:T(8,128)(2,1)S(1)} %copy-done), custom_call_target="tpu_custom_call" | custom-call | flops 1342177280 | bytes 4718592 | tf_op jit(solution)/shard_map/sens/pallas_call | solution.py:155
  72.4 0.1 collective-permute-start.10
  72.5 0.1 pad_add_fusion.place_ref
  72.5 1.1 %collective-permute-done.10.other_ref = f32[1,512]{1,0:T(1,128)S(1)} collective-permute-done((f32[1,512]{1,0:T(1,128)S(1)}, f32[1,512]{1,0:T(1,128)S(1)}, u32[]{:S(2)}, u32[]{:S(2)}) %collective-permute-start.10) | collective-permute-done | bytes 2080 | tf_op jit(solution)/shard_map/ppermute | solution.py:253
  73.6 0.6 hess.1
  74.2 2.5 %collective-permute-start.11 = (f32[4,512]{1,0:T(4,128)S(1)}, f32[4,512]{1,0:T(4,128)S(1)}, u32[]{:S(2)}, u32[]{:S(2)}) collective-permute-start(f32[4,512]{1,0:T(4,128)S(1)} %slice.22), channel_id=1, source_target_pairs={{0,16},{8,24},{16,0},{24,8},{1,17},{9,25},{17,1},{25,9},{2,18},{10... | collective-permute-start | bytes 24584 | tf_op jit(solution)/shard_map/ppermute | solution.py:188
  76.7 2.2 %collective-permute-done.11 = f32[4,512]{1,0:T(4,128)S(1)} collective-permute-done((f32[4,512]{1,0:T(4,128)S(1)}, f32[4,512]{1,0:T(4,128)S(1)}, u32[]{:S(2)}, u32[]{:S(2)}) %collective-permute-start.11) | collective-permute-done | bytes 8224 | tf_op jit(solution)/shard_map/ppermute | solution.py:188
  78.9 1.4 %collective-permute-start.12 = (f32[2,512]{1,0:T(2,128)S(1)}, f32[2,512]{1,0:T(2,128)S(1)}, u32[]{:S(2)}, u32[]{:S(2)}) collective-permute-start(f32[2,512]{1,0:T(2,128)S(1)} %slice.24), channel_id=1, source_target_pairs={{0,8},{8,0},{16,24},{24,16},{1,9},{9,1},{17,25},{25,17},{2,10},{10... | collective-permute-start | bytes 12296 | tf_op jit(solution)/shard_map/ppermute | solution.py:188
  80.3 2.3 %collective-permute-done.12 = f32[2,512]{1,0:T(2,128)S(1)} collective-permute-done((f32[2,512]{1,0:T(2,128)S(1)}, f32[2,512]{1,0:T(2,128)S(1)}, u32[]{:S(2)}, u32[]{:S(2)}) %collective-permute-start.12) | collective-permute-done | bytes 4128 | tf_op jit(solution)/shard_map/ppermute | solution.py:188
  82.5 0.6 slice_add_fusion.1
  (17 shorter events, 0.1 us)
Async XLA Ops:
  0.0 3.5 %copy-start.5 = (f32[2,512]{1,0:T(2,128)S(1)}, f32[2,512]{1,0:T(2,128)}, u32[]{:S(2)}) copy-start(f32[2,512]{1,0:T(2,128)} %param.6) | copy-start | bytes 12292
  2.9 14.0 %collective-permute-start.3 = (bf16[2,1024,512]{2,1,0:T(8,128)(2,1)}, bf16[2,1024,512]{2,1,0:T(8,128)(2,1)S(1)}, u32[]{:S(2)}, u32[]{:S(2)}) collective-permute-start(bf16[2,1024,512]{2,1,0:T(8,128)(2,1)} %take.1), channel_id=1, source_target_pairs={{0,1},{1,0},{2,3},{3,2},{4,5},{5,4},{6,7},{7,6},{8,9},{9,8},{10,11... | collective-permute-start | bytes 6291464 | tf_op jit(solution)/shard_map/ppermute | solution.py:201
  3.5 4.0 %collective-permute-start = (f32[2,512]{1,0:T(2,128)S(1)}, f32[2,512]{1,0:T(2,128)S(1)}, u32[]{:S(2)}, u32[]{:S(2)}) collective-permute-start(f32[2,512]{1,0:T(2,128)S(1)} %copy-done.5), channel_id=1, source_target_pairs={{0,1},{1,0},{2,3},{3,2},{4,5},{5,4},{6,7},{7,6},{8,9},{9,8},{10,11... | collective-permute-start | bytes 12296 | tf_op jit(solution)/shard_map/ppermute | solution.py:194
  7.5 4.6 %collective-permute-start.1 = (f32[1,2,1024]{2,1,0:T(2,128)S(1)}, f32[1,2,1024]{2,1,0:T(2,128)S(1)}, u32[]{:S(2)}, u32[]{:S(2)}) collective-permute-start(f32[1,2,1024]{2,1,0:T(2,128)S(1)} %maximum_bitcast_fusion), channel_id=1, source_target_pairs={{0,8},{8,0},{16,24},{24,16},{1,9},{9,1},{17,25},{25,17},{2,10},{10... | collective-permute-start | bytes 24584 | tf_op jit(solution)/shard_map/ppermute | solution.py:188
  12.1 4.8 %collective-permute-start.2 = (f32[2,2,1024]{2,1,0:T(2,128)S(1)}, f32[2,2,1024]{2,1,0:T(2,128)S(1)}, u32[]{:S(2)}, u32[]{:S(2)}) collective-permute-start(f32[2,2,1024]{2,1,0:T(2,128)S(1)} %pad_maximum_fusion.1), channel_id=1, source_target_pairs={{0,16},{8,24},{16,0},{24,8},{1,17},{9,25},{17,1},{25,9},{2,18},{10... | collective-permute-start | bytes 49160 | tf_op jit(solution)/shard_map/ppermute | solution.py:188
  16.9 5.5 %copy-start.1 = (f32[2,8]{1,0:T(2,128)S(1)}, f32[2,8]{1,0:T(2,128)}, u32[]{:S(2)}) copy-start(f32[2,8]{1,0:T(2,128)} %basis_ref.9) | copy-start | bytes 196
  16.9 1.4 %copy-start.4 = (bf16[2,1024,512]{2,1,0:T(8,128)(2,1)}, bf16[2,1024,512]{2,1,0:T(8,128)(2,1)S(1)}, u32[]{:S(2)}) copy-start(bf16[2,1024,512]{2,1,0:T(8,128)(2,1)S(1)} %collective-permute-done.3.theirs_ref) | copy-start | bytes 6291460
  22.4 2.2 %copy-start = (bf16[1024,2048]{1,0:T(8,128)(2,1)S(1)}, bf16[1024,2048]{1,0:T(8,128)(2,1)}, u32[]{:S(2)}) copy-start(bf16[1024,2048]{1,0:T(8,128)(2,1)} %field.1.green_ref) | copy-start | bytes 12582916
  26.8 9.2 %collective-permute-start.5 = (bf16[256,1024]{1,0:T(8,128)(2,1)S(1)}, bf16[256,1024]{1,0:T(8,128)(2,1)S(1)}, u32[]{:S(2)}, u32[]{:S(2)}) collective-permute-start(bf16[256,1024]{1,0:T(8,128)(2,1)S(1)} %corr.7), channel_id=1, source_target_pairs={{0,2},{1,5},{2,0},{3,7},{4,6},{5,1},{6,4},{7,3},{8,10},{9,13},{10,... | collective-permute-start | bytes 1572872 | tf_op jit(solution)/shard_map/ppermute | solution.py:185
  30.8 7.6 %copy-start.2 = (f32[2,1024]{1,0:T(2,128)S(1)}, f32[2,1024]{1,0:T(2,128)}, u32[]{:S(2)}) copy-start(f32[2,1024]{1,0:T(2,128)} %amp_ref.1) | copy-start | bytes 24580
  30.8 7.6 %copy-start.3 = (s32[16,16]{1,0:T(8,128)S(1)}, s32[16,16]{1,0:T(8,128)}, u32[]{:S(2)}) copy-start(s32[16,16]{1,0:T(8,128)} %mask_ref.1) | copy-start | bytes 3076
  30.8 16.4 %collective-permute-start.4 = (bf16[256,1024]{1,0:T(8,128)(2,1)S(1)}, bf16[256,1024]{1,0:T(8,128)(2,1)S(1)}, u32[]{:S(2)}, u32[]{:S(2)}) collective-permute-start(bf16[256,1024]{1,0:T(8,128)(2,1)S(1)} %corr.5), channel_id=1, source_target_pairs={{0,2},{1,5},{2,0},{3,7},{4,6},{5,1},{6,4},{7,3},{8,10},{9,13},{10,... | collective-permute-start | bytes 1572872 | tf_op jit(solution)/shard_map/ppermute | solution.py:185
  36.2 11.0 %collective-permute-start.6 = (bf16[256,1024]{1,0:T(8,128)(2,1)S(1)}, bf16[256,1024]{1,0:T(8,128)(2,1)S(1)}, u32[]{:S(2)}, u32[]{:S(2)}) collective-permute-start(bf16[256,1024]{1,0:T(8,128)(2,1)S(1)} %add_convert_fusion), channel_id=1, source_target_pairs={{0,4},{1,3},{2,6},{3,1},{4,0},{5,7},{6,2},{7,5},{8,12},{9,11},{10,... | collective-permute-start | bytes 1572872 | tf_op jit(solution)/shard_map/ppermute | solution.py:185
  47.5 12.3 %collective-permute-start.8 = (bf16[256,1024]{1,0:T(8,128)(2,1)S(1)}, bf16[256,1024]{1,0:T(8,128)(2,1)S(1)}, u32[]{:S(2)}, u32[]{:S(2)}) collective-permute-start(bf16[256,1024]{1,0:T(8,128)(2,1)S(1)} %multiply_convert_fusion.resid_ref), channel_id=1, source_target_pairs={{0,4},{1,3},{2,6},{3,1},{4,0},{5,7},{6,2},{7,5},{8,12},{9,11},{10,... | collective-permute-start | bytes 1572872 | tf_op jit(solution)/shard_map/ppermute | solution.py:185
  51.4 13.8 %collective-permute-start.7 = (bf16[256,1024]{1,0:T(8,128)(2,1)S(1)}, bf16[256,1024]{1,0:T(8,128)(2,1)S(1)}, u32[]{:S(2)}, u32[]{:S(2)}) collective-permute-start(bf16[256,1024]{1,0:T(8,128)(2,1)S(1)} %multiply_convert_fusion.resid_ref), channel_id=1, source_target_pairs={{0,2},{1,5},{2,0},{3,7},{4,6},{5,1},{6,4},{7,3},{8,10},{9,13},{10,... | collective-permute-start | bytes 1572872 | tf_op jit(solution)/shard_map/ppermute | solution.py:185
  59.8 10.6 %collective-permute-start.9 = (bf16[256,1024]{1,0:T(8,128)(2,1)S(1)}, bf16[256,1024]{1,0:T(8,128)(2,1)S(1)}, u32[]{:S(2)}, u32[]{:S(2)}) collective-permute-start(bf16[256,1024]{1,0:T(8,128)(2,1)S(1)} %collective-permute-done.8.resid_ref), channel_id=1, source_target_pairs={{0,2},{1,5},{2,0},{3,7},{4,6},{5,1},{6,4},{7,3},{8,10},{9,13},{10,... | collective-permute-start | bytes 1572872 | tf_op jit(solution)/shard_map/ppermute | solution.py:185
  72.4 1.2 %collective-permute-start.10 = (f32[1,512]{1,0:T(1,128)S(1)}, f32[1,512]{1,0:T(1,128)S(1)}, u32[]{:S(2)}, u32[]{:S(2)}) collective-permute-start(f32[1,512]{1,0:T(1,128)S(1)} %slice.20), channel_id=1, source_target_pairs={{0,1},{1,0},{2,3},{3,2},{4,5},{5,4},{6,7},{7,6},{8,9},{9,8},{10,11... | collective-permute-start | bytes 6152 | tf_op jit(solution)/shard_map/ppermute | solution.py:253
  74.2 4.6 %collective-permute-start.11 = (f32[4,512]{1,0:T(4,128)S(1)}, f32[4,512]{1,0:T(4,128)S(1)}, u32[]{:S(2)}, u32[]{:S(2)}) collective-permute-start(f32[4,512]{1,0:T(4,128)S(1)} %slice.22), channel_id=1, source_target_pairs={{0,16},{8,24},{16,0},{24,8},{1,17},{9,25},{17,1},{25,9},{2,18},{10... | collective-permute-start | bytes 24584 | tf_op jit(solution)/shard_map/ppermute | solution.py:188
  78.9 3.7 %collective-permute-start.12 = (f32[2,512]{1,0:T(2,128)S(1)}, f32[2,512]{1,0:T(2,128)S(1)}, u32[]{:S(2)}, u32[]{:S(2)}) collective-permute-start(f32[2,512]{1,0:T(2,128)S(1)} %slice.24), channel_id=1, source_target_pairs={{0,8},{8,0},{16,24},{24,16},{1,9},{9,1},{17,25},{25,17},{2,10},{10... | collective-permute-start | bytes 12296 | tf_op jit(solution)/shard_map/ppermute | solution.py:188

commit v3 on v2

--- a/solution.py
+++ b/solution.py
@@ -6,6 +6,7 @@
 from jax.experimental import pallas as pl
 from jax.experimental.pallas import tpu as pltpu
 from jax.sharding import PartitionSpec as P
+
 
 F32 = jnp.float32
 BF16 = jnp.bfloat16
@@ -151,7 +152,7 @@
 HBM = pl.BlockSpec(memory_space=pltpu.HBM)
 
 
-def call(kernel, name, shape, dtype, specs, flops, moved, grant, *args, scratch=()):
+def call(kernel, shape, dtype, specs, flops, moved, grant, *args, scratch=()):
     return pl.pallas_call(
         kernel,
         out_shape=jax.ShapeDtypeStruct(shape, dtype),
@@ -160,7 +161,6 @@
         scratch_shapes=scratch,
         compiler_params=pltpu.CompilerParams(vmem_limit_bytes=grant * MIB),
         cost_estimate=pl.CostEstimate(flops=flops, bytes_accessed=moved, transcendentals=0),
-        name=name,
     )(*args)
 
 
@@ -195,22 +195,23 @@
     core_only = core.reshape(1)
     two = [pltpu.SemaphoreType.DMA((2,))]
     theirs = call(
-        take_kernel, "take", (2, stations, cells), BF16, [SMEM, HBM], 0,
-        8 * stations * cells, 59, core_only, green, scratch=two,
+        take_kernel, (2, stations, cells), BF16, [SMEM, HBM], 0,
+        8 * stations * cells, 50, core_only, green, scratch=two,
     )
     theirs = lax.ppermute(theirs, "cell", swap_core)
     known = jnp.concatenate((coeffs, beside), axis=1)[None]
     for j in range(z_bits):
-        known = jnp.concatenate((known, swap_plane(known, j)), axis=0)
+        near = swap_plane(known, j)
+        known = jnp.concatenate((known, near), axis=0)
 
     field = call(
-        field_kernel, "field", (stations, width), BF16, [SMEM, HBM, HBM], 0,
-        4 * stations * width, 56, core_only, green, theirs, scratch=[pltpu.SemaphoreType.DMA((4,))],
+        field_kernel, (stations, width), BF16, [SMEM, HBM, HBM], 0,
+        4 * stations * width, 45, core_only, green, theirs, scratch=[pltpu.SemaphoreType.DMA((4,))],
     )
 
     def corr_piece(q):
         return call(
-            functools.partial(corr_kernel, n), "corr", (tile, stations), F32 if q % 2 == 0 else BF16,
+            functools.partial(corr_kernel, n), (tile, stations), F32 if q % 2 == 0 else BF16,
             [SMEM, SMEM, VMEM, VMEM], flops, moved, 24,
             jnp.stack((core, plane, piece_of(q))), basis, known, field,
         )
@@ -219,7 +220,7 @@
     for q in sorted(range(n), key=lambda q: (q % 2 == 0, -q)):
         held[q] = corr_piece(q)
     weight = call(
-        functools.partial(weight_kernel, n), "weight", (tile, stations), F32, [SMEM, VMEM, VMEM],
+        functools.partial(weight_kernel, n), (tile, stations), F32, [SMEM, VMEM, VMEM],
         0, 4 * tile * stations, 8, jnp.stack((core, piece_of(0))), amplitude, block_mask,
     )
     for j in range(bits):
@@ -231,7 +232,7 @@
 
     def sens_piece(q):
         return call(
-            functools.partial(sens_kernel, n, min(512, width // 2)), "sens", (1, width // 2), F32,
+            functools.partial(sens_kernel, n, min(512, width // 2)), (1, width // 2), F32,
             [SMEM, VMEM, VMEM], flops, moved, 24, piece_of(q).reshape(1), resid[q], field,
         )
 
@@ -252,7 +253,7 @@
 
     other = lax.ppermute(total[:, cells:], "cell", swap_core)
     partial = call(
-        functools.partial(hess_kernel, n_freq), "hess", (n_freq * each, cells), F32,
+        functools.partial(hess_kernel, n_freq), (n_freq * each, cells), F32,
         [SMEM, SMEM, VMEM, VMEM], 0, 4 * n_freq * each * cells, 4,
         jnp.stack((core, plane)), basis, total, other,
     )
@@ -271,10 +272,10 @@
         P(),
     )
     n_freq, n_cell = mesh.shape["freq"], mesh.shape["cell"]
+
+    def body(*args):
+        return on_device(n_freq, n_cell, *args)
+
     return jax.shard_map(
-        functools.partial(on_device, n_freq, n_cell),
-        mesh=mesh,
-        in_specs=placed,
-        out_specs=P("freq", "cell"),
-        check_vma=False,
-    )
+        body, mesh=mesh, in_specs=placed, out_specs=P("freq", "cell"), check_vma=False
+    )

time: 83.3 us -> 76.3 us (0.916)
  local copies, waits for them, and re-layouts: 3.56 us -> 0.04 us
  Pallas kernels: 24.7 us -> 21.6 us
    unnamed x12 -> x8, local copies, waits for them, and re-layouts: 3.55 us -> 0.02 us
    pallas_call x12, Pallas kernels: 24.7 us -> 21.6 us  [call(): pl.pallas_call(kernel, out_shape=jax.ShapeDtypeStruct(shape, dtype), in_s...]
  transfers between devices with their start and end apart: 13 -> 13, of which waited for: 10 -> 10; matrix products, arithmetic and copies ran while one was open for 1% -> 1% of each run, Pallas kernels for 16% -> 17%
where the time goes in v3:
time: 76.3 us; the launch traced here: 76.2 us
  waiting for transfers between devices  31 us (41%)
  starting transfers between devices  22 us (29%)
  Pallas kernels  21.6 us (28%)
  other arithmetic  1.39 us (2%)
    pallas_call x12, Pallas kernels, call(): pl.pallas_call(kernel, out_shape=jax.ShapeDtypeStruct(shape, dtype), in_s...  21.6 us
    ppermute x6, waiting for transfers between devices, swap_chip(): return lax.ppermute(value, 'cell', pairs)  18.6 us
    ppermute x6, starting transfers between devices, swap_chip(): return lax.ppermute(value, 'cell', pairs)  11.2 us
    ppermute x4, starting transfers between devices, swap_plane(): return lax.ppermute(value, 'freq', [(i, i ^ 1 << j) for i in range(n_freq)])  10 us
    ppermute x4, waiting for transfers between devices, swap_plane(): return lax.ppermute(value, 'freq', [(i, i ^ 1 << j) for i in range(n_freq)])  7.53 us
    ppermute x1, waiting for transfers between devices, on_device(): beside = lax.ppermute(coeffs, 'cell', swap_core)  3.83 us
  transfers between devices with their start and end apart: 13, of which 10 were waited for; matrix products, arithmetic and copies ran while one was open for 1% of the time, Pallas kernels for 17%

profile of v3, /device:TPU:0, one launch (start us, length us, event | category | flops | bytes accessed | tf_op | source)
XLA Modules:
  0.0 76.2 jit_solution(8521725892113751857)
XLA Ops:
  0.0 1.6 %shard_map.55 = bf16[2,1024,512]{2,1,0:T(8,128)(2,1)S(1)} custom-call(s32[1]{0:T(128)} %bitcast.core_ref, bf16[2,2,1024,512]{3,2,1,0:T(8,128)(2,1)} %green_ref.3), custom_call_target="tpu_custom_call" | custom-call | bytes 4194304 | tf_op jit(solution)/shard_map/pallas_call | solution.py:156
  1.6 0.6 collective-permute-start.3
  2.1 0.1 collective-permute-start
  2.2 3.8 %collective-permute-done = f32[2,512]{1,0:T(2,128)S(1)} collective-permute-done((f32[2,512]{1,0:T(2,128)S(1)}, f32[2,512]{1,0:T(2,128)S(1)}, u32[]{:S(2)}, u32[]{:S(2)}) %collective-permute-start) | collective-permute-done | bytes 4128 | tf_op jit(solution)/shard_map/ppermute | solution.py:194
  6.1 2.9 %collective-permute-start.1 = (f32[1,2,1024]{2,1,0:T(2,128)S(1)}, f32[1,2,1024]{2,1,0:T(2,128)S(1)}, u32[]{:S(2)}, u32[]{:S(2)}) collective-permute-start(f32[1,2,1024]{2,1,0:T(2,128)S(1)} %maximum_bitcast_fusion), channel_id=1, source_target_pairs={{0,8},{8,0},{16,24},{24,16},{1,9},{9,1},{17,25},{25,17},{2,10},{10... | collective-permute-start | bytes 24584 | tf_op jit(solution)/shard_map/ppermute | solution.py:188
  9.0 0.1 pad_add_fusion.3
  9.1 1.6 %collective-permute-done.1 = f32[1,2,1024]{2,1,0:T(2,128)S(1)} collective-permute-done((f32[1,2,1024]{2,1,0:T(2,128)S(1)}, f32[1,2,1024]{2,1,0:T(2,128)S(1)}, u32[]{:S(2)}, u32[]{:S(2)}) %collective-permute-start.1) | collective-permute-done | bytes 8224 | tf_op jit(solution)/shard_map/ppermute | solution.py:188
  10.6 3.1 %collective-permute-start.2 = (f32[2,2,1024]{2,1,0:T(2,128)S(1)}, f32[2,2,1024]{2,1,0:T(2,128)S(1)}, u32[]{:S(2)}, u32[]{:S(2)}) collective-permute-start(f32[2,2,1024]{2,1,0:T(2,128)S(1)} %pad_maximum_fusion.1), channel_id=1, source_target_pairs={{0,16},{8,24},{16,0},{24,8},{1,17},{9,25},{17,1},{25,9},{2,18},{10... | collective-permute-start | bytes 49160 | tf_op jit(solution)/shard_map/ppermute | solution.py:188
  13.7 0.1 pad_add_fusion.1
  13.8 1.6 %collective-permute-done.2 = f32[2,2,1024]{2,1,0:T(2,128)S(1)} collective-permute-done((f32[2,2,1024]{2,1,0:T(2,128)S(1)}, f32[2,2,1024]{2,1,0:T(2,128)S(1)}, u32[]{:S(2)}, u32[]{:S(2)}) %collective-permute-start.2) | collective-permute-done | bytes 16416 | tf_op jit(solution)/shard_map/ppermute | solution.py:188
  15.5 0.0 copy-start
  15.5 0.0 collective-permute-done.3.theirs_ref
  15.5 2.2 %shard_map.56.green_ref = bf16[1024,2048]{1,0:T(8,128)(2,1)S(1)} custom-call(s32[1]{0:T(128)} %bitcast.core_ref, bf16[2,2,1024,512]{3,2,1,0:T(8,128)(2,1)} %green_ref.3, bf16[2,1024,512]{2,1,0:T(8,128)(2,1)} %collective-permute-done.3.theirs_ref), custom_call_target="tpu_custom_call" | custom-call | bytes 8388608 | tf_op jit(solution)/shard_map/pallas_call | solution.py:156
  17.7 2.1 %shard_map.60 = bf16[256,1024]{1,0:T(8,128)(2,1)S(1)} custom-call(s32[3]{0:T(128)S(1)} %get-tuple-element.13.place_ref, f32[2,8]{1,0:T(2,128)S(1)} %copy-done, f32[4,2,1024]{2,1,0:T(2,128)S(1)} %pad_maximum_fusion.known_ref, bf16[1024,2048]{1,0:T(8,128)(2,1)S(1)} %shard_map.56.green_ref), custom_call_target="tpu_custom_call" | custom-call | flops 1342177280 | bytes 4718592 | tf_op jit(solution)/shard_map/pallas_call | solution.py:156
  19.9 1.9 %collective-permute-start.5 = (bf16[256,1024]{1,0:T(8,128)(2,1)S(1)}, bf16[256,1024]{1,0:T(8,128)(2,1)S(1)}, u32[]{:S(2)}, u32[]{:S(2)}) collective-permute-start(bf16[256,1024]{1,0:T(8,128)(2,1)S(1)} %shard_map.60), channel_id=1, source_target_pairs={{0,2},{1,5},{2,0},{3,7},{4,6},{5,1},{6,4},{7,3},{8,10},{9,13},{10,... | collective-permute-start | bytes 1572872 | tf_op jit(solution)/shard_map/ppermute | solution.py:185
  21.8 2.1 %shard_map.58 = bf16[256,1024]{1,0:T(8,128)(2,1)S(1)} custom-call(s32[3]{0:T(128)S(1)} %get-tuple-element.9.place_ref, f32[2,8]{1,0:T(2,128)S(1)} %copy-done, f32[4,2,1024]{2,1,0:T(2,128)S(1)} %pad_maximum_fusion.known_ref, bf16[1024,2048]{1,0:T(8,128)(2,1)S(1)} %shard_map.56.green_ref), custom_call_target="tpu_custom_call" | custom-call | flops 1342177280 | bytes 4718592 | tf_op jit(solution)/shard_map/pallas_call | solution.py:156
  23.9 0.0 copy-start.1
  23.9 0.0 copy-start.2
  23.9 0.3 collective-permute-start.4
  24.2 2.1 %shard_map.59 = f32[256,1024]{1,0:T(8,128)S(1)} custom-call(s32[3]{0:T(128)S(1)} %get-tuple-element.12.place_ref, f32[2,8]{1,0:T(2,128)S(1)} %copy-done, f32[4,2,1024]{2,1,0:T(2,128)S(1)} %pad_maximum_fusion.known_ref, bf16[1024,2048]{1,0:T(8,128)(2,1)S(1)} %shard_map.56.green_ref), custom_call_target="tpu_custom_call" | custom-call | flops 1342177280 | bytes 4718592 | tf_op jit(solution)/shard_map/pallas_call | solution.py:156
  26.3 2.8 %collective-permute-done.5 = bf16[256,1024]{1,0:T(8,128)(2,1)S(1)} collective-permute-done((bf16[256,1024]{1,0:T(8,128)(2,1)S(1)}, bf16[256,1024]{1,0:T(8,128)(2,1)S(1)}, u32[]{:S(2)}, u32[]{:S(2)}) %collective-permute-start.5) | collective-permute-done | bytes 524320 | tf_op jit(solution)/shard_map/ppermute | solution.py:185
  29.1 0.1 add_convert_fusion
  29.3 2.1 %collective-permute-start.6 = (bf16[256,1024]{1,0:T(8,128)(2,1)S(1)}, bf16[256,1024]{1,0:T(8,128)(2,1)S(1)}, u32[]{:S(2)}, u32[]{:S(2)}) collective-permute-start(bf16[256,1024]{1,0:T(8,128)(2,1)S(1)} %add_convert_fusion), channel_id=1, source_target_pairs={{0,4},{1,3},{2,6},{3,1},{4,0},{5,7},{6,2},{7,5},{8,12},{9,11},{10,... | collective-permute-start | bytes 1572872 | tf_op jit(solution)/shard_map/ppermute | solution.py:185
  31.4 0.1 pad_add_fusion.6.place_ref
  31.5 1.0 %shard_map.61 = f32[256,1024]{1,0:T(8,128)S(1)} custom-call(s32[2]{0:T(128)S(1)} %pad_add_fusion.6.place_ref, f32[2,1024]{1,0:T(2,128)S(1)} %copy-done.1, s32[16,16]{1,0:T(8,128)S(1)} %copy-done.2), custom_call_target="tpu_custom_call" | custom-call | bytes 1048576 | tf_op jit(solution)/shard_map/pallas_call | solution.py:156
  32.4 2.1 %shard_map.57 = f32[256,1024]{1,0:T(8,128)S(1)} custom-call(s32[3]{0:T(128)S(1)} %get-tuple-element.11.place_ref, f32[2,8]{1,0:T(2,128)S(1)} %copy-done, f32[4,2,1024]{2,1,0:T(2,128)S(1)} %pad_maximum_fusion.known_ref, bf16[1024,2048]{1,0:T(8,128)(2,1)S(1)} %shard_map.56.green_ref), custom_call_target="tpu_custom_call" | custom-call | flops 1342177280 | bytes 4718592 | tf_op jit(solution)/shard_map/pallas_call | solution.py:156
  34.6 5.7 %collective-permute-done.4 = bf16[256,1024]{1,0:T(8,128)(2,1)S(1)} collective-permute-done((bf16[256,1024]{1,0:T(8,128)(2,1)S(1)}, bf16[256,1024]{1,0:T(8,128)(2,1)S(1)}, u32[]{:S(2)}, u32[]{:S(2)}) %collective-permute-start.4) | collective-permute-done | bytes 524320 | tf_op jit(solution)/shard_map/ppermute | solution.py:185
  40.3 0.0 collective-permute-done.6
  40.3 0.3 multiply_convert_fusion.resid_ref
  40.6 2.0 %collective-permute-start.8 = (bf16[256,1024]{1,0:T(8,128)(2,1)S(1)}, bf16[256,1024]{1,0:T(8,128)(2,1)S(1)}, u32[]{:S(2)}, u32[]{:S(2)}) collective-permute-start(bf16[256,1024]{1,0:T(8,128)(2,1)S(1)} %multiply_convert_fusion.resid_ref), channel_id=1, source_target_pairs={{0,4},{1,3},{2,6},{3,1},{4,0},{5,7},{6,2},{7,5},{8,12},{9,11},{10,... | collective-permute-start | bytes 1572872 | tf_op jit(solution)/shard_map/ppermute | solution.py:185
  42.6 1.9 %shard_map.62 = f32[1,1024]{1,0:T(1,128)S(1)} custom-call(s32[1]{0:T(128)} %bitcast.2.piece_ref, bf16[256,1024]{1,0:T(8,128)(2,1)S(1)} %multiply_convert_fusion.resid_ref, bf16[1024,2048]{1,0:T(8,128)(2,1)S(1)} %shard_map.56.green_ref), custom_call_target="tpu_custom_call" | custom-call | flops 1342177280 | bytes 4718592 | tf_op jit(solution)/shard_map/pallas_call | solution.py:156
  44.5 1.5 %collective-permute-start.7 = (bf16[256,1024]{1,0:T(8,128)(2,1)S(1)}, bf16[256,1024]{1,0:T(8,128)(2,1)S(1)}, u32[]{:S(2)}, u32[]{:S(2)}) collective-permute-start(bf16[256,1024]{1,0:T(8,128)(2,1)S(1)} %multiply_convert_fusion.resid_ref), channel_id=1, source_target_pairs={{0,2},{1,5},{2,0},{3,7},{4,6},{5,1},{6,4},{7,3},{8,10},{9,13},{10,... | collective-permute-start | bytes 1572872 | tf_op jit(solution)/shard_map/ppermute | solution.py:185
  46.1 6.8 %collective-permute-done.8.resid_ref = bf16[256,1024]{1,0:T(8,128)(2,1)S(1)} collective-permute-done((bf16[256,1024]{1,0:T(8,128)(2,1)S(1)}, bf16[256,1024]{1,0:T(8,128)(2,1)S(1)}, u32[]{:S(2)}, u32[]{:S(2)}) %collective-permute-start.8) | collective-permute-done | bytes 524320 | tf_op jit(solution)/shard_map/ppermute | solution.py:185
  52.9 3.4 %collective-permute-start.9 = (bf16[256,1024]{1,0:T(8,128)(2,1)S(1)}, bf16[256,1024]{1,0:T(8,128)(2,1)S(1)}, u32[]{:S(2)}, u32[]{:S(2)}) collective-permute-start(bf16[256,1024]{1,0:T(8,128)(2,1)S(1)} %collective-permute-done.8.resid_ref), channel_id=1, source_target_pairs={{0,2},{1,5},{2,0},{3,7},{4,6},{5,1},{6,4},{7,3},{8,10},{9,13},{10,... | collective-permute-start | bytes 1572872 | tf_op jit(solution)/shard_map/ppermute | solution.py:185
  56.3 1.9 %shard_map.64 = f32[1,1024]{1,0:T(1,128)S(1)} custom-call(s32[1]{0:T(128)} %bitcast.5.piece_ref, bf16[256,1024]{1,0:T(8,128)(2,1)S(1)} %collective-permute-done.8.resid_ref, bf16[1024,2048]{1,0:T(8,128)(2,1)S(1)} %shard_map.56.green_ref), custom_call_target="tpu_custom_call" | custom-call | flops 1342177280 | bytes 4718592 | tf_op jit(solution)/shard_map/pallas_call | solution.py:156
  58.3 0.0 collective-permute-done.7.resid_ref
  58.3 1.9 %shard_map.63 = f32[1,1024]{1,0:T(1,128)S(1)} custom-call(s32[1]{0:T(128)} %bitcast.4.piece_ref, bf16[256,1024]{1,0:T(8,128)(2,1)S(1)} %collective-permute-done.7.resid_ref, bf16[1024,2048]{1,0:T(8,128)(2,1)S(1)} %shard_map.56.green_ref), custom_call_target="tpu_custom_call" | custom-call | flops 1342177280 | bytes 4718592 | tf_op jit(solution)/shard_map/pallas_call | solution.py:156
  60.2 3.3 %collective-permute-done.9.resid_ref = bf16[256,1024]{1,0:T(8,128)(2,1)S(1)} collective-permute-done((bf16[256,1024]{1,0:T(8,128)(2,1)S(1)}, bf16[256,1024]{1,0:T(8,128)(2,1)S(1)}, u32[]{:S(2)}, u32[]{:S(2)}) %collective-permute-start.9) | collective-permute-done | bytes 524320 | tf_op jit(solution)/shard_map/ppermute | solution.py:185
  63.5 1.9 %shard_map.65 = f32[1,1024]{1,0:T(1,128)S(1)} custom-call(s32[1]{0:T(128)} %bitcast.6.piece_ref, bf16[256,1024]{1,0:T(8,128)(2,1)S(1)} %collective-permute-done.9.resid_ref, bf16[1024,2048]{1,0:T(8,128)(2,1)S(1)} %shard_map.56.green_ref), custom_call_target="tpu_custom_call" | custom-call | flops 1342177280 | bytes 4718592 | tf_op jit(solution)/shard_map/pallas_call | solution.py:156
  65.5 0.1 collective-permute-start.10
  65.5 0.1 pad_add_fusion.place_ref
  65.6 1.1 %collective-permute-done.10.other_ref = f32[1,512]{1,0:T(1,128)S(1)} collective-permute-done((f32[1,512]{1,0:T(1,128)S(1)}, f32[1,512]{1,0:T(1,128)S(1)}, u32[]{:S(2)}, u32[]{:S(2)}) %collective-permute-start.10) | collective-permute-done | bytes 2080 | tf_op jit(solution)/shard_map/ppermute | solution.py:254
  66.7 0.6 shard_map.66
  67.3 2.5 %collective-permute-start.11 = (f32[4,512]{1,0:T(4,128)S(1)}, f32[4,512]{1,0:T(4,128)S(1)}, u32[]{:S(2)}, u32[]{:S(2)}) collective-permute-start(f32[4,512]{1,0:T(4,128)S(1)} %slice.22), channel_id=1, source_target_pairs={{0,16},{8,24},{16,0},{24,8},{1,17},{9,25},{17,1},{25,9},{2,18},{10... | collective-permute-start | bytes 24584 | tf_op jit(solution)/shard_map/ppermute | solution.py:188
  69.8 2.1 %collective-permute-done.11 = f32[4,512]{1,0:T(4,128)S(1)} collective-permute-done((f32[4,512]{1,0:T(4,128)S(1)}, f32[4,512]{1,0:T(4,128)S(1)}, u32[]{:S(2)}, u32[]{:S(2)}) %collective-permute-start.11) | collective-permute-done | bytes 8224 | tf_op jit(solution)/shard_map/ppermute | solution.py:188
  71.9 1.5 %collective-permute-start.12 = (f32[2,512]{1,0:T(2,128)S(1)}, f32[2,512]{1,0:T(2,128)S(1)}, u32[]{:S(2)}, u32[]{:S(2)}) collective-permute-start(f32[2,512]{1,0:T(2,128)S(1)} %slice.24), channel_id=1, source_target_pairs={{0,8},{8,0},{16,24},{24,16},{1,9},{9,1},{17,25},{25,17},{2,10},{10... | collective-permute-start | bytes 12296 | tf_op jit(solution)/shard_map/ppermute | solution.py:188
  73.4 2.2 %collective-permute-done.12 = f32[2,512]{1,0:T(2,128)S(1)} collective-permute-done((f32[2,512]{1,0:T(2,128)S(1)}, f32[2,512]{1,0:T(2,128)S(1)}, u32[]{:S(2)}, u32[]{:S(2)}) %collective-permute-start.12) | collective-permute-done | bytes 4128 | tf_op jit(solution)/shard_map/ppermute | solution.py:188
  75.6 0.6 slice_add_fusion.1
  (13 shorter events, 0.1 us)
Async XLA Ops:
  0.0 2.1 %copy-start.3 = (f32[2,512]{1,0:T(2,128)S(1)}, f32[2,512]{1,0:T(2,128)}, u32[]{:S(2)}) copy-start(f32[2,512]{1,0:T(2,128)} %param.6) | copy-start | bytes 12292
  1.6 13.9 %collective-permute-start.3 = (bf16[2,1024,512]{2,1,0:T(8,128)(2,1)S(1)}, bf16[2,1024,512]{2,1,0:T(8,128)(2,1)}, u32[]{:S(2)}, u32[]{:S(2)}) collective-permute-start(bf16[2,1024,512]{2,1,0:T(8,128)(2,1)S(1)} %shard_map.55), channel_id=1, source_target_pairs={{0,1},{1,0},{2,3},{3,2},{4,5},{5,4},{6,7},{7,6},{8,9},{9,8},{10,11... | collective-permute-start | bytes 6291464 | tf_op jit(solution)/shard_map/ppermute | solution.py:201
  2.1 3.9 %collective-permute-start = (f32[2,512]{1,0:T(2,128)S(1)}, f32[2,512]{1,0:T(2,128)S(1)}, u32[]{:S(2)}, u32[]{:S(2)}) collective-permute-start(f32[2,512]{1,0:T(2,128)S(1)} %copy-done.3), channel_id=1, source_target_pairs={{0,1},{1,0},{2,3},{3,2},{4,5},{5,4},{6,7},{7,6},{8,9},{9,8},{10,11... | collective-permute-start | bytes 12296 | tf_op jit(solution)/shard_map/ppermute | solution.py:194
  6.1 4.6 %collective-permute-start.1 = (f32[1,2,1024]{2,1,0:T(2,128)S(1)}, f32[1,2,1024]{2,1,0:T(2,128)S(1)}, u32[]{:S(2)}, u32[]{:S(2)}) collective-permute-start(f32[1,2,1024]{2,1,0:T(2,128)S(1)} %maximum_bitcast_fusion), channel_id=1, source_target_pairs={{0,8},{8,0},{16,24},{24,16},{1,9},{9,1},{17,25},{25,17},{2,10},{10... | collective-permute-start | bytes 24584 | tf_op jit(solution)/shard_map/ppermute | solution.py:188
  10.6 4.8 %collective-permute-start.2 = (f32[2,2,1024]{2,1,0:T(2,128)S(1)}, f32[2,2,1024]{2,1,0:T(2,128)S(1)}, u32[]{:S(2)}, u32[]{:S(2)}) collective-permute-start(f32[2,2,1024]{2,1,0:T(2,128)S(1)} %pad_maximum_fusion.1), channel_id=1, source_target_pairs={{0,16},{8,24},{16,0},{24,8},{1,17},{9,25},{17,1},{25,9},{2,18},{10... | collective-permute-start | bytes 49160 | tf_op jit(solution)/shard_map/ppermute | solution.py:188
  15.5 2.2 %copy-start = (f32[2,8]{1,0:T(2,128)S(1)}, f32[2,8]{1,0:T(2,128)}, u32[]{:S(2)}) copy-start(f32[2,8]{1,0:T(2,128)} %basis_ref.9) | copy-start | bytes 196
  19.9 9.2 %collective-permute-start.5 = (bf16[256,1024]{1,0:T(8,128)(2,1)S(1)}, bf16[256,1024]{1,0:T(8,128)(2,1)S(1)}, u32[]{:S(2)}, u32[]{:S(2)}) collective-permute-start(bf16[256,1024]{1,0:T(8,128)(2,1)S(1)} %shard_map.60), channel_id=1, source_target_pairs={{0,2},{1,5},{2,0},{3,7},{4,6},{5,1},{6,4},{7,3},{8,10},{9,13},{10,... | collective-permute-start | bytes 1572872 | tf_op jit(solution)/shard_map/ppermute | solution.py:185
  23.9 7.6 %copy-start.1 = (f32[2,1024]{1,0:T(2,128)S(1)}, f32[2,1024]{1,0:T(2,128)}, u32[]{:S(2)}) copy-start(f32[2,1024]{1,0:T(2,128)} %amp_ref.1) | copy-start | bytes 24580
  23.9 7.6 %copy-start.2 = (s32[16,16]{1,0:T(8,128)S(1)}, s32[16,16]{1,0:T(8,128)}, u32[]{:S(2)}) copy-start(s32[16,16]{1,0:T(8,128)} %mask_ref.1) | copy-start | bytes 3076
  23.9 16.4 %collective-permute-start.4 = (bf16[256,1024]{1,0:T(8,128)(2,1)S(1)}, bf16[256,1024]{1,0:T(8,128)(2,1)S(1)}, u32[]{:S(2)}, u32[]{:S(2)}) collective-permute-start(bf16[256,1024]{1,0:T(8,128)(2,1)S(1)} %shard_map.58), channel_id=1, source_target_pairs={{0,2},{1,5},{2,0},{3,7},{4,6},{5,1},{6,4},{7,3},{8,10},{9,13},{10,... | collective-permute-start | bytes 1572872 | tf_op jit(solution)/shard_map/ppermute | solution.py:185
  29.3 11.0 %collective-permute-start.6 = (bf16[256,1024]{1,0:T(8,128)(2,1)S(1)}, bf16[256,1024]{1,0:T(8,128)(2,1)S(1)}, u32[]{:S(2)}, u32[]{:S(2)}) collective-permute-start(bf16[256,1024]{1,0:T(8,128)(2,1)S(1)} %add_convert_fusion), channel_id=1, source_target_pairs={{0,4},{1,3},{2,6},{3,1},{4,0},{5,7},{6,2},{7,5},{8,12},{9,11},{10,... | collective-permute-start | bytes 1572872 | tf_op jit(solution)/shard_map/ppermute | solution.py:185
  40.6 12.3 %collective-permute-start.8 = (bf16[256,1024]{1,0:T(8,128)(2,1)S(1)}, bf16[256,1024]{1,0:T(8,128)(2,1)S(1)}, u32[]{:S(2)}, u32[]{:S(2)}) collective-permute-start(bf16[256,1024]{1,0:T(8,128)(2,1)S(1)} %multiply_convert_fusion.resid_ref), channel_id=1, source_target_pairs={{0,4},{1,3},{2,6},{3,1},{4,0},{5,7},{6,2},{7,5},{8,12},{9,11},{10,... | collective-permute-start | bytes 1572872 | tf_op jit(solution)/shard_map/ppermute | solution.py:185
  44.5 13.7 %collective-permute-start.7 = (bf16[256,1024]{1,0:T(8,128)(2,1)S(1)}, bf16[256,1024]{1,0:T(8,128)(2,1)S(1)}, u32[]{:S(2)}, u32[]{:S(2)}) collective-permute-start(bf16[256,1024]{1,0:T(8,128)(2,1)S(1)} %multiply_convert_fusion.resid_ref), channel_id=1, source_target_pairs={{0,2},{1,5},{2,0},{3,7},{4,6},{5,1},{6,4},{7,3},{8,10},{9,13},{10,... | collective-permute-start | bytes 1572872 | tf_op jit(solution)/shard_map/ppermute | solution.py:185
  52.9 10.6 %collective-permute-start.9 = (bf16[256,1024]{1,0:T(8,128)(2,1)S(1)}, bf16[256,1024]{1,0:T(8,128)(2,1)S(1)}, u32[]{:S(2)}, u32[]{:S(2)}) collective-permute-start(bf16[256,1024]{1,0:T(8,128)(2,1)S(1)} %collective-permute-done.8.resid_ref), channel_id=1, source_target_pairs={{0,2},{1,5},{2,0},{3,7},{4,6},{5,1},{6,4},{7,3},{8,10},{9,13},{10,... | collective-permute-start | bytes 1572872 | tf_op jit(solution)/shard_map/ppermute | solution.py:185
  65.5 1.2 %collective-permute-start.10 = (f32[1,512]{1,0:T(1,128)S(1)}, f32[1,512]{1,0:T(1,128)S(1)}, u32[]{:S(2)}, u32[]{:S(2)}) collective-permute-start(f32[1,512]{1,0:T(1,128)S(1)} %slice.20), channel_id=1, source_target_pairs={{0,1},{1,0},{2,3},{3,2},{4,5},{5,4},{6,7},{7,6},{8,9},{9,8},{10,11... | collective-permute-start | bytes 6152 | tf_op jit(solution)/shard_map/ppermute | solution.py:254
  67.3 4.6 %collective-permute-start.11 = (f32[4,512]{1,0:T(4,128)S(1)}, f32[4,512]{1,0:T(4,128)S(1)}, u32[]{:S(2)}, u32[]{:S(2)}) collective-permute-start(f32[4,512]{1,0:T(4,128)S(1)} %slice.22), channel_id=1, source_target_pairs={{0,16},{8,24},{16,0},{24,8},{1,17},{9,25},{17,1},{25,9},{2,18},{10... | collective-permute-start | bytes 24584 | tf_op jit(solution)/shard_map/ppermute | solution.py:188
  71.9 3.7 %collective-permute-start.12 = (f32[2,512]{1,0:T(2,128)S(1)}, f32[2,512]{1,0:T(2,128)S(1)}, u32[]{:S(2)}, u32[]{:S(2)}) collective-permute-start(f32[2,512]{1,0:T(2,128)S(1)} %slice.24), channel_id=1, source_target_pairs={{0,8},{8,0},{16,24},{24,16},{1,9},{9,1},{17,25},{25,17},{2,10},{10... | collective-permute-start | bytes 12296 | tf_op jit(solution)/shard_map/ppermute | solution.py:188

commit v4 on v3

v4 whole, which is shorter than its diff:
```python
import functools

import jax
import jax.numpy as jnp
from jax import lax
from jax.experimental import pallas as pl
from jax.experimental.pallas import tpu as pltpu
from jax.sharding import PartitionSpec as P


F32 = jnp.float32
BF16 = jnp.bfloat16
MIB = 1 << 20


def across(left, right):
    return lax.dot_general(left, right, (((1,), (1,)), ((), ())), preferred_element_type=F32)


def along(left, right):
    return jnp.dot(left, right, preferred_element_type=F32)


def copy_all(sems, pairs):
    copies = [pltpu.make_async_copy(src, dst, sems.at[i]) for i, (src, dst) in enumerate(pairs)]
    for copy in copies:
        copy.start()
    for copy in copies:
        copy.wait()


def take_kernel(core_ref, green_ref, out_ref, sems):
    other = 1 - core_ref[0]
    copy_all(sems, [(green_ref.at[p, other], out_ref.at[p]) for p in (0, 1)])


def mine_kernel(core_ref, green_ref, out_ref, sems):
    core, cells = core_ref[0], green_ref.shape[3]
    spots = [out_ref.at[:, pl.ds(2 * p * cells, cells)] for p in (0, 1)]
    copy_all(sems, [(green_ref.at[p, core], spots[p]) for p in (0, 1)])


def theirs_kernel(theirs_ref, field_ref, out_ref, sems):
    del field_ref
    cells = theirs_ref.shape[2]
    spots = [out_ref.at[:, pl.ds((2 * p + 1) * cells, cells)] for p in (0, 1)]
    copy_all(sems, [(theirs_ref.at[p], spots[p]) for p in (0, 1)])


def weight_kernel(n, place_ref, amp_ref, mask_ref, *out_refs):
    core, piece = place_ref[0], place_ref[1]
    tile = out_refs[0].shape[0]
    blocks = mask_ref.shape[0]
    size = n * tile // blocks

    def amp(start):
        both = amp_ref[:, pl.ds(pl.multiple_of(start, tile), tile)]
        return jnp.where(core == 0, both[0:1], both[1:2])

    here = piece * tile
    row = lax.broadcasted_iota(jnp.int32, (tile, tile), 0)
    col = lax.broadcasted_iota(jnp.int32, (tile, tile), 1)
    down = jnp.sum(jnp.where(row == col, amp(here), 0.0), axis=1, keepdims=True)
    mask = mask_ref[...].astype(BF16)
    low = lax.broadcasted_iota(jnp.int32, (tile, blocks), 1) * size
    at = here + lax.broadcasted_iota(jnp.int32, (tile, blocks), 0)
    pick = ((at >= low) & (at < low + size)).astype(BF16)
    rows = (0.5 * (along(pick, mask) + across(pick, mask))).astype(BF16)
    low = lax.broadcasted_iota(jnp.int32, (blocks, tile), 0) * size
    for d in range(n // 2 + 1):
        start = lax.rem(piece + d, n) * tile
        at = start + lax.broadcasted_iota(jnp.int32, (blocks, tile), 1)
        pick = ((at >= low) & (at < low + size)).astype(BF16)
        weight = down * amp(start) * along(rows, pick)
        for i in [0] if d == 0 else [n - 1] if d == n // 2 else [2 * d - 1, 2 * d]:
            u, at_block = divmod(i, n // 2)
            out_refs[u][:, at_block * tile : (at_block + 1) * tile] = weight


def corr_kernel(n, halves, place_ref, basis_ref, known_ref, green_ref, *out_refs):
    stations, width = green_ref.shape
    tile, half = stations // n, width // 2
    core, plane, piece = place_ref[0], place_ref[1], place_ref[2]

    def block(d):
        start = lax.rem(piece + d, n) * tile
        return green_ref[pl.ds(pl.multiple_of(start, tile), tile), :]

    def put(i, value):
        u, at = divmod(i, n // 2)
        out_ref = out_refs[halves.index(u)]
        out_ref[:, at * tile : (at + 1) * tile] = value.astype(out_ref.dtype)

    source = jnp.sum(basis_column(core, plane, basis_ref, known_ref.shape[0]) * known_ref[...], 0, keepdims=True)
    source = jnp.concatenate((source, source), axis=1)
    scaled = (block(0).astype(F32) * source).astype(BF16)
    turned = jnp.concatenate((scaled[:, half:], -scaled[:, :half]), axis=1)
    both = jnp.concatenate((scaled, turned), axis=0)
    wanted = [i for u in halves for i in range(u * (n // 2), (u + 1) * (n // 2))]
    if 0 in wanted:
        pair = across(both, block(0))
        row = lax.broadcasted_iota(jnp.int32, (tile, tile), 0)
        col = lax.broadcasted_iota(jnp.int32, (tile, tile), 1)
        put(0, jnp.where(row >= col, pair[:tile], pair[tile:]))
    for d in range(1, n // 2):
        if 2 * d - 1 in wanted and 2 * d in wanted:
            pair = across(both, block(d))
            put(2 * d - 1, pair[:tile])
            put(2 * d, pair[tile:])
        elif 2 * d - 1 in wanted:
            put(2 * d - 1, across(scaled, block(d)))
        elif 2 * d in wanted:
            put(2 * d, across(turned, block(d)))
    if n - 1 in wanted:
        put(n - 1, across(jnp.where(piece < n // 2, scaled, turned), block(n // 2)))


def basis_column(core, plane, basis_ref, count):
    each = count // PLANES[0]
    at = lax.broadcasted_iota(jnp.int32, (count, 1), 0)
    column = jnp.zeros((count, 1), F32)
    for i in range(count):
        column = jnp.where(at == i, basis_ref[core, (plane ^ (i // each)) * each + i % each], column)
    return column


PLANES = [0]


def sens_sum(n, u, step, piece, resid_ref, green_ref, emit):
    stations, width = green_ref.shape
    tile, half = stations // n, width // 2
    starts = [pl.multiple_of(lax.rem(piece + d, n) * tile, tile) for d in range(n // 2 + 1)]
    real = piece < n // 2
    terms = []
    for i in range(u * (n // 2), (u + 1) * (n // 2)):
        at = (i - u * (n // 2)) * tile
        value = resid_ref[:, at : at + tile]
        if i == 0:
            row = lax.broadcasted_iota(jnp.int32, (tile, tile), 0)
            col = lax.broadcasted_iota(jnp.int32, (tile, tile), 1)
            diag = value.astype(F32)
            low = jnp.where(row > col, diag, jnp.where(row == col, 0.5 * diag, 0.0))
            terms.append(("re", 0, low.astype(BF16)))
            terms.append(("im", 0, jnp.where(row < col, diag, 0.0).astype(BF16)))
        elif i == n - 1:
            terms.append(("either", n // 2, value))
        else:
            terms.append(("re" if i % 2 else "im", (i + 1) // 2, value))
    for at in range(0, half, step):

        def fields(d):
            rows = pl.ds(starts[d], tile)
            return green_ref[rows, at : at + step], green_ref[rows, half + at : half + at + step]

        yre, yim = jnp.zeros((tile, step), F32), jnp.zeros((tile, step), F32)
        for kind, d, value in terms:
            re, im = fields(d)
            tu, tv = along(value, re), along(value, im)
            if kind == "re":
                yre, yim = yre + tu, yim + tv
            elif kind == "im":
                yre, yim = yre - tv, yim + tu
            else:
                yre, yim = yre + jnp.where(real, tu, -tv), yim + jnp.where(real, tv, tu)
        re, im = fields(0)
        share = re.astype(F32) * yre + im.astype(F32) * yim
        emit(at, 2.0 * jnp.sum(share, axis=0, keepdims=True))


def sens_kernel(n, u, step, piece_ref, resid_ref, green_ref, out_ref):
    def emit(at, value):
        out_ref[:, at : at + step] = value

    sens_sum(n, u, step, piece_ref[0], resid_ref, green_ref, emit)


def last_kernel(n, u, step, place_ref, basis_ref, before_ref, resid_ref, green_ref, *out_refs):
    core, plane = place_ref[0], place_ref[1]
    rows = out_refs[0].shape[0]
    column = basis_column(core, plane, basis_ref, rows * len(out_refs))

    def emit(at, value):
        product = column * (before_ref[:, at : at + step] + value)
        for k, out_ref in enumerate(out_refs):
            out_ref[:, at : at + step] = product[k * rows : (k + 1) * rows]

    sens_sum(n, u, step, place_ref[2], resid_ref, green_ref, emit)


SMEM = pl.BlockSpec(memory_space=pltpu.SMEM)
VMEM = pl.BlockSpec(memory_space=pltpu.VMEM)
HBM = pl.BlockSpec(memory_space=pltpu.HBM)


def call(kernel, shapes, dtype, specs, flops, moved, grant, *args, scratch=(), alias={}):
    out_shape = [jax.ShapeDtypeStruct(shape, dtype) for shape in shapes]
    out = pl.pallas_call(
        kernel,
        out_shape=out_shape,
        in_specs=specs,
        out_specs=[VMEM] * len(shapes),
        scratch_shapes=scratch,
        input_output_aliases=alias,
        compiler_params=pltpu.CompilerParams(vmem_limit_bytes=grant * MIB),
        cost_estimate=pl.CostEstimate(flops=flops, bytes_accessed=moved, transcendentals=0),
    )(*args)
    return out if len(out) > 1 else out[0]


def on_device(n_freq, n_cell, green, coeffs, basis, amplitude, block_mask):
    n = n_cell // 2
    bits, z_bits = n.bit_length() - 1, n_freq.bit_length() - 1
    stations, cells = green.shape[2], green.shape[3]
    tile, width, each = stations // n, 4 * cells, coeffs.shape[0]
    PLANES[0] = n_freq
    here = lax.axis_index("cell").astype(jnp.int32)
    plane = lax.axis_index("freq").astype(jnp.int32)
    core, chip = here % 2, here // 2
    flops = tile * stations * width * 5 // 4
    moved = 2 * stations * width + 2 * tile * stations

    def dims(which):
        return [(which + j) % bits for j in range(bits)]

    swap_core = [(i, i ^ 1) for i in range(n_cell)]

    def swap_chip(value, j):
        pairs = [(i, i ^ (2 << dims(i % 2)[j])) for i in range(n_cell)]
        return lax.ppermute(value, "cell", pairs)

    def swap_plane(value, j):
        return lax.ppermute(value, "freq", [(i, i ^ (1 << j)) for i in range(n_freq)])

    def piece_of(q):
        flips = [sum(((q >> j) & 1) << dims(which)[j] for j in range(bits)) for which in (0, 1)]
        return chip ^ jnp.where(core == 0, flips[0], flips[1])

    beside = lax.ppermute(coeffs, "cell", swap_core)
    core_only = core.reshape(1)
    placed_green = pltpu.with_memory_space_constraint(green, pltpu.HBM)
    two = [pltpu.SemaphoreType.DMA((2,))]
    theirs = call(
        take_kernel, [(2, stations, cells)], BF16, [SMEM, HBM], 0,
        8 * stations * cells, 16, core_only, placed_green, scratch=two,
    )
    theirs = lax.ppermute(theirs, "cell", swap_core)
    theirs = pltpu.with_memory_space_constraint(theirs, pltpu.HBM)
    known = jnp.concatenate((coeffs, beside), axis=1)
    for j in range(z_bits):
        near = swap_plane(known, j)
        known = jnp.concatenate((known, near), axis=0)

    field = call(
        mine_kernel, [(stations, width)], BF16, [SMEM, HBM], 0,
        2 * stations * width, 16, core_only, placed_green, scratch=two,
    )
    field = call(
        theirs_kernel, [(stations, width)], BF16, [HBM, VMEM], 0,
        2 * stations * width, 45, theirs, field, scratch=two, alias={1: 0},
    )

    def corr_piece(q, halves, dtype):
        out = call(
            functools.partial(corr_kernel, n, halves), [(tile, stations // 2)] * len(halves), dtype,
            [SMEM, SMEM, VMEM, VMEM], flops * len(halves), moved, 24,
            jnp.stack((core, plane, piece_of(q))), basis, known, field,
        )
        return out if len(halves) > 1 else [out]

    held = {}
    for q in sorted(range(n), key=lambda q: (q % 2 == 0, -q)):
        if q % 2:
            for u in (0, 1):
                held[q, u] = corr_piece(q, (u,), BF16)[0]
        else:
            held[q, 0], held[q, 1] = corr_piece(q, (0, 1), F32)
    weight = call(
        functools.partial(weight_kernel, n), [(tile, stations // 2)] * 2, F32, [SMEM, VMEM, VMEM],
        0, 4 * tile * stations, 8, jnp.stack((core, piece_of(0))), amplitude, block_mask,
    )
    for j in range(bits):
        for q in sorted((q for q in range(n) if q % (1 << j) == 0 and (q >> j) & 1), reverse=True):
            for u in (0, 1):
                got = swap_chip(held[q, u].astype(BF16), j)
                held[q ^ (1 << j), u] = held[q ^ (1 << j), u] + got.astype(F32)
    resid = {(0, u): (held[0, u] * weight[u]).astype(BF16) for u in (0, 1)}

    order = [0]
    for j in reversed(range(bits)):
        for q in list(order):
            order.append(q | (1 << j))
            for u in (0, 1):
                resid[order[-1], u] = swap_chip(resid[q, u], j)
    step = min(512, width // 2)
    sens = 0.0
    for q in order:
        for u in (0, 1):
            if (q, u) == (order[-1], 1):
                continue
            sens = sens + call(
                functools.partial(sens_kernel, n, u, step), [(1, width // 2)], F32,
                [SMEM, VMEM, VMEM], flops, moved, 24, piece_of(q).reshape(1), resid[q, u], field,
            )
    rows = n_freq * each // 2
    low, high = call(
        functools.partial(last_kernel, n, 1, step), [(rows, width // 2)] * 2, F32,
        [SMEM, SMEM, VMEM, VMEM, VMEM], flops, moved, 24,
        jnp.stack((core, plane, piece_of(order[-1]))), basis, sens, resid[order[-1], 1], field,
    )

    for j in reversed(range(z_bits)):
        kept = low + swap_plane(high, j)
        low, high = kept[: kept.shape[0] // 2], kept[kept.shape[0] // 2 :]
    return kept[:, :cells] + lax.ppermute(kept[:, cells:], "cell", swap_core)


def solution(mesh):
    placed = (
        P(None, "freq", None, "cell"),
        P("freq", "cell"),
        P("freq", None),
        P("freq", None),
        P(),
    )
    n_freq, n_cell = mesh.shape["freq"], mesh.shape["cell"]

    def body(*args):
        return on_device(n_freq, n_cell, *args)

    return jax.shard_map(
        body, mesh=mesh, in_specs=placed, out_specs=P("freq", "cell"), check_vma=False
    )
```

time: 76.3 us -> 71.1 us (0.932)
  waiting for transfers between devices: 31 us -> 19.9 us
  Pallas kernels: 21.6 us -> 25 us
  starting transfers between devices: 22 us -> 24.3 us
    ppermute x6 -> x12, waiting for transfers between devices: 18.6 us -> 9.02 us  [swap_chip(): return lax.ppermute(value, 'cell', pairs)]
    pallas_call x12 -> x18, Pallas kernels: 21.6 us -> 25 us  [call(): pl.pallas_call(kernel, out_shape=out_shape, in_specs=specs, out_specs=[VM...]
    ppermute x6 -> x12, starting transfers between devices: 11.2 us -> 13.6 us  [swap_chip(): return lax.ppermute(value, 'cell', pairs)]
    ppermute x4, waiting for transfers between devices: 7.53 us -> 6.02 us  [swap_plane(): return lax.ppermute(value, 'freq', [(i, i ^ 1 << j) for i in range(n_freq)])]
  transfers between devices with their start and end apart: 13 -> 19, of which waited for: 10 -> 8; matrix products, arithmetic and copies ran while one was open for 1% -> 1% of each run, Pallas kernels for 17% -> 25%
where the time goes in v4:
time: 71.1 us; the launch traced here: 70.9 us
  Pallas kernels  25 us (35%)
  starting transfers between devices  24.3 us (34%)
  waiting for transfers between devices  19.9 us (28%)
  other arithmetic  1.32 us (2%)
    pallas_call x18, Pallas kernels, call(): pl.pallas_call(kernel, out_shape=out_shape, in_specs=specs, out_specs=[VM...  25 us
    ppermute x12, starting transfers between devices, swap_chip(): return lax.ppermute(value, 'cell', pairs)  13.6 us
    ppermute x4, starting transfers between devices, swap_plane(): return lax.ppermute(value, 'freq', [(i, i ^ 1 << j) for i in range(n_freq)])  9.99 us
    ppermute x12, waiting for transfers between devices, swap_chip(): return lax.ppermute(value, 'cell', pairs)  9.02 us
    ppermute x4, waiting for transfers between devices, swap_plane(): return lax.ppermute(value, 'freq', [(i, i ^ 1 << j) for i in range(n_freq)])  6.02 us
    ppermute x1, waiting for transfers between devices, on_device(): beside = lax.ppermute(coeffs, 'cell', swap_core)  3.75 us
  transfers between devices with their start and end apart: 19, of which 8 were waited for; matrix products, arithmetic and copies ran while one was open for 1% of the time, Pallas kernels for 25%

profile of v4, /device:TPU:0, one launch (start us, length us, event | category | flops | bytes accessed | tf_op | source)
XLA Modules:
  0.0 70.9 jit_solution(17970995275333952483)
XLA Ops:
  0.0 1.6 %shard_map.55 = bf16[2,1024,512]{2,1,0:T(8,128)(2,1)S(1)} custom-call(s32[1]{0:T(128)} %bitcast.core_ref, bf16[2,2,1024,512]{3,2,1,0:T(8,128)(2,1)} %green_ref.3), custom_call_target="tpu_custom_call" | custom-call | bytes 4194304 | tf_op jit(solution)/shard_map/pallas_call | solution.py:198
  1.6 0.6 collective-permute-start.3
  2.1 0.1 collective-permute-start
  2.3 3.8 %collective-permute-done = f32[2,512]{1,0:T(2,128)S(1)} collective-permute-done((f32[2,512]{1,0:T(2,128)S(1)}, f32[2,512]{1,0:T(2,128)S(1)}, u32[]{:S(2)}, u32[]{:S(2)}) %collective-permute-start) | collective-permute-done | bytes 4128 | tf_op jit(solution)/shard_map/ppermute | solution.py:239
  6.1 2.9 %collective-permute-start.1 = (f32[2,1024]{1,0:T(2,128)S(1)}, f32[2,1024]{1,0:T(2,128)S(1)}, u32[]{:S(2)}, u32[]{:S(2)}) collective-permute-start(f32[2,1024]{1,0:T(2,128)S(1)} %constant_dynamic-update-slice_fusion), channel_id=1, source_target_pairs={{0,8},{8,0},{16,24},{24,16},{1,9},{9,1},{17,25},{25,17},{2,10},{10... | collective-permute-start | bytes 24584 | tf_op jit(solution)/shard_map/ppermute | solution.py:233
  9.0 0.1 pad_add_fusion.2
  9.1 1.6 %collective-permute-done.1 = f32[2,1024]{1,0:T(2,128)S(1)} collective-permute-done((f32[2,1024]{1,0:T(2,128)S(1)}, f32[2,1024]{1,0:T(2,128)S(1)}, u32[]{:S(2)}, u32[]{:S(2)}) %collective-permute-start.1) | collective-permute-done | bytes 8224 | tf_op jit(solution)/shard_map/ppermute | solution.py:233
  10.6 3.1 %collective-permute-start.2 = (f32[4,1024]{1,0:T(4,128)S(1)}, f32[4,1024]{1,0:T(4,128)S(1)}, u32[]{:S(2)}, u32[]{:S(2)}) collective-permute-start(f32[4,1024]{1,0:T(4,128)S(1)} %pad_maximum_fusion.1), channel_id=1, source_target_pairs={{0,16},{8,24},{16,0},{24,8},{1,17},{9,25},{17,1},{25,9},{2,18},{10... | collective-permute-start | bytes 49160 | tf_op jit(solution)/shard_map/ppermute | solution.py:233
  13.8 1.6 %shard_map.56.field_ref = bf16[1024,2048]{1,0:T(8,128)(2,1)S(1)} custom-call(s32[1]{0:T(128)} %bitcast.core_ref, bf16[2,2,1024,512]{3,2,1,0:T(8,128)(2,1)} %green_ref.3), custom_call_target="tpu_custom_call" | custom-call | bytes 4194304 | tf_op jit(solution)/shard_map/pallas_call | solution.py:198
  15.4 1.0 %shard_map.62 = (f32[256,512]{1,0:T(8,128)S(1)}, f32[256,512]{1,0:T(8,128)S(1)}) custom-call(s32[2]{0:T(128)S(1)} %pad_add_fusion.5.place_ref, f32[2,1024]{1,0:T(2,128)S(1)} %copy-done.1, s32[16,16]{1,0:T(8,128)S(1)} %copy-done.2), custom_call_target="tpu_custom_call" | custom-call | bytes 1048576 | tf_op jit(solution)/shard_map/pallas_call | solution.py:198
  16.5 1.6 %shard_map.57.green_ref = bf16[1024,2048]{1,0:T(8,128)(2,1)S(1)} custom-call(bf16[2,1024,512]{2,1,0:T(8,128)(2,1)} %collective-permute-done.3.theirs_ref, bf16[1024,2048]{1,0:T(8,128)(2,1)S(1)} %shard_map.56.field_ref), custom_call_target="tpu_custom_call", output_to_operand_aliasing={{}: (1, {})} | custom-call | bytes 4194304 | tf_op jit(solution)/shard_map/pallas_call | solution.py:198
  18.0 1.3 %shard_map.65 = bf16[256,512]{1,0:T(8,128)(2,1)S(1)} custom-call(s32[3]{0:T(128)S(1)} %get-tuple-element.25.place_ref, f32[2,8]{1,0:T(2,128)S(1)} %copy-done, f32[8,1024]{1,0:T(8,128)S(1)} %pad_maximum_fusion.known_ref, bf16[1024,2048]{1,0:T(8,128)(2,1)S(1)} %shard_map.57.green_ref), custom_call_target="tpu_custom_call" | custom-call | flops 671088640 | bytes 4718592 | tf_op jit(solution)/shard_map/pallas_call | solution.py:198
  19.4 1.6 %shard_map.61 = bf16[256,512]{1,0:T(8,128)(2,1)S(1)} custom-call(s32[3]{0:T(128)S(1)} %get-tuple-element.25.place_ref, f32[2,8]{1,0:T(2,128)S(1)} %copy-done, f32[8,1024]{1,0:T(8,128)S(1)} %pad_maximum_fusion.known_ref, bf16[1024,2048]{1,0:T(8,128)(2,1)S(1)} %shard_map.57.green_ref), custom_call_target="tpu_custom_call" | custom-call | flops 671088640 | bytes 4718592 | tf_op jit(solution)/shard_map/pallas_call | solution.py:198
  20.9 1.6 %collective-permute-start.8 = (bf16[256,512]{1,0:T(8,128)(2,1)S(1)}, bf16[256,512]{1,0:T(8,128)(2,1)S(1)}, u32[]{:S(2)}, u32[]{:S(2)}) collective-permute-start(bf16[256,512]{1,0:T(8,128)(2,1)S(1)} %shard_map.65), channel_id=1, source_target_pairs={{0,2},{1,5},{2,0},{3,7},{4,6},{5,1},{6,4},{7,3},{8,10},{9,13},{10,... | collective-permute-start | bytes 786440 | tf_op jit(solution)/shard_map/ppermute | solution.py:230
  22.5 0.5 collective-permute-start.5
  23.0 1.6 %shard_map.59 = bf16[256,512]{1,0:T(8,128)(2,1)S(1)} custom-call(s32[3]{0:T(128)S(1)} %get-tuple-element.21.place_ref, f32[2,8]{1,0:T(2,128)S(1)} %copy-done, f32[8,1024]{1,0:T(8,128)S(1)} %pad_maximum_fusion.known_ref, bf16[1024,2048]{1,0:T(8,128)(2,1)S(1)} %shard_map.57.green_ref), custom_call_target="tpu_custom_call" | custom-call | flops 671088640 | bytes 4718592 | tf_op jit(solution)/shard_map/pallas_call | solution.py:198
  24.6 1.6 %collective-permute-start.4 = (bf16[256,512]{1,0:T(8,128)(2,1)S(1)}, bf16[256,512]{1,0:T(8,128)(2,1)S(1)}, u32[]{:S(2)}, u32[]{:S(2)}) collective-permute-start(bf16[256,512]{1,0:T(8,128)(2,1)S(1)} %shard_map.59), channel_id=1, source_target_pairs={{0,2},{1,5},{2,0},{3,7},{4,6},{5,1},{6,4},{7,3},{8,10},{9,13},{10,... | collective-permute-start | bytes 786440 | tf_op jit(solution)/shard_map/ppermute | solution.py:230
  26.2 2.1 %shard_map.60 = (f32[256,512]{1,0:T(8,128)S(1)}, f32[256,512]{1,0:T(8,128)S(1)}) custom-call(s32[3]{0:T(128)S(1)} %get-tuple-element.24.place_ref, f32[2,8]{1,0:T(2,128)S(1)} %copy-done, f32[8,1024]{1,0:T(8,128)S(1)} %pad_maximum_fusion.known_ref, bf16[1024,2048]{1,0:T(8,128)(2,1)S(1)} %shard_map.57.green_ref), custom_call_target="tpu_custom_call" | custom-call | flops 1342177280 | bytes 4718592 | tf_op jit(solution)/shard_map/pallas_call | solution.py:198
  28.3 2.1 %shard_map.58 = (f32[256,512]{1,0:T(8,128)S(1)}, f32[256,512]{1,0:T(8,128)S(1)}) custom-call(s32[3]{0:T(128)S(1)} %get-tuple-element.23.place_ref, f32[2,8]{1,0:T(2,128)S(1)} %copy-done, f32[8,1024]{1,0:T(8,128)S(1)} %pad_maximum_fusion.known_ref, bf16[1024,2048]{1,0:T(8,128)(2,1)S(1)} %shard_map.57.green_ref), custom_call_target="tpu_custom_call" | custom-call | flops 1342177280 | bytes 4718592 | tf_op jit(solution)/shard_map/pallas_call | solution.py:198
  30.5 1.6 %collective-permute-start.6 = (bf16[256,512]{1,0:T(8,128)(2,1)S(1)}, bf16[256,512]{1,0:T(8,128)(2,1)S(1)}, u32[]{:S(2)}, u32[]{:S(2)}) collective-permute-start(bf16[256,512]{1,0:T(8,128)(2,1)S(1)} %add_convert_fusion.1), channel_id=1, source_target_pairs={{0,4},{1,3},{2,6},{3,1},{4,0},{5,7},{6,2},{7,5},{8,12},{9,11},{10,... | collective-permute-start | bytes 786440 | tf_op jit(solution)/shard_map/ppermute | solution.py:230
  32.1 1.3 %shard_map.64 = bf16[256,512]{1,0:T(8,128)(2,1)S(1)} custom-call(s32[3]{0:T(128)S(1)} %get-tuple-element.21.place_ref, f32[2,8]{1,0:T(2,128)S(1)} %copy-done, f32[8,1024]{1,0:T(8,128)S(1)} %pad_maximum_fusion.known_ref, bf16[1024,2048]{1,0:T(8,128)(2,1)S(1)} %shard_map.57.green_ref), custom_call_target="tpu_custom_call" | custom-call | flops 671088640 | bytes 4718592 | tf_op jit(solution)/shard_map/pallas_call | solution.py:198
  33.4 1.3 %collective-permute-start.7 = (bf16[256,512]{1,0:T(8,128)(2,1)S(1)}, bf16[256,512]{1,0:T(8,128)(2,1)S(1)}, u32[]{:S(2)}, u32[]{:S(2)}) collective-permute-start(bf16[256,512]{1,0:T(8,128)(2,1)S(1)} %shard_map.64), channel_id=1, source_target_pairs={{0,2},{1,5},{2,0},{3,7},{4,6},{5,1},{6,4},{7,3},{8,10},{9,13},{10,... | collective-permute-start | bytes 786440 | tf_op jit(solution)/shard_map/ppermute | solution.py:230
  34.8 0.6 collective-permute-start.9
  35.4 3.9 %collective-permute-done.6 = bf16[256,512]{1,0:T(8,128)(2,1)S(1)} collective-permute-done((bf16[256,512]{1,0:T(8,128)(2,1)S(1)}, bf16[256,512]{1,0:T(8,128)(2,1)S(1)}, u32[]{:S(2)}, u32[]{:S(2)}) %collective-permute-start.6) | collective-permute-done | bytes 262176 | tf_op jit(solution)/shard_map/ppermute | solution.py:230
  39.3 0.2 multiply_convert_fusion.1.resid_ref
  39.4 1.3 %collective-permute-start.10 = (bf16[256,512]{1,0:T(8,128)(2,1)S(1)}, bf16[256,512]{1,0:T(8,128)(2,1)S(1)}, u32[]{:S(2)}, u32[]{:S(2)}) collective-permute-start(bf16[256,512]{1,0:T(8,128)(2,1)S(1)} %multiply_convert_fusion.1.resid_ref), channel_id=1, source_target_pairs={{0,4},{1,3},{2,6},{3,1},{4,0},{5,7},{6,2},{7,5},{8,12},{9,11},{10,... | collective-permute-start | bytes 786440 | tf_op jit(solution)/shard_map/ppermute | solution.py:230
  40.7 1.9 %collective-permute-done.7 = bf16[256,512]{1,0:T(8,128)(2,1)S(1)} collective-permute-done((bf16[256,512]{1,0:T(8,128)(2,1)S(1)}, bf16[256,512]{1,0:T(8,128)(2,1)S(1)}, u32[]{:S(2)}, u32[]{:S(2)}) %collective-permute-start.7) | collective-permute-done | bytes 262176 | tf_op jit(solution)/shard_map/ppermute | solution.py:230
  42.7 0.2 multiply_convert_fusion.resid_ref
  42.8 0.7 %collective-permute-start.11 = (bf16[256,512]{1,0:T(8,128)(2,1)S(1)}, bf16[256,512]{1,0:T(8,128)(2,1)S(1)}, u32[]{:S(2)}, u32[]{:S(2)}) collective-permute-start(bf16[256,512]{1,0:T(8,128)(2,1)S(1)} %multiply_convert_fusion.resid_ref), channel_id=1, source_target_pairs={{0,4},{1,3},{2,6},{3,1},{4,0},{5,7},{6,2},{7,5},{8,12},{9,11},{10,... | collective-permute-start | bytes 786440 | tf_op jit(solution)/shard_map/ppermute | solution.py:230
  43.5 1.1 %collective-permute-start.12 = (bf16[256,512]{1,0:T(8,128)(2,1)S(1)}, bf16[256,512]{1,0:T(8,128)(2,1)S(1)}, u32[]{:S(2)}, u32[]{:S(2)}) collective-permute-start(bf16[256,512]{1,0:T(8,128)(2,1)S(1)} %multiply_convert_fusion.1.resid_ref), channel_id=1, source_target_pairs={{0,2},{1,5},{2,0},{3,7},{4,6},{5,1},{6,4},{7,3},{8,10},{9,13},{10,... | collective-permute-start | bytes 786440 | tf_op jit(solution)/shard_map/ppermute | solution.py:230
  44.6 0.9 %collective-permute-start.13 = (bf16[256,512]{1,0:T(8,128)(2,1)S(1)}, bf16[256,512]{1,0:T(8,128)(2,1)S(1)}, u32[]{:S(2)}, u32[]{:S(2)}) collective-permute-start(bf16[256,512]{1,0:T(8,128)(2,1)S(1)} %multiply_convert_fusion.resid_ref), channel_id=1, source_target_pairs={{0,2},{1,5},{2,0},{3,7},{4,6},{5,1},{6,4},{7,3},{8,10},{9,13},{10,... | collective-permute-start | bytes 786440 | tf_op jit(solution)/shard_map/ppermute | solution.py:230
  45.6 1.0 %shard_map.66 = f32[1,1024]{1,0:T(1,128)S(1)} custom-call(s32[1]{0:T(128)} %bitcast.3.piece_ref, bf16[256,512]{1,0:T(8,128)(2,1)S(1)} %multiply_convert_fusion.resid_ref, bf16[1024,2048]{1,0:T(8,128)(2,1)S(1)} %shard_map.57.green_ref), custom_call_target="tpu_custom_call" | custom-call | flops 671088640 | bytes 4718592 | tf_op jit(solution)/shard_map/pallas_call | solution.py:198
  46.6 1.2 %collective-permute-start.14 = (bf16[256,512]{1,0:T(8,128)(2,1)S(1)}, bf16[256,512]{1,0:T(8,128)(2,1)S(1)}, u32[]{:S(2)}, u32[]{:S(2)}) collective-permute-start(bf16[256,512]{1,0:T(8,128)(2,1)S(1)} %collective-permute-done.10.resid_ref), channel_id=1, source_target_pairs={{0,2},{1,5},{2,0},{3,7},{4,6},{5,1},{6,4},{7,3},{8,10},{9,13},{10,... | collective-permute-start | bytes 786440 | tf_op jit(solution)/shard_map/ppermute | solution.py:230
  47.7 1.1 %shard_map.63 = f32[1,1024]{1,0:T(1,128)S(1)} custom-call(s32[1]{0:T(128)} %bitcast.3.piece_ref, bf16[256,512]{1,0:T(8,128)(2,1)S(1)} %multiply_convert_fusion.1.resid_ref, bf16[1024,2048]{1,0:T(8,128)(2,1)S(1)} %shard_map.57.green_ref), custom_call_target="tpu_custom_call" | custom-call | flops 671088640 | bytes 4718592 | tf_op jit(solution)/shard_map/pallas_call | solution.py:198
  48.9 3.2 %collective-permute-done.11.resid_ref = bf16[256,512]{1,0:T(8,128)(2,1)S(1)} collective-permute-done((bf16[256,512]{1,0:T(8,128)(2,1)S(1)}, bf16[256,512]{1,0:T(8,128)(2,1)S(1)}, u32[]{:S(2)}, u32[]{:S(2)}) %collective-permute-start.11) | collective-permute-done | bytes 262176 | tf_op jit(solution)/shard_map/ppermute | solution.py:230
  52.1 1.2 %collective-permute-start.15 = (bf16[256,512]{1,0:T(8,128)(2,1)S(1)}, bf16[256,512]{1,0:T(8,128)(2,1)S(1)}, u32[]{:S(2)}, u32[]{:S(2)}) collective-permute-start(bf16[256,512]{1,0:T(8,128)(2,1)S(1)} %collective-permute-done.11.resid_ref), channel_id=1, source_target_pairs={{0,2},{1,5},{2,0},{3,7},{4,6},{5,1},{6,4},{7,3},{8,10},{9,13},{10,... | collective-permute-start | bytes 786440 | tf_op jit(solution)/shard_map/ppermute | solution.py:230
  53.3 1.1 %shard_map.67 = f32[1,1024]{1,0:T(1,128)S(1)} custom-call(s32[1]{0:T(128)} %bitcast.5.piece_ref, bf16[256,512]{1,0:T(8,128)(2,1)S(1)} %collective-permute-done.10.resid_ref, bf16[1024,2048]{1,0:T(8,128)(2,1)S(1)} %shard_map.57.green_ref), custom_call_target="tpu_custom_call" | custom-call | flops 671088640 | bytes 4718592 | tf_op jit(solution)/shard_map/pallas_call | solution.py:198
  54.5 1.0 %shard_map.68 = f32[1,1024]{1,0:T(1,128)S(1)} custom-call(s32[1]{0:T(128)} %bitcast.5.piece_ref, bf16[256,512]{1,0:T(8,128)(2,1)S(1)} %collective-permute-done.11.resid_ref, bf16[1024,2048]{1,0:T(8,128)(2,1)S(1)} %shard_map.57.green_ref), custom_call_target="tpu_custom_call" | custom-call | flops 671088640 | bytes 4718592 | tf_op jit(solution)/shard_map/pallas_call | solution.py:198
  55.5 1.3 %shard_map.69 = f32[1,1024]{1,0:T(1,128)S(1)} custom-call(s32[1]{0:T(128)} %bitcast.4.piece_ref, bf16[256,512]{1,0:T(8,128)(2,1)S(1)} %collective-permute-done.12.resid_ref, bf16[1024,2048]{1,0:T(8,128)(2,1)S(1)} %shard_map.57.green_ref), custom_call_target="tpu_custom_call" | custom-call | flops 671088640 | bytes 4718592 | tf_op jit(solution)/shard_map/pallas_call | solution.py:198
  56.8 1.0 %shard_map.70 = f32[1,1024]{1,0:T(1,128)S(1)} custom-call(s32[1]{0:T(128)} %bitcast.4.piece_ref, bf16[256,512]{1,0:T(8,128)(2,1)S(1)} %collective-permute-done.13.resid_ref, bf16[1024,2048]{1,0:T(8,128)(2,1)S(1)} %shard_map.57.green_ref), custom_call_target="tpu_custom_call" | custom-call | flops 671088640 | bytes 4718592 | tf_op jit(solution)/shard_map/pallas_call | solution.py:198
  57.8 1.1 %shard_map.71 = f32[1,1024]{1,0:T(1,128)S(1)} custom-call(s32[1]{0:T(128)} %bitcast.2.piece_ref, bf16[256,512]{1,0:T(8,128)(2,1)S(1)} %collective-permute-done.14.resid_ref, bf16[1024,2048]{1,0:T(8,128)(2,1)S(1)} %shard_map.57.green_ref), custom_call_target="tpu_custom_call" | custom-call | flops 671088640 | bytes 4718592 | tf_op jit(solution)/shard_map/pallas_call | solution.py:198
  59.0 1.6 %shard_map.72 = (f32[4,1024]{1,0:T(4,128)S(1)}, f32[4,1024]{1,0:T(4,128)S(1)}) custom-call(s32[3]{0:T(128)S(1)} %get-tuple-element.25.place_ref, f32[2,8]{1,0:T(2,128)S(1)} %copy-done, f32[1,1024]{1,0:T(1,128)S(1)} %add_add_fusion.before_ref, bf16[256,512]{1,0:T(8,128)(2,1)S(1)} %collective-permute-done.15.resid_ref, bf16[1024,2048]{1,0:T(8,128)(2,1)S(1)} %shard_map.57.green_ref), custom_call_target="tpu_custom_call" | custom-call | flops 671088640 | bytes 4718592 | tf_op jit(solution)/shard_map/pallas_call | solution.py:198
  60.6 2.3 %collective-permute-start.16 = (f32[4,1024]{1,0:T(4,128)S(1)}, f32[4,1024]{1,0:T(4,128)S(1)}, u32[]{:S(2)}, u32[]{:S(2)}) collective-permute-start(f32[4,1024]{1,0:T(4,128)S(1)} %get-tuple-element.20), channel_id=1, source_target_pairs={{0,16},{8,24},{16,0},{24,8},{1,17},{9,25},{17,1},{25,9},{2,18},{10... | collective-permute-start | bytes 49160 | tf_op jit(solution)/shard_map/ppermute | solution.py:233
  62.9 2.4 %collective-permute-done.16 = f32[4,1024]{1,0:T(4,128)S(1)} collective-permute-done((f32[4,1024]{1,0:T(4,128)S(1)}, f32[4,1024]{1,0:T(4,128)S(1)}, u32[]{:S(2)}, u32[]{:S(2)}) %collective-permute-start.16) | collective-permute-done | bytes 16416 | tf_op jit(solution)/shard_map/ppermute | solution.py:233
  65.3 1.6 %collective-permute-start.17 = (f32[2,1024]{1,0:T(2,128)S(1)}, f32[2,1024]{1,0:T(2,128)S(1)}, u32[]{:S(2)}, u32[]{:S(2)}) collective-permute-start(f32[2,1024]{1,0:T(2,128)S(1)} %slice.17), channel_id=1, source_target_pairs={{0,8},{8,0},{16,24},{24,16},{1,9},{9,1},{17,25},{25,17},{2,10},{10... | collective-permute-start | bytes 24584 | tf_op jit(solution)/shard_map/ppermute | solution.py:233
  67.0 2.1 %collective-permute-done.17 = f32[2,1024]{1,0:T(2,128)S(1)} collective-permute-done((f32[2,1024]{1,0:T(2,128)S(1)}, f32[2,1024]{1,0:T(2,128)S(1)}, u32[]{:S(2)}, u32[]{:S(2)}) %collective-permute-start.17) | collective-permute-done | bytes 8224 | tf_op jit(solution)/shard_map/ppermute | solution.py:233
  69.1 1.2 %collective-permute-done.18 = f32[2,512]{1,0:T(2,128)S(1)} collective-permute-done((f32[2,512]{1,0:T(2,128)S(1)}, f32[2,512]{1,0:T(2,128)S(1)}, u32[]{:S(2)}, u32[]{:S(2)}) %collective-permute-start.18) | collective-permute-done | bytes 4128 | tf_op jit(solution)/shard_map/ppermute | solution.py:315
  70.3 0.6 slice_add_fusion.1
  (33 shorter events, 0.5 us)
Async XLA Ops:
  0.0 2.1 %copy-start.3 = (f32[2,512]{1,0:T(2,128)S(1)}, f32[2,512]{1,0:T(2,128)}, u32[]{:S(2)}) copy-start(f32[2,512]{1,0:T(2,128)} %param.6) | copy-start | bytes 12292
  1.6 14.9 %collective-permute-start.3 = (bf16[2,1024,512]{2,1,0:T(8,128)(2,1)S(1)}, bf16[2,1024,512]{2,1,0:T(8,128)(2,1)}, u32[]{:S(2)}, u32[]{:S(2)}) collective-permute-start(bf16[2,1024,512]{2,1,0:T(8,128)(2,1)S(1)} %shard_map.55), channel_id=1, source_target_pairs={{0,1},{1,0},{2,3},{3,2},{4,5},{5,4},{6,7},{7,6},{8,9},{9,8},{10,11... | collective-permute-start | bytes 6291464 | tf_op jit(solution)/shard_map/ppermute | solution.py:247
  2.1 3.9 %collective-permute-start = (f32[2,512]{1,0:T(2,128)S(1)}, f32[2,512]{1,0:T(2,128)S(1)}, u32[]{:S(2)}, u32[]{:S(2)}) collective-permute-start(f32[2,512]{1,0:T(2,128)S(1)} %copy-done.3), channel_id=1, source_target_pairs={{0,1},{1,0},{2,3},{3,2},{4,5},{5,4},{6,7},{7,6},{8,9},{9,8},{10,11... | collective-permute-start | bytes 12296 | tf_op jit(solution)/shard_map/ppermute | solution.py:239
  6.1 4.6 %collective-permute-start.1 = (f32[2,1024]{1,0:T(2,128)S(1)}, f32[2,1024]{1,0:T(2,128)S(1)}, u32[]{:S(2)}, u32[]{:S(2)}) collective-permute-start(f32[2,1024]{1,0:T(2,128)S(1)} %constant_dynamic-update-slice_fusion), channel_id=1, source_target_pairs={{0,8},{8,0},{16,24},{24,16},{1,9},{9,1},{17,25},{25,17},{2,10},{10... | collective-permute-start | bytes 24584 | tf_op jit(solution)/shard_map/ppermute | solution.py:233
  10.6 5.8 %collective-permute-start.2 = (f32[4,1024]{1,0:T(4,128)S(1)}, f32[4,1024]{1,0:T(4,128)S(1)}, u32[]{:S(2)}, u32[]{:S(2)}) collective-permute-start(f32[4,1024]{1,0:T(4,128)S(1)} %pad_maximum_fusion.1), channel_id=1, source_target_pairs={{0,16},{8,24},{16,0},{24,8},{1,17},{9,25},{17,1},{25,9},{2,18},{10... | collective-permute-start | bytes 49160 | tf_op jit(solution)/shard_map/ppermute | solution.py:233
  13.8 1.6 %copy-start.1 = (f32[2,1024]{1,0:T(2,128)S(1)}, f32[2,1024]{1,0:T(2,128)}, u32[]{:S(2)}) copy-start(f32[2,1024]{1,0:T(2,128)} %amp_ref.1) | copy-start | bytes 24580
  13.8 1.6 %copy-start.2 = (s32[16,16]{1,0:T(8,128)S(1)}, s32[16,16]{1,0:T(8,128)}, u32[]{:S(2)}) copy-start(s32[16,16]{1,0:T(8,128)} %mask_ref.1) | copy-start | bytes 3076
  16.4 1.6 %copy-start = (f32[2,8]{1,0:T(2,128)S(1)}, f32[2,8]{1,0:T(2,128)}, u32[]{:S(2)}) copy-start(f32[2,8]{1,0:T(2,128)} %basis_ref.13) | copy-start | bytes 196
  20.9 13.8 %collective-permute-start.8 = (bf16[256,512]{1,0:T(8,128)(2,1)S(1)}, bf16[256,512]{1,0:T(8,128)(2,1)S(1)}, u32[]{:S(2)}, u32[]{:S(2)}) collective-permute-start(bf16[256,512]{1,0:T(8,128)(2,1)S(1)} %shard_map.65), channel_id=1, source_target_pairs={{0,2},{1,5},{2,0},{3,7},{4,6},{5,1},{6,4},{7,3},{8,10},{9,13},{10,... | collective-permute-start | bytes 786440 | tf_op jit(solution)/shard_map/ppermute | solution.py:230
  22.5 7.9 %collective-permute-start.5 = (bf16[256,512]{1,0:T(8,128)(2,1)S(1)}, bf16[256,512]{1,0:T(8,128)(2,1)S(1)}, u32[]{:S(2)}, u32[]{:S(2)}) collective-permute-start(bf16[256,512]{1,0:T(8,128)(2,1)S(1)} %shard_map.61), channel_id=1, source_target_pairs={{0,2},{1,5},{2,0},{3,7},{4,6},{5,1},{6,4},{7,3},{8,10},{9,13},{10,... | collective-permute-start | bytes 786440 | tf_op jit(solution)/shard_map/ppermute | solution.py:230
  24.6 10.7 %collective-permute-start.4 = (bf16[256,512]{1,0:T(8,128)(2,1)S(1)}, bf16[256,512]{1,0:T(8,128)(2,1)S(1)}, u32[]{:S(2)}, u32[]{:S(2)}) collective-permute-start(bf16[256,512]{1,0:T(8,128)(2,1)S(1)} %shard_map.59), channel_id=1, source_target_pairs={{0,2},{1,5},{2,0},{3,7},{4,6},{5,1},{6,4},{7,3},{8,10},{9,13},{10,... | collective-permute-start | bytes 786440 | tf_op jit(solution)/shard_map/ppermute | solution.py:230
  30.5 8.8 %collective-permute-start.6 = (bf16[256,512]{1,0:T(8,128)(2,1)S(1)}, bf16[256,512]{1,0:T(8,128)(2,1)S(1)}, u32[]{:S(2)}, u32[]{:S(2)}) collective-permute-start(bf16[256,512]{1,0:T(8,128)(2,1)S(1)} %add_convert_fusion.1), channel_id=1, source_target_pairs={{0,4},{1,3},{2,6},{3,1},{4,0},{5,7},{6,2},{7,5},{8,12},{9,11},{10,... | collective-permute-start | bytes 786440 | tf_op jit(solution)/shard_map/ppermute | solution.py:230
  33.4 9.2 %collective-permute-start.7 = (bf16[256,512]{1,0:T(8,128)(2,1)S(1)}, bf16[256,512]{1,0:T(8,128)(2,1)S(1)}, u32[]{:S(2)}, u32[]{:S(2)}) collective-permute-start(bf16[256,512]{1,0:T(8,128)(2,1)S(1)} %shard_map.64), channel_id=1, source_target_pairs={{0,2},{1,5},{2,0},{3,7},{4,6},{5,1},{6,4},{7,3},{8,10},{9,13},{10,... | collective-permute-start | bytes 786440 | tf_op jit(solution)/shard_map/ppermute | solution.py:230
  34.8 7.9 %collective-permute-start.9 = (bf16[256,512]{1,0:T(8,128)(2,1)S(1)}, bf16[256,512]{1,0:T(8,128)(2,1)S(1)}, u32[]{:S(2)}, u32[]{:S(2)}) collective-permute-start(bf16[256,512]{1,0:T(8,128)(2,1)S(1)} %add_convert_fusion), channel_id=1, source_target_pairs={{0,4},{1,3},{2,6},{3,1},{4,0},{5,7},{6,2},{7,5},{8,12},{9,11},{10,... | collective-permute-start | bytes 786440 | tf_op jit(solution)/shard_map/ppermute | solution.py:230
  39.4 7.1 %collective-permute-start.10 = (bf16[256,512]{1,0:T(8,128)(2,1)S(1)}, bf16[256,512]{1,0:T(8,128)(2,1)S(1)}, u32[]{:S(2)}, u32[]{:S(2)}) collective-permute-start(bf16[256,512]{1,0:T(8,128)(2,1)S(1)} %multiply_convert_fusion.1.resid_ref), channel_id=1, source_target_pairs={{0,4},{1,3},{2,6},{3,1},{4,0},{5,7},{6,2},{7,5},{8,12},{9,11},{10,... | collective-permute-start | bytes 786440 | tf_op jit(solution)/shard_map/ppermute | solution.py:230
  42.8 9.2 %collective-permute-start.11 = (bf16[256,512]{1,0:T(8,128)(2,1)S(1)}, bf16[256,512]{1,0:T(8,128)(2,1)S(1)}, u32[]{:S(2)}, u32[]{:S(2)}) collective-permute-start(bf16[256,512]{1,0:T(8,128)(2,1)S(1)} %multiply_convert_fusion.resid_ref), channel_id=1, source_target_pairs={{0,4},{1,3},{2,6},{3,1},{4,0},{5,7},{6,2},{7,5},{8,12},{9,11},{10,... | collective-permute-start | bytes 786440 | tf_op jit(solution)/shard_map/ppermute | solution.py:230
  43.5 11.9 %collective-permute-start.12 = (bf16[256,512]{1,0:T(8,128)(2,1)S(1)}, bf16[256,512]{1,0:T(8,128)(2,1)S(1)}, u32[]{:S(2)}, u32[]{:S(2)}) collective-permute-start(bf16[256,512]{1,0:T(8,128)(2,1)S(1)} %multiply_convert_fusion.1.resid_ref), channel_id=1, source_target_pairs={{0,2},{1,5},{2,0},{3,7},{4,6},{5,1},{6,4},{7,3},{8,10},{9,13},{10,... | collective-permute-start | bytes 786440 | tf_op jit(solution)/shard_map/ppermute | solution.py:230
  44.6 12.2 %collective-permute-start.13 = (bf16[256,512]{1,0:T(8,128)(2,1)S(1)}, bf16[256,512]{1,0:T(8,128)(2,1)S(1)}, u32[]{:S(2)}, u32[]{:S(2)}) collective-permute-start(bf16[256,512]{1,0:T(8,128)(2,1)S(1)} %multiply_convert_fusion.resid_ref), channel_id=1, source_target_pairs={{0,2},{1,5},{2,0},{3,7},{4,6},{5,1},{6,4},{7,3},{8,10},{9,13},{10,... | collective-permute-start | bytes 786440 | tf_op jit(solution)/shard_map/ppermute | solution.py:230
  46.6 11.3 %collective-permute-start.14 = (bf16[256,512]{1,0:T(8,128)(2,1)S(1)}, bf16[256,512]{1,0:T(8,128)(2,1)S(1)}, u32[]{:S(2)}, u32[]{:S(2)}) collective-permute-start(bf16[256,512]{1,0:T(8,128)(2,1)S(1)} %collective-permute-done.10.resid_ref), channel_id=1, source_target_pairs={{0,2},{1,5},{2,0},{3,7},{4,6},{5,1},{6,4},{7,3},{8,10},{9,13},{10,... | collective-permute-start | bytes 786440 | tf_op jit(solution)/shard_map/ppermute | solution.py:230
  52.1 7.0 %collective-permute-start.15 = (bf16[256,512]{1,0:T(8,128)(2,1)S(1)}, bf16[256,512]{1,0:T(8,128)(2,1)S(1)}, u32[]{:S(2)}, u32[]{:S(2)}) collective-permute-start(bf16[256,512]{1,0:T(8,128)(2,1)S(1)} %collective-permute-done.11.resid_ref), channel_id=1, source_target_pairs={{0,2},{1,5},{2,0},{3,7},{4,6},{5,1},{6,4},{7,3},{8,10},{9,13},{10,... | collective-permute-start | bytes 786440 | tf_op jit(solution)/shard_map/ppermute | solution.py:230
  60.6 4.7 %collective-permute-start.16 = (f32[4,1024]{1,0:T(4,128)S(1)}, f32[4,1024]{1,0:T(4,128)S(1)}, u32[]{:S(2)}, u32[]{:S(2)}) collective-permute-start(f32[4,1024]{1,0:T(4,128)S(1)} %get-tuple-element.20), channel_id=1, source_target_pairs={{0,16},{8,24},{16,0},{24,8},{1,17},{9,25},{17,1},{25,9},{2,18},{10... | collective-permute-start | bytes 49160 | tf_op jit(solution)/shard_map/ppermute | solution.py:233
  65.3 3.7 %collective-permute-start.17 = (f32[2,1024]{1,0:T(2,128)S(1)}, f32[2,1024]{1,0:T(2,128)S(1)}, u32[]{:S(2)}, u32[]{:S(2)}) collective-permute-start(f32[2,1024]{1,0:T(2,128)S(1)} %slice.17), channel_id=1, source_target_pairs={{0,8},{8,0},{16,24},{24,16},{1,9},{9,1},{17,25},{25,17},{2,10},{10... | collective-permute-start | bytes 24584 | tf_op jit(solution)/shard_map/ppermute | solution.py:233
  69.0 1.2 %collective-permute-start.18 = (f32[2,512]{1,0:T(2,128)S(1)}, f32[2,512]{1,0:T(2,128)S(1)}, u32[]{:S(2)}, u32[]{:S(2)}) collective-permute-start(f32[2,512]{1,0:T(2,128)S(1)} %slice.19), channel_id=1, source_target_pairs={{0,1},{1,0},{2,3},{3,2},{4,5},{5,4},{6,7},{7,6},{8,9},{9,8},{10,11... | collective-permute-start | bytes 12296 | tf_op jit(solution)/shard_map/ppermute | solution.py:315

commit v5 on v4

v5 whole, which is shorter than its diff:
```python
import functools

import jax
import jax.numpy as jnp
from jax import lax
from jax.experimental import pallas as pl
from jax.experimental.pallas import tpu as pltpu
from jax.sharding import PartitionSpec as P


F32 = jnp.float32
BF16 = jnp.bfloat16
MIB = 1 << 20


def across(left, right):
    return lax.dot_general(left, right, (((1,), (1,)), ((), ())), preferred_element_type=F32)


def along(left, right):
    return jnp.dot(left, right, preferred_element_type=F32)


def start_all(sems, pairs):
    copies = [pltpu.make_async_copy(src, dst, sems.at[i]) for i, (src, dst) in enumerate(pairs)]
    for copy in copies:
        copy.start()
    return copies


def weight_kernel(n, core_ref, piece_ref, amp_ref, mask_ref, *weight_refs):
    core, piece = core_ref[0], piece_ref[0]
    tile = weight_refs[0].shape[0]
    blocks = mask_ref.shape[0]
    size = n * tile // blocks

    def amp(start):
        both = amp_ref[:, pl.ds(pl.multiple_of(start, tile), tile)]
        return jnp.where(core == 0, both[0:1], both[1:2])

    here = piece * tile
    row = lax.broadcasted_iota(jnp.int32, (tile, tile), 0)
    col = lax.broadcasted_iota(jnp.int32, (tile, tile), 1)
    down = jnp.sum(jnp.where(row == col, amp(here), 0.0), axis=1, keepdims=True)
    mask = mask_ref[...].astype(BF16)
    low = lax.broadcasted_iota(jnp.int32, (tile, blocks), 1) * size
    at = here + lax.broadcasted_iota(jnp.int32, (tile, blocks), 0)
    pick = ((at >= low) & (at < low + size)).astype(BF16)
    rows = (0.5 * (along(pick, mask) + across(pick, mask))).astype(BF16)
    low = lax.broadcasted_iota(jnp.int32, (blocks, tile), 0) * size
    for d in range(n // 2 + 1):
        start = lax.rem(piece + d, n) * tile
        at = start + lax.broadcasted_iota(jnp.int32, (blocks, tile), 1)
        pick = ((at >= low) & (at < low + size)).astype(BF16)
        weight = down * amp(start) * along(rows, pick)
        for i in [0] if d == 0 else [n - 1] if d == n // 2 else [2 * d - 1, 2 * d]:
            u, at_block = divmod(i, n // 2)
            weight_refs[u][:, at_block * tile : (at_block + 1) * tile] = weight


def take_kernel(core_ref, green_ref, *rest):
    out_ref, sems = rest[-2:]
    other = 1 - core_ref[0]
    for copy in start_all(sems, [(green_ref.at[p, other], out_ref.at[p]) for p in (0, 1)]):
        copy.wait()


def mine_kernel(core_ref, green_ref, out_ref, sems):
    core, cells = core_ref[0], green_ref.shape[3]
    spots = [out_ref.at[:, pl.ds(2 * p * cells, cells)] for p in (0, 1)]
    for copy in start_all(sems, [(green_ref.at[p, core], spots[p]) for p in (0, 1)]):
        copy.wait()


def theirs_kernel(planes, core_ref, plane_ref, basis_ref, theirs_ref, field_ref, out_ref, column_ref, sems):
    del field_ref
    core, plane, cells = core_ref[0], plane_ref[0], theirs_ref.shape[2]
    spots = [out_ref.at[:, pl.ds((2 * p + 1) * cells, cells)] for p in (0, 1)]
    copies = start_all(sems, [(theirs_ref.at[p], spots[p]) for p in (0, 1)])
    each = column_ref.shape[0] // planes
    at = lax.broadcasted_iota(jnp.int32, column_ref.shape, 0)
    column = jnp.zeros(column_ref.shape, F32)
    for i in range(column_ref.shape[0]):
        column = jnp.where(at == i, basis_ref[core, (plane ^ (i // each)) * each + i % each], column)
    column_ref[...] = column
    for copy in copies:
        copy.wait()


def corr_kernel(n, parts, piece_ref, column_ref, known_ref, green_ref, *out_refs):
    stations, width = green_ref.shape
    tile, half = stations // n, width // 2
    piece = piece_ref[0]

    def block(d):
        start = lax.rem(piece + d, n) * tile
        return green_ref[pl.ds(pl.multiple_of(start, tile), tile), :]

    def put(i, value):
        for part, out_ref in zip(parts, out_refs):
            if i in part:
                at = (i - part[0]) * tile
                out_ref[:, at : at + tile] = value.astype(out_ref.dtype)

    source = jnp.sum(column_ref[:, 0:1] * known_ref[...], axis=0, keepdims=True)
    source = jnp.concatenate((source, source), axis=1)
    scaled = (block(0).astype(F32) * source).astype(BF16)
    turned = jnp.concatenate((scaled[:, half:], -scaled[:, :half]), axis=1)
    both = jnp.concatenate((scaled, turned), axis=0)
    wanted = [i for part in parts for i in part]
    if 0 in wanted:
        pair = across(both, block(0))
        row = lax.broadcasted_iota(jnp.int32, (tile, tile), 0)
        col = lax.broadcasted_iota(jnp.int32, (tile, tile), 1)
        put(0, jnp.where(row >= col, pair[:tile], pair[tile:]))
    for d in range(1, n // 2):
        if 2 * d - 1 in wanted and 2 * d in wanted:
            pair = across(both, block(d))
            put(2 * d - 1, pair[:tile])
            put(2 * d, pair[tile:])
        elif 2 * d - 1 in wanted:
            put(2 * d - 1, across(scaled, block(d)))
        elif 2 * d in wanted:
            put(2 * d, across(turned, block(d)))
    if n - 1 in wanted:
        put(n - 1, across(jnp.where(piece < n // 2, scaled, turned), block(n // 2)))


def sens_sum(n, part, step, piece, resid_ref, green_ref, emit):
    stations, width = green_ref.shape
    tile, half = stations // n, width // 2
    starts = [pl.multiple_of(lax.rem(piece + d, n) * tile, tile) for d in range(n // 2 + 1)]
    real = piece < n // 2
    terms = []
    for i in part:
        at = (i - part[0]) * tile
        value = resid_ref[:, at : at + tile]
        if i == 0:
            row = lax.broadcasted_iota(jnp.int32, (tile, tile), 0)
            col = lax.broadcasted_iota(jnp.int32, (tile, tile), 1)
            diag = value.astype(F32)
            low = jnp.where(row > col, diag, jnp.where(row == col, 0.5 * diag, 0.0))
            terms.append(("re", 0, low.astype(BF16)))
            terms.append(("im", 0, jnp.where(row < col, diag, 0.0).astype(BF16)))
        elif i == n - 1:
            terms.append(("either", n // 2, value))
        else:
            terms.append(("re" if i % 2 else "im", (i + 1) // 2, value))
    for at in range(0, half, step):

        def fields(d):
            rows = pl.ds(starts[d], tile)
            return green_ref[rows, at : at + step], green_ref[rows, half + at : half + at + step]

        yre, yim = jnp.zeros((tile, step), F32), jnp.zeros((tile, step), F32)
        for kind, d, value in terms:
            re, im = fields(d)
            tu, tv = along(value, re), along(value, im)
            if kind == "re":
                yre, yim = yre + tu, yim + tv
            elif kind == "im":
                yre, yim = yre - tv, yim + tu
            else:
                yre, yim = yre + jnp.where(real, tu, -tv), yim + jnp.where(real, tv, tu)
        re, im = fields(0)
        share = re.astype(F32) * yre + im.astype(F32) * yim
        emit(at, 2.0 * jnp.sum(share, axis=0, keepdims=True))


def sens_kernel(n, part, step, piece_ref, resid_ref, green_ref, out_ref):
    def emit(at, value):
        out_ref[:, at : at + step] = value

    sens_sum(n, part, step, piece_ref[0], resid_ref, green_ref, emit)


def last_kernel(n, part, step, piece_ref, column_ref, before_ref, resid_ref, green_ref, *out_refs):
    rows = out_refs[0].shape[0]
    column = column_ref[:, 0:1]

    def emit(at, value):
        product = column * (before_ref[:, at : at + step] + value)
        for k, out_ref in enumerate(out_refs):
            out_ref[:, at : at + step] = product[k * rows : (k + 1) * rows]

    sens_sum(n, part, step, piece_ref[0], resid_ref, green_ref, emit)


def first_sent(n):
    return n - 1, 0


SMEM = pl.BlockSpec(memory_space=pltpu.SMEM)
VMEM = pl.BlockSpec(memory_space=pltpu.VMEM)
HBM = pl.BlockSpec(memory_space=pltpu.HBM)


def call(kernel, shapes, specs, flops, moved, *args, scratch=(), alias={}, grant=24):
    out_shape = [jax.ShapeDtypeStruct(shape, dtype) for shape, dtype in shapes]
    out = pl.pallas_call(
        kernel,
        out_shape=out_shape,
        in_specs=specs,
        out_specs=[VMEM] * len(shapes),
        scratch_shapes=scratch,
        input_output_aliases=alias,
        compiler_params=pltpu.CompilerParams(vmem_limit_bytes=grant * MIB),
        cost_estimate=pl.CostEstimate(flops=flops, bytes_accessed=moved, transcendentals=0),
    )(*args)
    return out if len(out) > 1 else out[0]


def on_device(n_freq, n_cell, green, coeffs, basis, amplitude, block_mask):
    n = n_cell // 2
    bits, z_bits = n.bit_length() - 1, n_freq.bit_length() - 1
    stations, cells = green.shape[2], green.shape[3]
    tile, width, each = stations // n, 4 * cells, coeffs.shape[0]
    here = lax.axis_index("cell").astype(jnp.int32)
    plane = lax.axis_index("freq").astype(jnp.int32)
    core, chip = here % 2, here // 2
    flops = 2 * tile * tile * width
    moved = 2 * stations * width + 2 * tile * stations
    halves = [tuple(range(u * n // 2, (u + 1) * n // 2)) for u in (0, 1)]

    def dims(which):
        return [(which + j) % bits for j in range(bits)]

    swap_core = [(i, i ^ 1) for i in range(n_cell)]

    def swap_chip(value, j):
        pairs = [(i, i ^ (2 << dims(i % 2)[j])) for i in range(n_cell)]
        return lax.ppermute(value, "cell", pairs)

    def swap_plane(value, j):
        return lax.ppermute(value, "freq", [(i, i ^ (1 << j)) for i in range(n_freq)])

    def piece_of(q):
        flips = [sum(((q >> j) & 1) << dims(which)[j] for j in range(bits)) for which in (0, 1)]
        return chip ^ jnp.where(core == 0, flips[0], flips[1])

    cores, planes = core.reshape(1), plane.reshape(1)
    pieces = [piece_of(q).reshape(1) for q in range(n)]
    green = pltpu.with_memory_space_constraint(green, pltpu.HBM)
    two = [pltpu.SemaphoreType.DMA((2,))]
    theirs = call(
        take_kernel, [((2, stations, cells), BF16)], [SMEM, HBM] + [SMEM] * (n + 1), 0,
        8 * stations * cells, cores, green, planes, *pieces, scratch=two,
    )
    theirs = lax.ppermute(theirs, "cell", swap_core)
    known = coeffs
    for j in range(z_bits):
        near = swap_plane(known, j)
        known = jnp.concatenate((known, near), axis=0)
    beside = lax.ppermute(known, "cell", swap_core)
    known = jnp.concatenate((known, beside), axis=1)

    field = call(
        mine_kernel, [((stations, width), BF16)], [SMEM, HBM], 0,
        2 * stations * width, cores, green, scratch=two,
    )
    field, column = call(
        functools.partial(theirs_kernel, n_freq),
        [((stations, width), BF16), ((n_freq * each, 128), F32)], [SMEM, SMEM, SMEM, VMEM, VMEM], 0,
        2 * stations * width, cores, planes, basis, theirs, field, scratch=two, alias={4: 0},
    )

    def corr_parts(q, parts, dtype):
        shapes = [((tile, len(part) * tile), dtype) for part in parts]
        out = call(
            functools.partial(corr_kernel, n, parts), shapes, [SMEM, VMEM, VMEM, VMEM],
            flops * sum(len(part) for part in parts), moved, pieces[q], column, known, field,
        )
        return out if len(parts) > 1 else [out]

    held = {}
    for q in sorted(range(n), key=lambda q: (q % 2 == 0, -q)):
        if q % 2 == 0:
            held[q, 0], held[q, 1] = corr_parts(q, halves, F32)
            continue
        for u in (0, 1):
            if (q, u) == first_sent(n):
                middle = n // 4
                held[q, "b"] = corr_parts(q, [halves[u][middle:]], BF16)[0]
                held[q, "a"] = corr_parts(q, [halves[u][:middle]], BF16)[0]
            else:
                held[q, u] = corr_parts(q, [halves[u]], BF16)[0]
    weight = call(
        functools.partial(weight_kernel, n), [((tile, stations // 2), F32)] * 2,
        [SMEM, SMEM, VMEM, VMEM], 0, 4 * tile * stations, cores, pieces[0], amplitude, block_mask,
    )
    for j in range(bits):
        for q in sorted((q for q in range(n) if q % (1 << j) == 0 and (q >> j) & 1), reverse=True):
            for u in (0, 1):
                if (q, u) == first_sent(n):
                    late, early = (swap_chip(held[q, k], j) for k in "ab")
                    got = jnp.concatenate((late, early), axis=1)
                else:
                    got = swap_chip(held[q, u].astype(BF16), j)
                held[q ^ (1 << j), u] = held[q ^ (1 << j), u] + got.astype(F32)
    resid = {(0, u): (held[0, u] * weight[u]).astype(BF16) for u in (0, 1)}

    order, parts = [0], {"0": halves[0], "1": halves[1], "c": halves[1][: n // 4], "d": halves[1][n // 4 :]}
    for j in reversed(range(bits)):
        for q in list(order):
            order.append(q | (1 << j))
            for u in (0, 1):
                if (order[-1], u) == (n - 1, 1):
                    cut = n // 4 * tile
                    resid[n - 1, "c"] = swap_chip(resid[q, u][:, :cut], j)
                    resid[n - 1, "d"] = swap_chip(resid[q, u][:, cut:], j)
                else:
                    resid[order[-1], u] = swap_chip(resid[q, u], j)
    step = min(512, width // 2)
    sens = 0.0
    for (q, u), value in resid.items():
        if (q, u) == (n - 1, "d"):
            continue
        part = parts[str(u)]
        sens = sens + call(
            functools.partial(sens_kernel, n, part, step), [((1, width // 2), F32)],
            [SMEM, VMEM, VMEM], flops * len(part), moved, pieces[q], value, field,
        )
    half_rows = ((n_freq * each // 2, width // 2), F32)
    low, high = call(
        functools.partial(last_kernel, n, parts["d"], step), [half_rows] * 2,
        [SMEM, VMEM, VMEM, VMEM, VMEM], flops * (n // 4), moved,
        pieces[n - 1], column, sens, resid[n - 1, "d"], field,
    )

    for j in reversed(range(z_bits)):
        kept = low + swap_plane(high, j)
        low, high = kept[: kept.shape[0] // 2], kept[kept.shape[0] // 2 :]
    return kept[:, :cells] + lax.ppermute(kept[:, cells:], "cell", swap_core)


def solution(mesh):
    placed = (
        P(None, "freq", None, "cell"),
        P("freq", "cell"),
        P("freq", None),
        P("freq", None),
        P(),
    )
    n_freq, n_cell = mesh.shape["freq"], mesh.shape["cell"]

    def body(*args):
        return on_device(n_freq, n_cell, *args)

    return jax.shard_map(
        body, mesh=mesh, in_specs=placed, out_specs=P("freq", "cell"), check_vma=False
    )
```

time: 71.1 us -> 69.8 us (0.982)
  starting transfers between devices: 24.3 us -> 30.8 us
  Pallas kernels: 25 us -> 20.3 us
  waiting for transfers between devices: 19.9 us -> 17 us
    ppermute x12 -> x14, starting transfers between devices: 13.6 us -> 19.3 us  [swap_chip(): return lax.ppermute(value, 'cell', pairs)]
    pallas_call x18 -> x20, Pallas kernels: 25 us -> 20.3 us  [call(): pl.pallas_call(kernel, out_shape=out_shape, in_specs=specs, out_specs=[VM...]
    ppermute x1, waiting for transfers between devices: 3.75 us -> 0.01 us  [on_device(): beside = lax.ppermute(known, 'cell', swap_core)]
    ppermute x4, starting transfers between devices: 9.99 us -> 10.8 us  [swap_plane(): return lax.ppermute(value, 'freq', [(i, i ^ 1 << j) for i in range(n_freq)])]
    ppermute x12 -> x14, waiting for transfers between devices: 9.02 us -> 9.13 us  [swap_chip(): return lax.ppermute(value, 'cell', pairs)]
  transfers between devices with their start and end apart: 19 -> 21, of which waited for: 8 -> 11; matrix products, arithmetic and copies ran while one was open for 1% -> 1% of each run, Pallas kernels for 25% -> 20%
where the time goes in v5:
time: 69.8 us; the launch traced here: 69.6 us
  starting transfers between devices  30.8 us (44%)
  Pallas kernels  20.3 us (29%)
  waiting for transfers between devices  17 us (24%)
  other arithmetic  1.11 us (2%)
    pallas_call x20, Pallas kernels, call(): pl.pallas_call(kernel, out_shape=out_shape, in_specs=specs, out_specs=[VM...  20.3 us
    ppermute x14, starting transfers between devices, swap_chip(): return lax.ppermute(value, 'cell', pairs)  19.3 us
    ppermute x4, starting transfers between devices, swap_plane(): return lax.ppermute(value, 'freq', [(i, i ^ 1 << j) for i in range(n_freq)])  10.8 us
    ppermute x14, waiting for transfers between devices, swap_chip(): return lax.ppermute(value, 'cell', pairs)  9.13 us
    ppermute x4, waiting for transfers between devices, swap_plane(): return lax.ppermute(value, 'freq', [(i, i ^ 1 << j) for i in range(n_freq)])  6.68 us
  transfers between devices with their start and end apart: 21, of which 11 were waited for; matrix products, arithmetic and copies ran while one was open for 1% of the time, Pallas kernels for 20%

profile of v5, /device:TPU:0, one launch (start us, length us, event | category | flops | bytes accessed | tf_op | source)
XLA Modules:
  0.0 69.6 jit_solution(9219382032733481832)
XLA Ops:
  0.0 1.6 %shard_map.55 = bf16[2,1024,512]{2,1,0:T(8,128)(2,1)S(1)} custom-call(s32[1]{0:T(128)} %bitcast.1.core_ref, bf16[2,2,1024,512]{3,2,1,0:T(8,128)(2,1)} %green_ref.3, s32[1]{0:T(128)} %bitcast.2.rest_0_.plane_ref, s32[1]{0:T(128)} %bitcast.3.rest_1_.piece_ref, s32[1]{0:T(128)} %bitcast.4.rest_2_.piece_ref, s32[1]{0:T(128)} %bitcast.5.rest_3_.piece_ref, ...), custom_call_target="tpu_custom_call" | custom-call | bytes 4194304 | tf_op jit(solution)/shard_map/pallas_call | solution.py:200
  1.6 0.6 collective-permute-start
  2.1 2.6 %collective-permute-start.1 = (f32[2,512]{1,0:T(2,128)S(1)}, f32[2,512]{1,0:T(2,128)S(1)}, u32[]{:S(2)}, u32[]{:S(2)}) collective-permute-start(f32[2,512]{1,0:T(2,128)S(1)} %copy-done.3), channel_id=1, source_target_pairs={{0,8},{8,0},{16,24},{24,16},{1,9},{9,1},{17,25},{25,17},{2,10},{10... | collective-permute-start | bytes 12296 | tf_op jit(solution)/shard_map/ppermute | solution.py:235
  4.8 1.6 %collective-permute-done.1 = f32[2,512]{1,0:T(2,128)S(1)} collective-permute-done((f32[2,512]{1,0:T(2,128)S(1)}, f32[2,512]{1,0:T(2,128)S(1)}, u32[]{:S(2)}, u32[]{:S(2)}) %collective-permute-start.1) | collective-permute-done | bytes 4128 | tf_op jit(solution)/shard_map/ppermute | solution.py:235
  6.4 3.1 %collective-permute-start.2 = (f32[4,512]{1,0:T(4,128)S(1)}, f32[4,512]{1,0:T(4,128)S(1)}, u32[]{:S(2)}, u32[]{:S(2)}) collective-permute-start(f32[4,512]{1,0:T(4,128)S(1)} %pad_maximum_fusion.2), channel_id=1, source_target_pairs={{0,16},{8,24},{16,0},{24,8},{1,17},{9,25},{17,1},{25,9},{2,18},{10... | collective-permute-start | bytes 24584 | tf_op jit(solution)/shard_map/ppermute | solution.py:235
  9.5 1.6 %collective-permute-done.2 = f32[4,512]{1,0:T(4,128)S(1)} collective-permute-done((f32[4,512]{1,0:T(4,128)S(1)}, f32[4,512]{1,0:T(4,128)S(1)}, u32[]{:S(2)}, u32[]{:S(2)}) %collective-permute-start.2) | collective-permute-done | bytes 8224 | tf_op jit(solution)/shard_map/ppermute | solution.py:235
  11.2 1.6 %shard_map.56.field_ref = bf16[1024,2048]{1,0:T(8,128)(2,1)S(1)} custom-call(s32[1]{0:T(128)} %bitcast.1.core_ref, bf16[2,2,1024,512]{3,2,1,0:T(8,128)(2,1)} %green_ref.3), custom_call_target="tpu_custom_call" | custom-call | bytes 4194304 | tf_op jit(solution)/shard_map/pallas_call | solution.py:200
  12.8 0.4 shard_map.63
  13.3 0.9 %shard_map.57 = (bf16[1024,2048]{1,0:T(8,128)(2,1)S(1)}, f32[8,128]{1,0:T(8,128)S(1)}) custom-call(s32[1]{0:T(128)} %bitcast.1.core_ref, s32[1]{0:T(128)} %bitcast.2.rest_0_.plane_ref, f32[2,8]{1,0:T(2,128)S(1)} %copy-done.2, bf16[2,1024,512]{2,1,0:T(8,128)(2,1)S(1)} %collective-permute-done.theirs_ref, ...), custom_call_target="tpu_custom_call", output_to_operand_aliasing={{0}: (4, {})} | custom-call | bytes 4194304 | tf_op jit(solution)/shard_map/pallas_call | solution.py:200
  14.2 1.6 %shard_map.58 = (f32[256,512]{1,0:T(8,128)S(1)}, f32[256,512]{1,0:T(8,128)S(1)}) custom-call(s32[1]{0:T(128)} %bitcast.3.rest_1_.piece_ref, f32[8,128]{1,0:T(8,128)S(1)} %get-tuple-element.15.column_ref, f32[8,1024]{1,0:T(8,128)S(1)} %pad_maximum_fusion.known_ref, bf16[1024,2048]{1,0:T(8,128)(2,1)S(1)} %get-tuple-element.16.green_ref), custom_call_target="tpu_custom_call" | custom-call | flops 1073741824 | bytes 4718592 | tf_op jit(solution)/shard_map/pallas_call | solution.py:200
  15.8 0.8 %shard_map.66 = bf16[256,512]{1,0:T(8,128)(2,1)S(1)} custom-call(s32[1]{0:T(128)} %bitcast.rest_4_.piece_ref, f32[8,128]{1,0:T(8,128)S(1)} %get-tuple-element.15.column_ref, f32[8,1024]{1,0:T(8,128)S(1)} %pad_maximum_fusion.known_ref, bf16[1024,2048]{1,0:T(8,128)(2,1)S(1)} %get-tuple-element.16.green_ref), custom_call_target="tpu_custom_call" | custom-call | flops 536870912 | bytes 4718592 | tf_op jit(solution)/shard_map/pallas_call | solution.py:200
  16.6 0.8 %shard_map.61 = bf16[256,256]{1,0:T(8,128)(2,1)S(1)} custom-call(s32[1]{0:T(128)} %bitcast.rest_4_.piece_ref, f32[8,128]{1,0:T(8,128)S(1)} %get-tuple-element.15.column_ref, f32[8,1024]{1,0:T(8,128)S(1)} %pad_maximum_fusion.known_ref, bf16[1024,2048]{1,0:T(8,128)(2,1)S(1)} %get-tuple-element.16.green_ref), custom_call_target="tpu_custom_call" | custom-call | flops 268435456 | bytes 4718592 | tf_op jit(solution)/shard_map/pallas_call | solution.py:200
  17.4 0.5 shard_map.62
  17.9 1.9 %collective-permute-start.9 = (bf16[256,512]{1,0:T(8,128)(2,1)S(1)}, bf16[256,512]{1,0:T(8,128)(2,1)S(1)}, u32[]{:S(2)}, u32[]{:S(2)}) collective-permute-start(bf16[256,512]{1,0:T(8,128)(2,1)S(1)} %shard_map.66), channel_id=1, source_target_pairs={{0,2},{1,5},{2,0},{3,7},{4,6},{5,1},{6,4},{7,3},{8,10},{9,13},{10,... | collective-permute-start | bytes 786440 | tf_op jit(solution)/shard_map/ppermute | solution.py:232
  20.0 1.8 %collective-permute-start.6 = (bf16[256,256]{1,0:T(8,128)(2,1)S(1)}, bf16[256,256]{1,0:T(8,128)(2,1)S(1)}, u32[]{:S(2)}, u32[]{:S(2)}) collective-permute-start(bf16[256,256]{1,0:T(8,128)(2,1)S(1)} %shard_map.62), channel_id=1, source_target_pairs={{0,2},{1,5},{2,0},{3,7},{4,6},{5,1},{6,4},{7,3},{8,10},{9,13},{10,... | collective-permute-start | bytes 393224 | tf_op jit(solution)/shard_map/ppermute | solution.py:232
  21.8 1.0 %shard_map.59 = bf16[256,512]{1,0:T(8,128)(2,1)S(1)} custom-call(s32[1]{0:T(128)} %bitcast.4.rest_2_.piece_ref, f32[8,128]{1,0:T(8,128)S(1)} %get-tuple-element.15.column_ref, f32[8,1024]{1,0:T(8,128)S(1)} %pad_maximum_fusion.known_ref, bf16[1024,2048]{1,0:T(8,128)(2,1)S(1)} %get-tuple-element.16.green_ref), custom_call_target="tpu_custom_call" | custom-call | flops 536870912 | bytes 4718592 | tf_op jit(solution)/shard_map/pallas_call | solution.py:200
  23.1 1.6 %shard_map.60 = (f32[256,512]{1,0:T(8,128)S(1)}, f32[256,512]{1,0:T(8,128)S(1)}) custom-call(s32[1]{0:T(128)} %bitcast.5.rest_3_.piece_ref, f32[8,128]{1,0:T(8,128)S(1)} %get-tuple-element.15.column_ref, f32[8,1024]{1,0:T(8,128)S(1)} %pad_maximum_fusion.known_ref, bf16[1024,2048]{1,0:T(8,128)(2,1)S(1)} %get-tuple-element.16.green_ref), custom_call_target="tpu_custom_call" | custom-call | flops 1073741824 | bytes 4718592 | tf_op jit(solution)/shard_map/pallas_call | solution.py:200
  24.7 1.0 %collective-permute-done.5 = bf16[256,256]{1,0:T(8,128)(2,1)S(1)} collective-permute-done((bf16[256,256]{1,0:T(8,128)(2,1)S(1)}, bf16[256,256]{1,0:T(8,128)(2,1)S(1)}, u32[]{:S(2)}, u32[]{:S(2)}) %collective-permute-start.5) | collective-permute-done | bytes 131104 | tf_op jit(solution)/shard_map/ppermute | solution.py:232
  25.7 1.4 %collective-permute-done.6 = bf16[256,256]{1,0:T(8,128)(2,1)S(1)} collective-permute-done((bf16[256,256]{1,0:T(8,128)(2,1)S(1)}, bf16[256,256]{1,0:T(8,128)(2,1)S(1)}, u32[]{:S(2)}, u32[]{:S(2)}) %collective-permute-start.6) | collective-permute-done | bytes 131104 | tf_op jit(solution)/shard_map/ppermute | solution.py:232
  27.2 1.9 %collective-permute-start.7 = (bf16[256,512]{1,0:T(8,128)(2,1)S(1)}, bf16[256,512]{1,0:T(8,128)(2,1)S(1)}, u32[]{:S(2)}, u32[]{:S(2)}) collective-permute-start(bf16[256,512]{1,0:T(8,128)(2,1)S(1)} %add_convert_fusion.1), channel_id=1, source_target_pairs={{0,4},{1,3},{2,6},{3,1},{4,0},{5,7},{6,2},{7,5},{8,12},{9,11},{10,... | collective-permute-start | bytes 786440 | tf_op jit(solution)/shard_map/ppermute | solution.py:232
  29.1 0.8 %shard_map.65 = bf16[256,512]{1,0:T(8,128)(2,1)S(1)} custom-call(s32[1]{0:T(128)} %bitcast.4.rest_2_.piece_ref, f32[8,128]{1,0:T(8,128)S(1)} %get-tuple-element.15.column_ref, f32[8,1024]{1,0:T(8,128)S(1)} %pad_maximum_fusion.known_ref, bf16[1024,2048]{1,0:T(8,128)(2,1)S(1)} %get-tuple-element.16.green_ref), custom_call_target="tpu_custom_call" | custom-call | flops 536870912 | bytes 4718592 | tf_op jit(solution)/shard_map/pallas_call | solution.py:200
  29.9 1.6 %collective-permute-start.8 = (bf16[256,512]{1,0:T(8,128)(2,1)S(1)}, bf16[256,512]{1,0:T(8,128)(2,1)S(1)}, u32[]{:S(2)}, u32[]{:S(2)}) collective-permute-start(bf16[256,512]{1,0:T(8,128)(2,1)S(1)} %shard_map.65), channel_id=1, source_target_pairs={{0,2},{1,5},{2,0},{3,7},{4,6},{5,1},{6,4},{7,3},{8,10},{9,13},{10,... | collective-permute-start | bytes 786440 | tf_op jit(solution)/shard_map/ppermute | solution.py:232
  31.5 0.6 collective-permute-start.10
  32.1 3.3 %collective-permute-done.7 = bf16[256,512]{1,0:T(8,128)(2,1)S(1)} collective-permute-done((bf16[256,512]{1,0:T(8,128)(2,1)S(1)}, bf16[256,512]{1,0:T(8,128)(2,1)S(1)}, u32[]{:S(2)}, u32[]{:S(2)}) %collective-permute-start.7) | collective-permute-done | bytes 262176 | tf_op jit(solution)/shard_map/ppermute | solution.py:232
  35.6 2.3 %collective-permute-start.11 = (bf16[256,512]{1,0:T(8,128)(2,1)S(1)}, bf16[256,512]{1,0:T(8,128)(2,1)S(1)}, u32[]{:S(2)}, u32[]{:S(2)}) collective-permute-start(bf16[256,512]{1,0:T(8,128)(2,1)S(1)} %multiply_convert_fusion.1.resid_ref), channel_id=1, source_target_pairs={{0,4},{1,3},{2,6},{3,1},{4,0},{5,7},{6,2},{7,5},{8,12},{9,11},{10,... | collective-permute-start | bytes 786440 | tf_op jit(solution)/shard_map/ppermute | solution.py:232
  37.8 2.0 %collective-permute-start.13 = (bf16[256,512]{1,0:T(8,128)(2,1)S(1)}, bf16[256,512]{1,0:T(8,128)(2,1)S(1)}, u32[]{:S(2)}, u32[]{:S(2)}) collective-permute-start(bf16[256,512]{1,0:T(8,128)(2,1)S(1)} %multiply_convert_fusion.1.resid_ref), channel_id=1, source_target_pairs={{0,2},{1,5},{2,0},{3,7},{4,6},{5,1},{6,4},{7,3},{8,10},{9,13},{10,... | collective-permute-start | bytes 786440 | tf_op jit(solution)/shard_map/ppermute | solution.py:232
  39.8 1.2 %collective-permute-done.10 = bf16[256,512]{1,0:T(8,128)(2,1)S(1)} collective-permute-done((bf16[256,512]{1,0:T(8,128)(2,1)S(1)}, bf16[256,512]{1,0:T(8,128)(2,1)S(1)}, u32[]{:S(2)}, u32[]{:S(2)}) %collective-permute-start.10) | collective-permute-done | bytes 262176 | tf_op jit(solution)/shard_map/ppermute | solution.py:232
  41.1 2.0 %collective-permute-start.12 = (bf16[256,512]{1,0:T(8,128)(2,1)S(1)}, bf16[256,512]{1,0:T(8,128)(2,1)S(1)}, u32[]{:S(2)}, u32[]{:S(2)}) collective-permute-start(bf16[256,512]{1,0:T(8,128)(2,1)S(1)} %multiply_convert_fusion.resid_ref), channel_id=1, source_target_pairs={{0,4},{1,3},{2,6},{3,1},{4,0},{5,7},{6,2},{7,5},{8,12},{9,11},{10,... | collective-permute-start | bytes 786440 | tf_op jit(solution)/shard_map/ppermute | solution.py:232
  43.1 1.1 %shard_map.64 = f32[1,1024]{1,0:T(1,128)S(1)} custom-call(s32[1]{0:T(128)} %bitcast.3.rest_1_.piece_ref, bf16[256,512]{1,0:T(8,128)(2,1)S(1)} %multiply_convert_fusion.1.resid_ref, bf16[1024,2048]{1,0:T(8,128)(2,1)S(1)} %get-tuple-element.16.green_ref), custom_call_target="tpu_custom_call" | custom-call | flops 536870912 | bytes 4718592 | tf_op jit(solution)/shard_map/pallas_call | solution.py:200
  44.3 1.7 %collective-permute-start.14 = (bf16[256,512]{1,0:T(8,128)(2,1)S(1)}, bf16[256,512]{1,0:T(8,128)(2,1)S(1)}, u32[]{:S(2)}, u32[]{:S(2)}) collective-permute-start(bf16[256,512]{1,0:T(8,128)(2,1)S(1)} %multiply_convert_fusion.resid_ref), channel_id=1, source_target_pairs={{0,2},{1,5},{2,0},{3,7},{4,6},{5,1},{6,4},{7,3},{8,10},{9,13},{10,... | collective-permute-start | bytes 786440 | tf_op jit(solution)/shard_map/ppermute | solution.py:232
  46.0 1.0 %shard_map.67 = f32[1,1024]{1,0:T(1,128)S(1)} custom-call(s32[1]{0:T(128)} %bitcast.3.rest_1_.piece_ref, bf16[256,512]{1,0:T(8,128)(2,1)S(1)} %multiply_convert_fusion.resid_ref, bf16[1024,2048]{1,0:T(8,128)(2,1)S(1)} %get-tuple-element.16.green_ref), custom_call_target="tpu_custom_call" | custom-call | flops 536870912 | bytes 4718592 | tf_op jit(solution)/shard_map/pallas_call | solution.py:200
  47.0 1.0 %collective-permute-start.15 = (bf16[256,512]{1,0:T(8,128)(2,1)S(1)}, bf16[256,512]{1,0:T(8,128)(2,1)S(1)}, u32[]{:S(2)}, u32[]{:S(2)}) collective-permute-start(bf16[256,512]{1,0:T(8,128)(2,1)S(1)} %collective-permute-done.11.resid_ref), channel_id=1, source_target_pairs={{0,2},{1,5},{2,0},{3,7},{4,6},{5,1},{6,4},{7,3},{8,10},{9,13},{10,... | collective-permute-start | bytes 786440 | tf_op jit(solution)/shard_map/ppermute | solution.py:232
  48.0 1.1 %shard_map.68 = f32[1,1024]{1,0:T(1,128)S(1)} custom-call(s32[1]{0:T(128)} %bitcast.5.rest_3_.piece_ref, bf16[256,512]{1,0:T(8,128)(2,1)S(1)} %collective-permute-done.11.resid_ref, bf16[1024,2048]{1,0:T(8,128)(2,1)S(1)} %get-tuple-element.16.green_ref), custom_call_target="tpu_custom_call" | custom-call | flops 536870912 | bytes 4718592 | tf_op jit(solution)/shard_map/pallas_call | solution.py:200
  49.1 1.1 %shard_map.70 = f32[1,1024]{1,0:T(1,128)S(1)} custom-call(s32[1]{0:T(128)} %bitcast.4.rest_2_.piece_ref, bf16[256,512]{1,0:T(8,128)(2,1)S(1)} %collective-permute-done.13.resid_ref, bf16[1024,2048]{1,0:T(8,128)(2,1)S(1)} %get-tuple-element.16.green_ref), custom_call_target="tpu_custom_call" | custom-call | flops 536870912 | bytes 4718592 | tf_op jit(solution)/shard_map/pallas_call | solution.py:200
  50.3 1.3 %collective-permute-done.12.resid_ref = bf16[256,512]{1,0:T(8,128)(2,1)S(1)} collective-permute-done((bf16[256,512]{1,0:T(8,128)(2,1)S(1)}, bf16[256,512]{1,0:T(8,128)(2,1)S(1)}, u32[]{:S(2)}, u32[]{:S(2)}) %collective-permute-start.12) | collective-permute-done | bytes 262176 | tf_op jit(solution)/shard_map/ppermute | solution.py:232
  51.6 2.1 %collective-permute-start.16 = (bf16[256,256]{1,0:T(8,128)(2,1)S(1)}, bf16[256,256]{1,0:T(8,128)(2,1)S(1)}, u32[]{:S(2)}, u32[]{:S(2)}) collective-permute-start(bf16[256,256]{1,0:T(8,128)(2,1)S(1)} %get-tuple-element.26), channel_id=1, source_target_pairs={{0,2},{1,5},{2,0},{3,7},{4,6},{5,1},{6,4},{7,3},{8,10},{9,13},{10,... | collective-permute-start | bytes 393224 | tf_op jit(solution)/shard_map/ppermute | solution.py:232
  53.8 1.2 %shard_map.69 = f32[1,1024]{1,0:T(1,128)S(1)} custom-call(s32[1]{0:T(128)} %bitcast.5.rest_3_.piece_ref, bf16[256,512]{1,0:T(8,128)(2,1)S(1)} %collective-permute-done.12.resid_ref, bf16[1024,2048]{1,0:T(8,128)(2,1)S(1)} %get-tuple-element.16.green_ref), custom_call_target="tpu_custom_call" | custom-call | flops 536870912 | bytes 4718592 | tf_op jit(solution)/shard_map/pallas_call | solution.py:200
  54.9 1.0 %shard_map.71 = f32[1,1024]{1,0:T(1,128)S(1)} custom-call(s32[1]{0:T(128)} %bitcast.4.rest_2_.piece_ref, bf16[256,512]{1,0:T(8,128)(2,1)S(1)} %collective-permute-done.14.resid_ref, bf16[1024,2048]{1,0:T(8,128)(2,1)S(1)} %get-tuple-element.16.green_ref), custom_call_target="tpu_custom_call" | custom-call | flops 536870912 | bytes 4718592 | tf_op jit(solution)/shard_map/pallas_call | solution.py:200
  56.0 1.2 %shard_map.72 = f32[1,1024]{1,0:T(1,128)S(1)} custom-call(s32[1]{0:T(128)} %bitcast.rest_4_.piece_ref, bf16[256,512]{1,0:T(8,128)(2,1)S(1)} %collective-permute-done.15.resid_ref, bf16[1024,2048]{1,0:T(8,128)(2,1)S(1)} %get-tuple-element.16.green_ref), custom_call_target="tpu_custom_call" | custom-call | flops 536870912 | bytes 4718592 | tf_op jit(solution)/shard_map/pallas_call | solution.py:200
  57.1 0.5 shard_map.73
  57.7 0.9 %collective-permute-done.17.resid_ref = bf16[256,256]{1,0:T(8,128)(2,1)S(1)} collective-permute-done((bf16[256,256]{1,0:T(8,128)(2,1)S(1)}, bf16[256,256]{1,0:T(8,128)(2,1)S(1)}, u32[]{:S(2)}, u32[]{:S(2)}) %collective-permute-start.17) | collective-permute-done | bytes 131104 | tf_op jit(solution)/shard_map/ppermute | solution.py:232
  58.6 0.6 shard_map.74
  59.2 3.1 %collective-permute-start.18 = (f32[4,1024]{1,0:T(4,128)S(1)}, f32[4,1024]{1,0:T(4,128)S(1)}, u32[]{:S(2)}, u32[]{:S(2)}) collective-permute-start(f32[4,1024]{1,0:T(4,128)S(1)} %get-tuple-element.24), channel_id=1, source_target_pairs={{0,16},{8,24},{16,0},{24,8},{1,17},{9,25},{17,1},{25,9},{2,18},{10... | collective-permute-start | bytes 49160 | tf_op jit(solution)/shard_map/ppermute | solution.py:235
  62.3 1.7 %collective-permute-done.18 = f32[4,1024]{1,0:T(4,128)S(1)} collective-permute-done((f32[4,1024]{1,0:T(4,128)S(1)}, f32[4,1024]{1,0:T(4,128)S(1)}, u32[]{:S(2)}, u32[]{:S(2)}) %collective-permute-start.18) | collective-permute-done | bytes 16416 | tf_op jit(solution)/shard_map/ppermute | solution.py:235
  64.1 2.0 %collective-permute-start.19 = (f32[2,1024]{1,0:T(2,128)S(1)}, f32[2,1024]{1,0:T(2,128)S(1)}, u32[]{:S(2)}, u32[]{:S(2)}) collective-permute-start(f32[2,1024]{1,0:T(2,128)S(1)} %slice.27), channel_id=1, source_target_pairs={{0,8},{8,0},{16,24},{24,16},{1,9},{9,1},{17,25},{25,17},{2,10},{10... | collective-permute-start | bytes 24584 | tf_op jit(solution)/shard_map/ppermute | solution.py:235
  66.0 1.7 %collective-permute-done.19 = f32[2,1024]{1,0:T(2,128)S(1)} collective-permute-done((f32[2,1024]{1,0:T(2,128)S(1)}, f32[2,1024]{1,0:T(2,128)S(1)}, u32[]{:S(2)}, u32[]{:S(2)}) %collective-permute-start.19) | collective-permute-done | bytes 8224 | tf_op jit(solution)/shard_map/ppermute | solution.py:235
  67.9 1.2 %collective-permute-done.20 = f32[2,512]{1,0:T(2,128)S(1)} collective-permute-done((f32[2,512]{1,0:T(2,128)S(1)}, f32[2,512]{1,0:T(2,128)S(1)}, u32[]{:S(2)}, u32[]{:S(2)}) %collective-permute-start.20) | collective-permute-done | bytes 4128 | tf_op jit(solution)/shard_map/ppermute | solution.py:333
  69.0 0.6 slice_add_fusion.1
  (36 shorter events, 1.3 us)
Async XLA Ops:
  0.0 2.1 %copy-start.3 = (f32[2,512]{1,0:T(2,128)S(1)}, f32[2,512]{1,0:T(2,128)}, u32[]{:S(2)}) copy-start(f32[2,512]{1,0:T(2,128)} %param.6) | copy-start | bytes 12292
  1.6 11.7 %collective-permute-start = (bf16[2,1024,512]{2,1,0:T(8,128)(2,1)S(1)}, bf16[2,1024,512]{2,1,0:T(8,128)(2,1)S(1)}, u32[]{:S(2)}, u32[]{:S(2)}) collective-permute-start(bf16[2,1024,512]{2,1,0:T(8,128)(2,1)S(1)} %shard_map.55), channel_id=1, source_target_pairs={{0,1},{1,0},{2,3},{3,2},{4,5},{5,4},{6,7},{7,6},{8,9},{9,8},{10,11... | collective-permute-start | bytes 6291464 | tf_op jit(solution)/shard_map/ppermute | solution.py:249
  2.1 4.2 %collective-permute-start.1 = (f32[2,512]{1,0:T(2,128)S(1)}, f32[2,512]{1,0:T(2,128)S(1)}, u32[]{:S(2)}, u32[]{:S(2)}) collective-permute-start(f32[2,512]{1,0:T(2,128)S(1)} %copy-done.3), channel_id=1, source_target_pairs={{0,8},{8,0},{16,24},{24,16},{1,9},{9,1},{17,25},{25,17},{2,10},{10... | collective-permute-start | bytes 12296 | tf_op jit(solution)/shard_map/ppermute | solution.py:235
  6.4 4.7 %collective-permute-start.2 = (f32[4,512]{1,0:T(4,128)S(1)}, f32[4,512]{1,0:T(4,128)S(1)}, u32[]{:S(2)}, u32[]{:S(2)}) collective-permute-start(f32[4,512]{1,0:T(4,128)S(1)} %pad_maximum_fusion.2), channel_id=1, source_target_pairs={{0,16},{8,24},{16,0},{24,8},{1,17},{9,25},{17,1},{25,9},{2,18},{10... | collective-permute-start | bytes 24584 | tf_op jit(solution)/shard_map/ppermute | solution.py:235
  11.1 1.7 %copy-start = (f32[2,1024]{1,0:T(2,128)S(1)}, f32[2,1024]{1,0:T(2,128)}, u32[]{:S(2)}) copy-start(f32[2,1024]{1,0:T(2,128)} %amp_ref.1) | copy-start | bytes 24580
  11.1 1.7 %copy-start.1 = (s32[16,16]{1,0:T(8,128)S(1)}, s32[16,16]{1,0:T(8,128)}, u32[]{:S(2)}) copy-start(s32[16,16]{1,0:T(8,128)} %mask_ref.1) | copy-start | bytes 3076
  11.2 2.2 %copy-start.2 = (f32[2,8]{1,0:T(2,128)S(1)}, f32[2,8]{1,0:T(2,128)}, u32[]{:S(2)}) copy-start(f32[2,8]{1,0:T(2,128)} %basis_ref.1) | copy-start | bytes 196
  11.2 2.1 %collective-permute-start.3 = (f32[8,512]{1,0:T(8,128)S(1)}, f32[8,512]{1,0:T(8,128)S(1)}, u32[]{:S(2)}, u32[]{:S(2)}) collective-permute-start(f32[8,512]{1,0:T(8,128)S(1)} %pad_maximum_fusion.1), channel_id=1, source_target_pairs={{0,1},{1,0},{2,3},{3,2},{4,5},{5,4},{6,7},{7,6},{8,9},{9,8},{10,11... | collective-permute-start | bytes 49160 | tf_op jit(solution)/shard_map/ppermute | solution.py:254
  17.9 13.6 %collective-permute-start.9 = (bf16[256,512]{1,0:T(8,128)(2,1)S(1)}, bf16[256,512]{1,0:T(8,128)(2,1)S(1)}, u32[]{:S(2)}, u32[]{:S(2)}) collective-permute-start(bf16[256,512]{1,0:T(8,128)(2,1)S(1)} %shard_map.66), channel_id=1, source_target_pairs={{0,2},{1,5},{2,0},{3,7},{4,6},{5,1},{6,4},{7,3},{8,10},{9,13},{10,... | collective-permute-start | bytes 786440 | tf_op jit(solution)/shard_map/ppermute | solution.py:232
  19.8 6.0 %collective-permute-start.5 = (bf16[256,256]{1,0:T(8,128)(2,1)S(1)}, bf16[256,256]{1,0:T(8,128)(2,1)S(1)}, u32[]{:S(2)}, u32[]{:S(2)}) collective-permute-start(bf16[256,256]{1,0:T(8,128)(2,1)S(1)} %shard_map.61), channel_id=1, source_target_pairs={{0,2},{1,5},{2,0},{3,7},{4,6},{5,1},{6,4},{7,3},{8,10},{9,13},{10,... | collective-permute-start | bytes 393224 | tf_op jit(solution)/shard_map/ppermute | solution.py:232
  20.0 7.2 %collective-permute-start.6 = (bf16[256,256]{1,0:T(8,128)(2,1)S(1)}, bf16[256,256]{1,0:T(8,128)(2,1)S(1)}, u32[]{:S(2)}, u32[]{:S(2)}) collective-permute-start(bf16[256,256]{1,0:T(8,128)(2,1)S(1)} %shard_map.62), channel_id=1, source_target_pairs={{0,2},{1,5},{2,0},{3,7},{4,6},{5,1},{6,4},{7,3},{8,10},{9,13},{10,... | collective-permute-start | bytes 393224 | tf_op jit(solution)/shard_map/ppermute | solution.py:232
  22.9 9.2 %collective-permute-start.4 = (bf16[256,512]{1,0:T(8,128)(2,1)S(1)}, bf16[256,512]{1,0:T(8,128)(2,1)S(1)}, u32[]{:S(2)}, u32[]{:S(2)}) collective-permute-start(bf16[256,512]{1,0:T(8,128)(2,1)S(1)} %shard_map.59), channel_id=1, source_target_pairs={{0,2},{1,5},{2,0},{3,7},{4,6},{5,1},{6,4},{7,3},{8,10},{9,13},{10,... | collective-permute-start | bytes 786440 | tf_op jit(solution)/shard_map/ppermute | solution.py:232
  27.2 8.2 %collective-permute-start.7 = (bf16[256,512]{1,0:T(8,128)(2,1)S(1)}, bf16[256,512]{1,0:T(8,128)(2,1)S(1)}, u32[]{:S(2)}, u32[]{:S(2)}) collective-permute-start(bf16[256,512]{1,0:T(8,128)(2,1)S(1)} %add_convert_fusion.1), channel_id=1, source_target_pairs={{0,4},{1,3},{2,6},{3,1},{4,0},{5,7},{6,2},{7,5},{8,12},{9,11},{10,... | collective-permute-start | bytes 786440 | tf_op jit(solution)/shard_map/ppermute | solution.py:232
  29.9 9.9 %collective-permute-start.8 = (bf16[256,512]{1,0:T(8,128)(2,1)S(1)}, bf16[256,512]{1,0:T(8,128)(2,1)S(1)}, u32[]{:S(2)}, u32[]{:S(2)}) collective-permute-start(bf16[256,512]{1,0:T(8,128)(2,1)S(1)} %shard_map.65), channel_id=1, source_target_pairs={{0,2},{1,5},{2,0},{3,7},{4,6},{5,1},{6,4},{7,3},{8,10},{9,13},{10,... | collective-permute-start | bytes 786440 | tf_op jit(solution)/shard_map/ppermute | solution.py:232
  31.5 9.4 %collective-permute-start.10 = (bf16[256,512]{1,0:T(8,128)(2,1)S(1)}, bf16[256,512]{1,0:T(8,128)(2,1)S(1)}, u32[]{:S(2)}, u32[]{:S(2)}) collective-permute-start(bf16[256,512]{1,0:T(8,128)(2,1)S(1)} %add_convert_fusion), channel_id=1, source_target_pairs={{0,4},{1,3},{2,6},{3,1},{4,0},{5,7},{6,2},{7,5},{8,12},{9,11},{10,... | collective-permute-start | bytes 786440 | tf_op jit(solution)/shard_map/ppermute | solution.py:232
  35.6 11.4 %collective-permute-start.11 = (bf16[256,512]{1,0:T(8,128)(2,1)S(1)}, bf16[256,512]{1,0:T(8,128)(2,1)S(1)}, u32[]{:S(2)}, u32[]{:S(2)}) collective-permute-start(bf16[256,512]{1,0:T(8,128)(2,1)S(1)} %multiply_convert_fusion.1.resid_ref), channel_id=1, source_target_pairs={{0,4},{1,3},{2,6},{3,1},{4,0},{5,7},{6,2},{7,5},{8,12},{9,11},{10,... | collective-permute-start | bytes 786440 | tf_op jit(solution)/shard_map/ppermute | solution.py:232
  37.8 11.3 %collective-permute-start.13 = (bf16[256,512]{1,0:T(8,128)(2,1)S(1)}, bf16[256,512]{1,0:T(8,128)(2,1)S(1)}, u32[]{:S(2)}, u32[]{:S(2)}) collective-permute-start(bf16[256,512]{1,0:T(8,128)(2,1)S(1)} %multiply_convert_fusion.1.resid_ref), channel_id=1, source_target_pairs={{0,2},{1,5},{2,0},{3,7},{4,6},{5,1},{6,4},{7,3},{8,10},{9,13},{10,... | collective-permute-start | bytes 786440 | tf_op jit(solution)/shard_map/ppermute | solution.py:232
  41.1 10.4 %collective-permute-start.12 = (bf16[256,512]{1,0:T(8,128)(2,1)S(1)}, bf16[256,512]{1,0:T(8,128)(2,1)S(1)}, u32[]{:S(2)}, u32[]{:S(2)}) collective-permute-start(bf16[256,512]{1,0:T(8,128)(2,1)S(1)} %multiply_convert_fusion.resid_ref), channel_id=1, source_target_pairs={{0,4},{1,3},{2,6},{3,1},{4,0},{5,7},{6,2},{7,5},{8,12},{9,11},{10,... | collective-permute-start | bytes 786440 | tf_op jit(solution)/shard_map/ppermute | solution.py:232
  44.3 10.6 %collective-permute-start.14 = (bf16[256,512]{1,0:T(8,128)(2,1)S(1)}, bf16[256,512]{1,0:T(8,128)(2,1)S(1)}, u32[]{:S(2)}, u32[]{:S(2)}) collective-permute-start(bf16[256,512]{1,0:T(8,128)(2,1)S(1)} %multiply_convert_fusion.resid_ref), channel_id=1, source_target_pairs={{0,2},{1,5},{2,0},{3,7},{4,6},{5,1},{6,4},{7,3},{8,10},{9,13},{10,... | collective-permute-start | bytes 786440 | tf_op jit(solution)/shard_map/ppermute | solution.py:232
  47.0 9.0 %collective-permute-start.15 = (bf16[256,512]{1,0:T(8,128)(2,1)S(1)}, bf16[256,512]{1,0:T(8,128)(2,1)S(1)}, u32[]{:S(2)}, u32[]{:S(2)}) collective-permute-start(bf16[256,512]{1,0:T(8,128)(2,1)S(1)} %collective-permute-done.11.resid_ref), channel_id=1, source_target_pairs={{0,2},{1,5},{2,0},{3,7},{4,6},{5,1},{6,4},{7,3},{8,10},{9,13},{10,... | collective-permute-start | bytes 786440 | tf_op jit(solution)/shard_map/ppermute | solution.py:232
  51.6 5.6 %collective-permute-start.16 = (bf16[256,256]{1,0:T(8,128)(2,1)S(1)}, bf16[256,256]{1,0:T(8,128)(2,1)S(1)}, u32[]{:S(2)}, u32[]{:S(2)}) collective-permute-start(bf16[256,256]{1,0:T(8,128)(2,1)S(1)} %get-tuple-element.26), channel_id=1, source_target_pairs={{0,2},{1,5},{2,0},{3,7},{4,6},{5,1},{6,4},{7,3},{8,10},{9,13},{10,... | collective-permute-start | bytes 393224 | tf_op jit(solution)/shard_map/ppermute | solution.py:232
  53.7 5.0 %collective-permute-start.17 = (bf16[256,256]{1,0:T(8,128)(2,1)S(1)}, bf16[256,256]{1,0:T(8,128)(2,1)S(1)}, u32[]{:S(2)}, u32[]{:S(2)}) collective-permute-start(bf16[256,256]{1,0:T(8,128)(2,1)S(1)} %get-tuple-element.25), channel_id=1, source_target_pairs={{0,2},{1,5},{2,0},{3,7},{4,6},{5,1},{6,4},{7,3},{8,10},{9,13},{10,... | collective-permute-start | bytes 393224 | tf_op jit(solution)/shard_map/ppermute | solution.py:232
  59.2 4.8 %collective-permute-start.18 = (f32[4,1024]{1,0:T(4,128)S(1)}, f32[4,1024]{1,0:T(4,128)S(1)}, u32[]{:S(2)}, u32[]{:S(2)}) collective-permute-start(f32[4,1024]{1,0:T(4,128)S(1)} %get-tuple-element.24), channel_id=1, source_target_pairs={{0,16},{8,24},{16,0},{24,8},{1,17},{9,25},{17,1},{25,9},{2,18},{10... | collective-permute-start | bytes 49160 | tf_op jit(solution)/shard_map/ppermute | solution.py:235
  64.1 3.7 %collective-permute-start.19 = (f32[2,1024]{1,0:T(2,128)S(1)}, f32[2,1024]{1,0:T(2,128)S(1)}, u32[]{:S(2)}, u32[]{:S(2)}) collective-permute-start(f32[2,1024]{1,0:T(2,128)S(1)} %slice.27), channel_id=1, source_target_pairs={{0,8},{8,0},{16,24},{24,16},{1,9},{9,1},{17,25},{25,17},{2,10},{10... | collective-permute-start | bytes 24584 | tf_op jit(solution)/shard_map/ppermute | solution.py:235
  67.8 1.2 %collective-permute-start.20 = (f32[2,512]{1,0:T(2,128)S(1)}, f32[2,512]{1,0:T(2,128)S(1)}, u32[]{:S(2)}, u32[]{:S(2)}) collective-permute-start(f32[2,512]{1,0:T(2,128)S(1)} %slice.29), channel_id=1, source_target_pairs={{0,1},{1,0},{2,3},{3,2},{4,5},{5,4},{6,7},{7,6},{8,9},{9,8},{10,11... | collective-permute-start | bytes 12296 | tf_op jit(solution)/shard_map/ppermute | solution.py:333

commit v6 on v5

--- a/solution.py
+++ b/solution.py
@@ -300,14 +300,16 @@
     resid = {(0, u): (held[0, u] * weight[u]).astype(BF16) for u in (0, 1)}
 
     order, parts = [0], {"0": halves[0], "1": halves[1], "c": halves[1][: n // 4], "d": halves[1][n // 4 :]}
+    cut = n // 4 * tile
+    ends = {(0, "c"): resid[0, 1][:, :cut], (0, "d"): resid[0, 1][:, cut:]}
     for j in reversed(range(bits)):
         for q in list(order):
             order.append(q | (1 << j))
             for u in (0, 1):
-                if (order[-1], u) == (n - 1, 1):
-                    cut = n // 4 * tile
-                    resid[n - 1, "c"] = swap_chip(resid[q, u][:, :cut], j)
-                    resid[n - 1, "d"] = swap_chip(resid[q, u][:, cut:], j)
+                if u == 1 and order[-1] >= n // 2:
+                    for k in "cd":
+                        resid[order[-1], k] = swap_chip(ends[q, k], j)
+                        ends[order[-1], k] = resid[order[-1], k]
                 else:
                     resid[order[-1], u] = swap_chip(resid[q, u], j)
     step = min(512, width // 2)

time: 69.8 us -> 70.3 us (level)
  starting transfers between devices: 30.8 us -> 33 us
  waiting for transfers between devices: 17 us -> 15 us
    ppermute x14 -> x15, waiting for transfers between devices: 9.13 us -> 7.29 us  [swap_chip(): return lax.ppermute(value, 'cell', pairs)]
    ppermute x14 -> x15, starting transfers between devices: 19.3 us -> 21.1 us  [swap_chip(): return lax.ppermute(value, 'cell', pairs)]
    pallas_call x20 -> x21, Pallas kernels: 20.3 us -> 20.5 us  [call(): pl.pallas_call(kernel, out_shape=out_shape, in_specs=specs, out_specs=[VM...]
  transfers between devices with their start and end apart: 21 -> 22, of which waited for: 11 -> 10; matrix products, arithmetic and copies ran while one was open for 1% -> 1% of each run, Pallas kernels for 20% -> 20%
where the time goes in v6:
time: 70.3 us; the launch traced here: 70.1 us
  starting transfers between devices  33 us (47%)
  Pallas kernels  20.5 us (29%)
  waiting for transfers between devices  15 us (21%)
  other arithmetic  1.11 us (2%)
    ppermute x15, starting transfers between devices, swap_chip(): return lax.ppermute(value, 'cell', pairs)  21.1 us
    pallas_call x21, Pallas kernels, call(): pl.pallas_call(kernel, out_shape=out_shape, in_specs=specs, out_specs=[VM...  20.5 us
    ppermute x4, starting transfers between devices, swap_plane(): return lax.ppermute(value, 'freq', [(i, i ^ 1 << j) for i in range(n_freq)])  11.2 us
    ppermute x15, waiting for transfers between devices, swap_chip(): return lax.ppermute(value, 'cell', pairs)  7.29 us
    ppermute x4, waiting for transfers between devices, swap_plane(): return lax.ppermute(value, 'freq', [(i, i ^ 1 << j) for i in range(n_freq)])  6.6 us
  transfers between devices with their start and end apart: 22, of which 10 were waited for; matrix products, arithmetic and copies ran while one was open for 1% of the time, Pallas kernels for 20%

profile of v6, /device:TPU:0, one launch (start us, length us, event | category | flops | bytes accessed | tf_op | source)
XLA Modules:
  0.0 70.1 jit_solution(7065505011862105132)
XLA Ops:
  0.0 1.6 %shard_map.55 = bf16[2,1024,512]{2,1,0:T(8,128)(2,1)S(1)} custom-call(s32[1]{0:T(128)} %bitcast.1.core_ref, bf16[2,2,1024,512]{3,2,1,0:T(8,128)(2,1)} %green_ref.3, s32[1]{0:T(128)} %bitcast.2.rest_0_.plane_ref, s32[1]{0:T(128)} %bitcast.3.rest_1_.piece_ref, s32[1]{0:T(128)} %bitcast.4.rest_2_.piece_ref, s32[1]{0:T(128)} %bitcast.5.rest_3_.piece_ref, ...), custom_call_target="tpu_custom_call" | custom-call | bytes 4194304 | tf_op jit(solution)/shard_map/pallas_call | solution.py:200
  1.6 0.6 collective-permute-start
  2.1 2.6 %collective-permute-start.1 = (f32[2,512]{1,0:T(2,128)S(1)}, f32[2,512]{1,0:T(2,128)S(1)}, u32[]{:S(2)}, u32[]{:S(2)}) collective-permute-start(f32[2,512]{1,0:T(2,128)S(1)} %copy-done.3), channel_id=1, source_target_pairs={{0,8},{8,0},{16,24},{24,16},{1,9},{9,1},{17,25},{25,17},{2,10},{10... | collective-permute-start | bytes 12296 | tf_op jit(solution)/shard_map/ppermute | solution.py:235
  4.8 1.6 %collective-permute-done.1 = f32[2,512]{1,0:T(2,128)S(1)} collective-permute-done((f32[2,512]{1,0:T(2,128)S(1)}, f32[2,512]{1,0:T(2,128)S(1)}, u32[]{:S(2)}, u32[]{:S(2)}) %collective-permute-start.1) | collective-permute-done | bytes 4128 | tf_op jit(solution)/shard_map/ppermute | solution.py:235
  6.4 3.1 %collective-permute-start.2 = (f32[4,512]{1,0:T(4,128)S(1)}, f32[4,512]{1,0:T(4,128)S(1)}, u32[]{:S(2)}, u32[]{:S(2)}) collective-permute-start(f32[4,512]{1,0:T(4,128)S(1)} %pad_maximum_fusion.2), channel_id=1, source_target_pairs={{0,16},{8,24},{16,0},{24,8},{1,17},{9,25},{17,1},{25,9},{2,18},{10... | collective-permute-start | bytes 24584 | tf_op jit(solution)/shard_map/ppermute | solution.py:235
  9.5 1.6 %collective-permute-done.2 = f32[4,512]{1,0:T(4,128)S(1)} collective-permute-done((f32[4,512]{1,0:T(4,128)S(1)}, f32[4,512]{1,0:T(4,128)S(1)}, u32[]{:S(2)}, u32[]{:S(2)}) %collective-permute-start.2) | collective-permute-done | bytes 8224 | tf_op jit(solution)/shard_map/ppermute | solution.py:235
  11.2 1.6 %shard_map.56.field_ref = bf16[1024,2048]{1,0:T(8,128)(2,1)S(1)} custom-call(s32[1]{0:T(128)} %bitcast.1.core_ref, bf16[2,2,1024,512]{3,2,1,0:T(8,128)(2,1)} %green_ref.3), custom_call_target="tpu_custom_call" | custom-call | bytes 4194304 | tf_op jit(solution)/shard_map/pallas_call | solution.py:200
  12.8 0.4 shard_map.63
  13.3 0.9 %shard_map.57 = (bf16[1024,2048]{1,0:T(8,128)(2,1)S(1)}, f32[8,128]{1,0:T(8,128)S(1)}) custom-call(s32[1]{0:T(128)} %bitcast.1.core_ref, s32[1]{0:T(128)} %bitcast.2.rest_0_.plane_ref, f32[2,8]{1,0:T(2,128)S(1)} %copy-done.2, bf16[2,1024,512]{2,1,0:T(8,128)(2,1)S(1)} %collective-permute-done.theirs_ref, ...), custom_call_target="tpu_custom_call", output_to_operand_aliasing={{0}: (4, {})} | custom-call | bytes 4194304 | tf_op jit(solution)/shard_map/pallas_call | solution.py:200
  14.2 1.6 %shard_map.58 = (f32[256,512]{1,0:T(8,128)S(1)}, f32[256,512]{1,0:T(8,128)S(1)}) custom-call(s32[1]{0:T(128)} %bitcast.3.rest_1_.piece_ref, f32[8,128]{1,0:T(8,128)S(1)} %get-tuple-element.15.column_ref, f32[8,1024]{1,0:T(8,128)S(1)} %pad_maximum_fusion.known_ref, bf16[1024,2048]{1,0:T(8,128)(2,1)S(1)} %get-tuple-element.16.green_ref), custom_call_target="tpu_custom_call" | custom-call | flops 1073741824 | bytes 4718592 | tf_op jit(solution)/shard_map/pallas_call | solution.py:200
  15.8 0.8 %shard_map.66 = bf16[256,512]{1,0:T(8,128)(2,1)S(1)} custom-call(s32[1]{0:T(128)} %bitcast.rest_4_.piece_ref, f32[8,128]{1,0:T(8,128)S(1)} %get-tuple-element.15.column_ref, f32[8,1024]{1,0:T(8,128)S(1)} %pad_maximum_fusion.known_ref, bf16[1024,2048]{1,0:T(8,128)(2,1)S(1)} %get-tuple-element.16.green_ref), custom_call_target="tpu_custom_call" | custom-call | flops 536870912 | bytes 4718592 | tf_op jit(solution)/shard_map/pallas_call | solution.py:200
  16.6 0.8 %shard_map.61 = bf16[256,256]{1,0:T(8,128)(2,1)S(1)} custom-call(s32[1]{0:T(128)} %bitcast.rest_4_.piece_ref, f32[8,128]{1,0:T(8,128)S(1)} %get-tuple-element.15.column_ref, f32[8,1024]{1,0:T(8,128)S(1)} %pad_maximum_fusion.known_ref, bf16[1024,2048]{1,0:T(8,128)(2,1)S(1)} %get-tuple-element.16.green_ref), custom_call_target="tpu_custom_call" | custom-call | flops 268435456 | bytes 4718592 | tf_op jit(solution)/shard_map/pallas_call | solution.py:200
  17.4 0.5 shard_map.62
  17.9 1.9 %collective-permute-start.9 = (bf16[256,512]{1,0:T(8,128)(2,1)S(1)}, bf16[256,512]{1,0:T(8,128)(2,1)S(1)}, u32[]{:S(2)}, u32[]{:S(2)}) collective-permute-start(bf16[256,512]{1,0:T(8,128)(2,1)S(1)} %shard_map.66), channel_id=1, source_target_pairs={{0,2},{1,5},{2,0},{3,7},{4,6},{5,1},{6,4},{7,3},{8,10},{9,13},{10,... | collective-permute-start | bytes 786440 | tf_op jit(solution)/shard_map/ppermute | solution.py:232
  20.0 1.8 %collective-permute-start.6 = (bf16[256,256]{1,0:T(8,128)(2,1)S(1)}, bf16[256,256]{1,0:T(8,128)(2,1)S(1)}, u32[]{:S(2)}, u32[]{:S(2)}) collective-permute-start(bf16[256,256]{1,0:T(8,128)(2,1)S(1)} %shard_map.62), channel_id=1, source_target_pairs={{0,2},{1,5},{2,0},{3,7},{4,6},{5,1},{6,4},{7,3},{8,10},{9,13},{10,... | collective-permute-start | bytes 393224 | tf_op jit(solution)/shard_map/ppermute | solution.py:232
  21.8 1.0 %shard_map.59 = bf16[256,512]{1,0:T(8,128)(2,1)S(1)} custom-call(s32[1]{0:T(128)} %bitcast.4.rest_2_.piece_ref, f32[8,128]{1,0:T(8,128)S(1)} %get-tuple-element.15.column_ref, f32[8,1024]{1,0:T(8,128)S(1)} %pad_maximum_fusion.known_ref, bf16[1024,2048]{1,0:T(8,128)(2,1)S(1)} %get-tuple-element.16.green_ref), custom_call_target="tpu_custom_call" | custom-call | flops 536870912 | bytes 4718592 | tf_op jit(solution)/shard_map/pallas_call | solution.py:200
  23.1 1.6 %shard_map.60 = (f32[256,512]{1,0:T(8,128)S(1)}, f32[256,512]{1,0:T(8,128)S(1)}) custom-call(s32[1]{0:T(128)} %bitcast.5.rest_3_.piece_ref, f32[8,128]{1,0:T(8,128)S(1)} %get-tuple-element.15.column_ref, f32[8,1024]{1,0:T(8,128)S(1)} %pad_maximum_fusion.known_ref, bf16[1024,2048]{1,0:T(8,128)(2,1)S(1)} %get-tuple-element.16.green_ref), custom_call_target="tpu_custom_call" | custom-call | flops 1073741824 | bytes 4718592 | tf_op jit(solution)/shard_map/pallas_call | solution.py:200
  24.7 1.0 %collective-permute-done.5 = bf16[256,256]{1,0:T(8,128)(2,1)S(1)} collective-permute-done((bf16[256,256]{1,0:T(8,128)(2,1)S(1)}, bf16[256,256]{1,0:T(8,128)(2,1)S(1)}, u32[]{:S(2)}, u32[]{:S(2)}) %collective-permute-start.5) | collective-permute-done | bytes 131104 | tf_op jit(solution)/shard_map/ppermute | solution.py:232
  25.7 1.4 %collective-permute-done.6 = bf16[256,256]{1,0:T(8,128)(2,1)S(1)} collective-permute-done((bf16[256,256]{1,0:T(8,128)(2,1)S(1)}, bf16[256,256]{1,0:T(8,128)(2,1)S(1)}, u32[]{:S(2)}, u32[]{:S(2)}) %collective-permute-start.6) | collective-permute-done | bytes 131104 | tf_op jit(solution)/shard_map/ppermute | solution.py:232
  27.2 1.9 %collective-permute-start.7 = (bf16[256,512]{1,0:T(8,128)(2,1)S(1)}, bf16[256,512]{1,0:T(8,128)(2,1)S(1)}, u32[]{:S(2)}, u32[]{:S(2)}) collective-permute-start(bf16[256,512]{1,0:T(8,128)(2,1)S(1)} %add_convert_fusion.1), channel_id=1, source_target_pairs={{0,4},{1,3},{2,6},{3,1},{4,0},{5,7},{6,2},{7,5},{8,12},{9,11},{10,... | collective-permute-start | bytes 786440 | tf_op jit(solution)/shard_map/ppermute | solution.py:232
  29.1 0.8 %shard_map.65 = bf16[256,512]{1,0:T(8,128)(2,1)S(1)} custom-call(s32[1]{0:T(128)} %bitcast.4.rest_2_.piece_ref, f32[8,128]{1,0:T(8,128)S(1)} %get-tuple-element.15.column_ref, f32[8,1024]{1,0:T(8,128)S(1)} %pad_maximum_fusion.known_ref, bf16[1024,2048]{1,0:T(8,128)(2,1)S(1)} %get-tuple-element.16.green_ref), custom_call_target="tpu_custom_call" | custom-call | flops 536870912 | bytes 4718592 | tf_op jit(solution)/shard_map/pallas_call | solution.py:200
  29.9 1.6 %collective-permute-start.8 = (bf16[256,512]{1,0:T(8,128)(2,1)S(1)}, bf16[256,512]{1,0:T(8,128)(2,1)S(1)}, u32[]{:S(2)}, u32[]{:S(2)}) collective-permute-start(bf16[256,512]{1,0:T(8,128)(2,1)S(1)} %shard_map.65), channel_id=1, source_target_pairs={{0,2},{1,5},{2,0},{3,7},{4,6},{5,1},{6,4},{7,3},{8,10},{9,13},{10,... | collective-permute-start | bytes 786440 | tf_op jit(solution)/shard_map/ppermute | solution.py:232
  31.5 0.6 collective-permute-start.10
  32.1 3.3 %collective-permute-done.7 = bf16[256,512]{1,0:T(8,128)(2,1)S(1)} collective-permute-done((bf16[256,512]{1,0:T(8,128)(2,1)S(1)}, bf16[256,512]{1,0:T(8,128)(2,1)S(1)}, u32[]{:S(2)}, u32[]{:S(2)}) %collective-permute-start.7) | collective-permute-done | bytes 262176 | tf_op jit(solution)/shard_map/ppermute | solution.py:232
  35.6 2.3 %collective-permute-start.11 = (bf16[256,512]{1,0:T(8,128)(2,1)S(1)}, bf16[256,512]{1,0:T(8,128)(2,1)S(1)}, u32[]{:S(2)}, u32[]{:S(2)}) collective-permute-start(bf16[256,512]{1,0:T(8,128)(2,1)S(1)} %multiply_convert_fusion.1.resid_ref), channel_id=1, source_target_pairs={{0,4},{1,3},{2,6},{3,1},{4,0},{5,7},{6,2},{7,5},{8,12},{9,11},{10,... | collective-permute-start | bytes 786440 | tf_op jit(solution)/shard_map/ppermute | solution.py:232
  37.8 2.0 %collective-permute-start.14 = (bf16[256,512]{1,0:T(8,128)(2,1)S(1)}, bf16[256,512]{1,0:T(8,128)(2,1)S(1)}, u32[]{:S(2)}, u32[]{:S(2)}) collective-permute-start(bf16[256,512]{1,0:T(8,128)(2,1)S(1)} %multiply_convert_fusion.1.resid_ref), channel_id=1, source_target_pairs={{0,2},{1,5},{2,0},{3,7},{4,6},{5,1},{6,4},{7,3},{8,10},{9,13},{10,... | collective-permute-start | bytes 786440 | tf_op jit(solution)/shard_map/ppermute | solution.py:232
  39.8 1.2 %collective-permute-done.10 = bf16[256,512]{1,0:T(8,128)(2,1)S(1)} collective-permute-done((bf16[256,512]{1,0:T(8,128)(2,1)S(1)}, bf16[256,512]{1,0:T(8,128)(2,1)S(1)}, u32[]{:S(2)}, u32[]{:S(2)}) %collective-permute-start.10) | collective-permute-done | bytes 262176 | tf_op jit(solution)/shard_map/ppermute | solution.py:232
  41.1 2.0 %collective-permute-start.12 = (bf16[256,256]{1,0:T(8,128)(2,1)S(1)}, bf16[256,256]{1,0:T(8,128)(2,1)S(1)}, u32[]{:S(2)}, u32[]{:S(2)}) collective-permute-start(bf16[256,256]{1,0:T(8,128)(2,1)S(1)} %get-tuple-element.26), channel_id=1, source_target_pairs={{0,4},{1,3},{2,6},{3,1},{4,0},{5,7},{6,2},{7,5},{8,12},{9,11},{10,... | collective-permute-start | bytes 393224 | tf_op jit(solution)/shard_map/ppermute | solution.py:232
  43.2 1.6 %collective-permute-start.15 = (bf16[256,512]{1,0:T(8,128)(2,1)S(1)}, bf16[256,512]{1,0:T(8,128)(2,1)S(1)}, u32[]{:S(2)}, u32[]{:S(2)}) collective-permute-start(bf16[256,512]{1,0:T(8,128)(2,1)S(1)} %multiply_convert_fusion.resid_ref), channel_id=1, source_target_pairs={{0,2},{1,5},{2,0},{3,7},{4,6},{5,1},{6,4},{7,3},{8,10},{9,13},{10,... | collective-permute-start | bytes 786440 | tf_op jit(solution)/shard_map/ppermute | solution.py:232
  45.1 1.1 %shard_map.64 = f32[1,1024]{1,0:T(1,128)S(1)} custom-call(s32[1]{0:T(128)} %bitcast.3.rest_1_.piece_ref, bf16[256,512]{1,0:T(8,128)(2,1)S(1)} %multiply_convert_fusion.1.resid_ref, bf16[1024,2048]{1,0:T(8,128)(2,1)S(1)} %get-tuple-element.16.green_ref), custom_call_target="tpu_custom_call" | custom-call | flops 536870912 | bytes 4718592 | tf_op jit(solution)/shard_map/pallas_call | solution.py:200
  46.6 1.8 %collective-permute-start.16 = (bf16[256,512]{1,0:T(8,128)(2,1)S(1)}, bf16[256,512]{1,0:T(8,128)(2,1)S(1)}, u32[]{:S(2)}, u32[]{:S(2)}) collective-permute-start(bf16[256,512]{1,0:T(8,128)(2,1)S(1)} %collective-permute-done.11.resid_ref), channel_id=1, source_target_pairs={{0,2},{1,5},{2,0},{3,7},{4,6},{5,1},{6,4},{7,3},{8,10},{9,13},{10,... | collective-permute-start | bytes 786440 | tf_op jit(solution)/shard_map/ppermute | solution.py:232
  48.4 1.0 %shard_map.67 = f32[1,1024]{1,0:T(1,128)S(1)} custom-call(s32[1]{0:T(128)} %bitcast.3.rest_1_.piece_ref, bf16[256,512]{1,0:T(8,128)(2,1)S(1)} %multiply_convert_fusion.resid_ref, bf16[1024,2048]{1,0:T(8,128)(2,1)S(1)} %get-tuple-element.16.green_ref), custom_call_target="tpu_custom_call" | custom-call | flops 536870912 | bytes 4718592 | tf_op jit(solution)/shard_map/pallas_call | solution.py:200
  49.4 1.8 %collective-permute-start.17 = (bf16[256,256]{1,0:T(8,128)(2,1)S(1)}, bf16[256,256]{1,0:T(8,128)(2,1)S(1)}, u32[]{:S(2)}, u32[]{:S(2)}) collective-permute-start(bf16[256,256]{1,0:T(8,128)(2,1)S(1)} %collective-permute-done.12.resid_ref), channel_id=1, source_target_pairs={{0,2},{1,5},{2,0},{3,7},{4,6},{5,1},{6,4},{7,3},{8,10},{9,13},{10,... | collective-permute-start | bytes 393224 | tf_op jit(solution)/shard_map/ppermute | solution.py:232
  51.2 1.1 %shard_map.68 = f32[1,1024]{1,0:T(1,128)S(1)} custom-call(s32[1]{0:T(128)} %bitcast.5.rest_3_.piece_ref, bf16[256,512]{1,0:T(8,128)(2,1)S(1)} %collective-permute-done.11.resid_ref, bf16[1024,2048]{1,0:T(8,128)(2,1)S(1)} %get-tuple-element.16.green_ref), custom_call_target="tpu_custom_call" | custom-call | flops 536870912 | bytes 4718592 | tf_op jit(solution)/shard_map/pallas_call | solution.py:200
  52.4 0.6 shard_map.69
  52.9 1.1 %collective-permute-start.18 = (bf16[256,256]{1,0:T(8,128)(2,1)S(1)}, bf16[256,256]{1,0:T(8,128)(2,1)S(1)}, u32[]{:S(2)}, u32[]{:S(2)}) collective-permute-start(bf16[256,256]{1,0:T(8,128)(2,1)S(1)} %collective-permute-done.13.resid_ref), channel_id=1, source_target_pairs={{0,2},{1,5},{2,0},{3,7},{4,6},{5,1},{6,4},{7,3},{8,10},{9,13},{10,... | collective-permute-start | bytes 393224 | tf_op jit(solution)/shard_map/ppermute | solution.py:232
  54.0 0.6 shard_map.70
  54.6 1.4 %shard_map.71 = f32[1,1024]{1,0:T(1,128)S(1)} custom-call(s32[1]{0:T(128)} %bitcast.4.rest_2_.piece_ref, bf16[256,512]{1,0:T(8,128)(2,1)S(1)} %collective-permute-done.14.resid_ref, bf16[1024,2048]{1,0:T(8,128)(2,1)S(1)} %get-tuple-element.16.green_ref), custom_call_target="tpu_custom_call" | custom-call | flops 536870912 | bytes 4718592 | tf_op jit(solution)/shard_map/pallas_call | solution.py:200
  56.0 1.0 %shard_map.72 = f32[1,1024]{1,0:T(1,128)S(1)} custom-call(s32[1]{0:T(128)} %bitcast.4.rest_2_.piece_ref, bf16[256,512]{1,0:T(8,128)(2,1)S(1)} %collective-permute-done.15.resid_ref, bf16[1024,2048]{1,0:T(8,128)(2,1)S(1)} %get-tuple-element.16.green_ref), custom_call_target="tpu_custom_call" | custom-call | flops 536870912 | bytes 4718592 | tf_op jit(solution)/shard_map/pallas_call | solution.py:200
  57.0 0.5 shard_map.74
  57.6 1.2 %shard_map.73 = f32[1,1024]{1,0:T(1,128)S(1)} custom-call(s32[1]{0:T(128)} %bitcast.rest_4_.piece_ref, bf16[256,512]{1,0:T(8,128)(2,1)S(1)} %collective-permute-done.16.resid_ref, bf16[1024,2048]{1,0:T(8,128)(2,1)S(1)} %get-tuple-element.16.green_ref), custom_call_target="tpu_custom_call" | custom-call | flops 536870912 | bytes 4718592 | tf_op jit(solution)/shard_map/pallas_call | solution.py:200
  58.8 0.6 shard_map.75
  59.4 3.4 %collective-permute-start.19 = (f32[4,1024]{1,0:T(4,128)S(1)}, f32[4,1024]{1,0:T(4,128)S(1)}, u32[]{:S(2)}, u32[]{:S(2)}) collective-permute-start(f32[4,1024]{1,0:T(4,128)S(1)} %get-tuple-element.24), channel_id=1, source_target_pairs={{0,16},{8,24},{16,0},{24,8},{1,17},{9,25},{17,1},{25,9},{2,18},{10... | collective-permute-start | bytes 49160 | tf_op jit(solution)/shard_map/ppermute | solution.py:235
  62.8 1.7 %collective-permute-done.19 = f32[4,1024]{1,0:T(4,128)S(1)} collective-permute-done((f32[4,1024]{1,0:T(4,128)S(1)}, f32[4,1024]{1,0:T(4,128)S(1)}, u32[]{:S(2)}, u32[]{:S(2)}) %collective-permute-start.19) | collective-permute-done | bytes 16416 | tf_op jit(solution)/shard_map/ppermute | solution.py:235
  64.5 2.1 %collective-permute-start.20 = (f32[2,1024]{1,0:T(2,128)S(1)}, f32[2,1024]{1,0:T(2,128)S(1)}, u32[]{:S(2)}, u32[]{:S(2)}) collective-permute-start(f32[2,1024]{1,0:T(2,128)S(1)} %slice.27), channel_id=1, source_target_pairs={{0,8},{8,0},{16,24},{24,16},{1,9},{9,1},{17,25},{25,17},{2,10},{10... | collective-permute-start | bytes 24584 | tf_op jit(solution)/shard_map/ppermute | solution.py:235
  66.6 1.7 %collective-permute-done.20 = f32[2,1024]{1,0:T(2,128)S(1)} collective-permute-done((f32[2,1024]{1,0:T(2,128)S(1)}, f32[2,1024]{1,0:T(2,128)S(1)}, u32[]{:S(2)}, u32[]{:S(2)}) %collective-permute-start.20) | collective-permute-done | bytes 8224 | tf_op jit(solution)/shard_map/ppermute | solution.py:235
  68.3 1.2 %collective-permute-done.21 = f32[2,512]{1,0:T(2,128)S(1)} collective-permute-done((f32[2,512]{1,0:T(2,128)S(1)}, f32[2,512]{1,0:T(2,128)S(1)}, u32[]{:S(2)}, u32[]{:S(2)}) %collective-permute-start.21) | collective-permute-done | bytes 4128 | tf_op jit(solution)/shard_map/ppermute | solution.py:335
  69.5 0.6 slice_add_fusion.1
  (39 shorter events, 1.8 us)
Async XLA Ops:
  0.0 2.1 %copy-start.3 = (f32[2,512]{1,0:T(2,128)S(1)}, f32[2,512]{1,0:T(2,128)}, u32[]{:S(2)}) copy-start(f32[2,512]{1,0:T(2,128)} %param.6) | copy-start | bytes 12292
  1.6 11.7 %collective-permute-start = (bf16[2,1024,512]{2,1,0:T(8,128)(2,1)S(1)}, bf16[2,1024,512]{2,1,0:T(8,128)(2,1)S(1)}, u32[]{:S(2)}, u32[]{:S(2)}) collective-permute-start(bf16[2,1024,512]{2,1,0:T(8,128)(2,1)S(1)} %shard_map.55), channel_id=1, source_target_pairs={{0,1},{1,0},{2,3},{3,2},{4,5},{5,4},{6,7},{7,6},{8,9},{9,8},{10,11... | collective-permute-start | bytes 6291464 | tf_op jit(solution)/shard_map/ppermute | solution.py:249
  2.1 4.2 %collective-permute-start.1 = (f32[2,512]{1,0:T(2,128)S(1)}, f32[2,512]{1,0:T(2,128)S(1)}, u32[]{:S(2)}, u32[]{:S(2)}) collective-permute-start(f32[2,512]{1,0:T(2,128)S(1)} %copy-done.3), channel_id=1, source_target_pairs={{0,8},{8,0},{16,24},{24,16},{1,9},{9,1},{17,25},{25,17},{2,10},{10... | collective-permute-start | bytes 12296 | tf_op jit(solution)/shard_map/ppermute | solution.py:235
  6.4 4.7 %collective-permute-start.2 = (f32[4,512]{1,0:T(4,128)S(1)}, f32[4,512]{1,0:T(4,128)S(1)}, u32[]{:S(2)}, u32[]{:S(2)}) collective-permute-start(f32[4,512]{1,0:T(4,128)S(1)} %pad_maximum_fusion.2), channel_id=1, source_target_pairs={{0,16},{8,24},{16,0},{24,8},{1,17},{9,25},{17,1},{25,9},{2,18},{10... | collective-permute-start | bytes 24584 | tf_op jit(solution)/shard_map/ppermute | solution.py:235
  11.1 1.7 %copy-start = (f32[2,1024]{1,0:T(2,128)S(1)}, f32[2,1024]{1,0:T(2,128)}, u32[]{:S(2)}) copy-start(f32[2,1024]{1,0:T(2,128)} %amp_ref.1) | copy-start | bytes 24580
  11.1 1.7 %copy-start.1 = (s32[16,16]{1,0:T(8,128)S(1)}, s32[16,16]{1,0:T(8,128)}, u32[]{:S(2)}) copy-start(s32[16,16]{1,0:T(8,128)} %mask_ref.1) | copy-start | bytes 3076
  11.2 2.2 %copy-start.2 = (f32[2,8]{1,0:T(2,128)S(1)}, f32[2,8]{1,0:T(2,128)}, u32[]{:S(2)}) copy-start(f32[2,8]{1,0:T(2,128)} %basis_ref.1) | copy-start | bytes 196
  11.2 2.1 %collective-permute-start.3 = (f32[8,512]{1,0:T(8,128)S(1)}, f32[8,512]{1,0:T(8,128)S(1)}, u32[]{:S(2)}, u32[]{:S(2)}) collective-permute-start(f32[8,512]{1,0:T(8,128)S(1)} %pad_maximum_fusion.1), channel_id=1, source_target_pairs={{0,1},{1,0},{2,3},{3,2},{4,5},{5,4},{6,7},{7,6},{8,9},{9,8},{10,11... | collective-permute-start | bytes 49160 | tf_op jit(solution)/shard_map/ppermute | solution.py:254
  17.9 13.6 %collective-permute-start.9 = (bf16[256,512]{1,0:T(8,128)(2,1)S(1)}, bf16[256,512]{1,0:T(8,128)(2,1)S(1)}, u32[]{:S(2)}, u32[]{:S(2)}) collective-permute-start(bf16[256,512]{1,0:T(8,128)(2,1)S(1)} %shard_map.66), channel_id=1, source_target_pairs={{0,2},{1,5},{2,0},{3,7},{4,6},{5,1},{6,4},{7,3},{8,10},{9,13},{10,... | collective-permute-start | bytes 786440 | tf_op jit(solution)/shard_map/ppermute | solution.py:232
  19.8 6.0 %collective-permute-start.5 = (bf16[256,256]{1,0:T(8,128)(2,1)S(1)}, bf16[256,256]{1,0:T(8,128)(2,1)S(1)}, u32[]{:S(2)}, u32[]{:S(2)}) collective-permute-start(bf16[256,256]{1,0:T(8,128)(2,1)S(1)} %shard_map.61), channel_id=1, source_target_pairs={{0,2},{1,5},{2,0},{3,7},{4,6},{5,1},{6,4},{7,3},{8,10},{9,13},{10,... | collective-permute-start | bytes 393224 | tf_op jit(solution)/shard_map/ppermute | solution.py:232
  20.0 7.2 %collective-permute-start.6 = (bf16[256,256]{1,0:T(8,128)(2,1)S(1)}, bf16[256,256]{1,0:T(8,128)(2,1)S(1)}, u32[]{:S(2)}, u32[]{:S(2)}) collective-permute-start(bf16[256,256]{1,0:T(8,128)(2,1)S(1)} %shard_map.62), channel_id=1, source_target_pairs={{0,2},{1,5},{2,0},{3,7},{4,6},{5,1},{6,4},{7,3},{8,10},{9,13},{10,... | collective-permute-start | bytes 393224 | tf_op jit(solution)/shard_map/ppermute | solution.py:232
  22.9 9.2 %collective-permute-start.4 = (bf16[256,512]{1,0:T(8,128)(2,1)S(1)}, bf16[256,512]{1,0:T(8,128)(2,1)S(1)}, u32[]{:S(2)}, u32[]{:S(2)}) collective-permute-start(bf16[256,512]{1,0:T(8,128)(2,1)S(1)} %shard_map.59), channel_id=1, source_target_pairs={{0,2},{1,5},{2,0},{3,7},{4,6},{5,1},{6,4},{7,3},{8,10},{9,13},{10,... | collective-permute-start | bytes 786440 | tf_op jit(solution)/shard_map/ppermute | solution.py:232
  27.2 8.2 %collective-permute-start.7 = (bf16[256,512]{1,0:T(8,128)(2,1)S(1)}, bf16[256,512]{1,0:T(8,128)(2,1)S(1)}, u32[]{:S(2)}, u32[]{:S(2)}) collective-permute-start(bf16[256,512]{1,0:T(8,128)(2,1)S(1)} %add_convert_fusion.1), channel_id=1, source_target_pairs={{0,4},{1,3},{2,6},{3,1},{4,0},{5,7},{6,2},{7,5},{8,12},{9,11},{10,... | collective-permute-start | bytes 786440 | tf_op jit(solution)/shard_map/ppermute | solution.py:232
  29.9 9.9 %collective-permute-start.8 = (bf16[256,512]{1,0:T(8,128)(2,1)S(1)}, bf16[256,512]{1,0:T(8,128)(2,1)S(1)}, u32[]{:S(2)}, u32[]{:S(2)}) collective-permute-start(bf16[256,512]{1,0:T(8,128)(2,1)S(1)} %shard_map.65), channel_id=1, source_target_pairs={{0,2},{1,5},{2,0},{3,7},{4,6},{5,1},{6,4},{7,3},{8,10},{9,13},{10,... | collective-permute-start | bytes 786440 | tf_op jit(solution)/shard_map/ppermute | solution.py:232
  31.5 9.4 %collective-permute-start.10 = (bf16[256,512]{1,0:T(8,128)(2,1)S(1)}, bf16[256,512]{1,0:T(8,128)(2,1)S(1)}, u32[]{:S(2)}, u32[]{:S(2)}) collective-permute-start(bf16[256,512]{1,0:T(8,128)(2,1)S(1)} %add_convert_fusion), channel_id=1, source_target_pairs={{0,4},{1,3},{2,6},{3,1},{4,0},{5,7},{6,2},{7,5},{8,12},{9,11},{10,... | collective-permute-start | bytes 786440 | tf_op jit(solution)/shard_map/ppermute | solution.py:232
  35.6 11.0 %collective-permute-start.11 = (bf16[256,512]{1,0:T(8,128)(2,1)S(1)}, bf16[256,512]{1,0:T(8,128)(2,1)S(1)}, u32[]{:S(2)}, u32[]{:S(2)}) collective-permute-start(bf16[256,512]{1,0:T(8,128)(2,1)S(1)} %multiply_convert_fusion.1.resid_ref), channel_id=1, source_target_pairs={{0,4},{1,3},{2,6},{3,1},{4,0},{5,7},{6,2},{7,5},{8,12},{9,11},{10,... | collective-permute-start | bytes 786440 | tf_op jit(solution)/shard_map/ppermute | solution.py:232
  37.8 16.8 %collective-permute-start.14 = (bf16[256,512]{1,0:T(8,128)(2,1)S(1)}, bf16[256,512]{1,0:T(8,128)(2,1)S(1)}, u32[]{:S(2)}, u32[]{:S(2)}) collective-permute-start(bf16[256,512]{1,0:T(8,128)(2,1)S(1)} %multiply_convert_fusion.1.resid_ref), channel_id=1, source_target_pairs={{0,2},{1,5},{2,0},{3,7},{4,6},{5,1},{6,4},{7,3},{8,10},{9,13},{10,... | collective-permute-start | bytes 786440 | tf_op jit(solution)/shard_map/ppermute | solution.py:232
  41.1 8.3 %collective-permute-start.12 = (bf16[256,256]{1,0:T(8,128)(2,1)S(1)}, bf16[256,256]{1,0:T(8,128)(2,1)S(1)}, u32[]{:S(2)}, u32[]{:S(2)}) collective-permute-start(bf16[256,256]{1,0:T(8,128)(2,1)S(1)} %get-tuple-element.26), channel_id=1, source_target_pairs={{0,4},{1,3},{2,6},{3,1},{4,0},{5,7},{6,2},{7,5},{8,12},{9,11},{10,... | collective-permute-start | bytes 393224 | tf_op jit(solution)/shard_map/ppermute | solution.py:232
  43.2 12.8 %collective-permute-start.15 = (bf16[256,512]{1,0:T(8,128)(2,1)S(1)}, bf16[256,512]{1,0:T(8,128)(2,1)S(1)}, u32[]{:S(2)}, u32[]{:S(2)}) collective-permute-start(bf16[256,512]{1,0:T(8,128)(2,1)S(1)} %multiply_convert_fusion.resid_ref), channel_id=1, source_target_pairs={{0,2},{1,5},{2,0},{3,7},{4,6},{5,1},{6,4},{7,3},{8,10},{9,13},{10,... | collective-permute-start | bytes 786440 | tf_op jit(solution)/shard_map/ppermute | solution.py:232
  44.8 8.1 %collective-permute-start.13 = (bf16[256,256]{1,0:T(8,128)(2,1)S(1)}, bf16[256,256]{1,0:T(8,128)(2,1)S(1)}, u32[]{:S(2)}, u32[]{:S(2)}) collective-permute-start(bf16[256,256]{1,0:T(8,128)(2,1)S(1)} %get-tuple-element.25), channel_id=1, source_target_pairs={{0,4},{1,3},{2,6},{3,1},{4,0},{5,7},{6,2},{7,5},{8,12},{9,11},{10,... | collective-permute-start | bytes 393224 | tf_op jit(solution)/shard_map/ppermute | solution.py:232
  46.6 11.0 %collective-permute-start.16 = (bf16[256,512]{1,0:T(8,128)(2,1)S(1)}, bf16[256,512]{1,0:T(8,128)(2,1)S(1)}, u32[]{:S(2)}, u32[]{:S(2)}) collective-permute-start(bf16[256,512]{1,0:T(8,128)(2,1)S(1)} %collective-permute-done.11.resid_ref), channel_id=1, source_target_pairs={{0,2},{1,5},{2,0},{3,7},{4,6},{5,1},{6,4},{7,3},{8,10},{9,13},{10,... | collective-permute-start | bytes 786440 | tf_op jit(solution)/shard_map/ppermute | solution.py:232
  49.4 7.6 %collective-permute-start.17 = (bf16[256,256]{1,0:T(8,128)(2,1)S(1)}, bf16[256,256]{1,0:T(8,128)(2,1)S(1)}, u32[]{:S(2)}, u32[]{:S(2)}) collective-permute-start(bf16[256,256]{1,0:T(8,128)(2,1)S(1)} %collective-permute-done.12.resid_ref), channel_id=1, source_target_pairs={{0,2},{1,5},{2,0},{3,7},{4,6},{5,1},{6,4},{7,3},{8,10},{9,13},{10,... | collective-permute-start | bytes 393224 | tf_op jit(solution)/shard_map/ppermute | solution.py:232
  52.9 5.8 %collective-permute-start.18 = (bf16[256,256]{1,0:T(8,128)(2,1)S(1)}, bf16[256,256]{1,0:T(8,128)(2,1)S(1)}, u32[]{:S(2)}, u32[]{:S(2)}) collective-permute-start(bf16[256,256]{1,0:T(8,128)(2,1)S(1)} %collective-permute-done.13.resid_ref), channel_id=1, source_target_pairs={{0,2},{1,5},{2,0},{3,7},{4,6},{5,1},{6,4},{7,3},{8,10},{9,13},{10,... | collective-permute-start | bytes 393224 | tf_op jit(solution)/shard_map/ppermute | solution.py:232
  59.4 5.1 %collective-permute-start.19 = (f32[4,1024]{1,0:T(4,128)S(1)}, f32[4,1024]{1,0:T(4,128)S(1)}, u32[]{:S(2)}, u32[]{:S(2)}) collective-permute-start(f32[4,1024]{1,0:T(4,128)S(1)} %get-tuple-element.24), channel_id=1, source_target_pairs={{0,16},{8,24},{16,0},{24,8},{1,17},{9,25},{17,1},{25,9},{2,18},{10... | collective-permute-start | bytes 49160 | tf_op jit(solution)/shard_map/ppermute | solution.py:235
  64.5 3.7 %collective-permute-start.20 = (f32[2,1024]{1,0:T(2,128)S(1)}, f32[2,1024]{1,0:T(2,128)S(1)}, u32[]{:S(2)}, u32[]{:S(2)}) collective-permute-start(f32[2,1024]{1,0:T(2,128)S(1)} %slice.27), channel_id=1, source_target_pairs={{0,8},{8,0},{16,24},{24,16},{1,9},{9,1},{17,25},{25,17},{2,10},{10... | collective-permute-start | bytes 24584 | tf_op jit(solution)/shard_map/ppermute | solution.py:235
  68.3 1.2 %collective-permute-start.21 = (f32[2,512]{1,0:T(2,128)S(1)}, f32[2,512]{1,0:T(2,128)S(1)}, u32[]{:S(2)}, u32[]{:S(2)}) collective-permute-start(f32[2,512]{1,0:T(2,128)S(1)} %slice.29), channel_id=1, source_target_pairs={{0,1},{1,0},{2,3},{3,2},{4,5},{5,4},{6,7},{7,6},{8,9},{9,8},{10,11... | collective-permute-start | bytes 12296 | tf_op jit(solution)/shard_map/ppermute | solution.py:335

commit v7 on v5

--- a/solution.py
+++ b/solution.py
@@ -54,7 +54,8 @@
         pick = ((at >= low) & (at < low + size)).astype(BF16)
         weight = down * amp(start) * along(rows, pick)
         for i in [0] if d == 0 else [n - 1] if d == n // 2 else [2 * d - 1, 2 * d]:
-            u, at_block = divmod(i, n // 2)
+            u = int(i >= split_at(n))
+            at_block = i - u * split_at(n)
             weight_refs[u][:, at_block * tile : (at_block + 1) * tile] = weight
 
 
@@ -186,8 +187,8 @@
     sens_sum(n, part, step, piece_ref[0], resid_ref, green_ref, emit)
 
 
-def first_sent(n):
-    return n - 1, 0
+def split_at(n):
+    return n // 2
 
 
 SMEM = pl.BlockSpec(memory_space=pltpu.SMEM)
@@ -220,7 +221,7 @@
     core, chip = here % 2, here // 2
     flops = 2 * tile * tile * width
     moved = 2 * stations * width + 2 * tile * stations
-    halves = [tuple(range(u * n // 2, (u + 1) * n // 2)) for u in (0, 1)]
+    halves = [tuple(range(split_at(n))), tuple(range(split_at(n), n))]
 
     def dims(which):
         return [(which + j) % bits for j in range(bits)]
@@ -278,53 +279,39 @@
             held[q, 0], held[q, 1] = corr_parts(q, halves, F32)
             continue
         for u in (0, 1):
-            if (q, u) == first_sent(n):
-                middle = n // 4
-                held[q, "b"] = corr_parts(q, [halves[u][middle:]], BF16)[0]
-                held[q, "a"] = corr_parts(q, [halves[u][:middle]], BF16)[0]
-            else:
-                held[q, u] = corr_parts(q, [halves[u]], BF16)[0]
+            held[q, u] = corr_parts(q, [halves[u]], BF16)[0]
     weight = call(
-        functools.partial(weight_kernel, n), [((tile, stations // 2), F32)] * 2,
+        functools.partial(weight_kernel, n), [((tile, len(half) * tile), F32) for half in halves],
         [SMEM, SMEM, VMEM, VMEM], 0, 4 * tile * stations, cores, pieces[0], amplitude, block_mask,
     )
     for j in range(bits):
         for q in sorted((q for q in range(n) if q % (1 << j) == 0 and (q >> j) & 1), reverse=True):
             for u in (0, 1):
-                if (q, u) == first_sent(n):
-                    late, early = (swap_chip(held[q, k], j) for k in "ab")
-                    got = jnp.concatenate((late, early), axis=1)
-                else:
-                    got = swap_chip(held[q, u].astype(BF16), j)
+                got = swap_chip(held[q, u].astype(BF16), j)
                 held[q ^ (1 << j), u] = held[q ^ (1 << j), u] + got.astype(F32)
     resid = {(0, u): (held[0, u] * weight[u]).astype(BF16) for u in (0, 1)}
 
-    order, parts = [0], {"0": halves[0], "1": halves[1], "c": halves[1][: n // 4], "d": halves[1][n // 4 :]}
+    order = [0]
     for j in reversed(range(bits)):
         for q in list(order):
             order.append(q | (1 << j))
             for u in (0, 1):
-                if (order[-1], u) == (n - 1, 1):
-                    cut = n // 4 * tile
-                    resid[n - 1, "c"] = swap_chip(resid[q, u][:, :cut], j)
-                    resid[n - 1, "d"] = swap_chip(resid[q, u][:, cut:], j)
-                else:
-                    resid[order[-1], u] = swap_chip(resid[q, u], j)
+                resid[order[-1], u] = swap_chip(resid[q, u], j)
     step = min(512, width // 2)
     sens = 0.0
     for (q, u), value in resid.items():
-        if (q, u) == (n - 1, "d"):
+        if (q, u) == (n - 1, 1):
             continue
-        part = parts[str(u)]
+        part = halves[u]
         sens = sens + call(
             functools.partial(sens_kernel, n, part, step), [((1, width // 2), F32)],
             [SMEM, VMEM, VMEM], flops * len(part), moved, pieces[q], value, field,
         )
     half_rows = ((n_freq * each // 2, width // 2), F32)
     low, high = call(
-        functools.partial(last_kernel, n, parts["d"], step), [half_rows] * 2,
-        [SMEM, VMEM, VMEM, VMEM, VMEM], flops * (n // 4), moved,
-        pieces[n - 1], column, sens, resid[n - 1, "d"], field,
+        functools.partial(last_kernel, n, halves[1], step), [half_rows] * 2,
+        [SMEM, VMEM, VMEM, VMEM, VMEM], flops * len(halves[1]), moved,
+        pieces[n - 1], column, sens, resid[n - 1, 1], field,
     )
 
     for j in reversed(range(z_bits)):

time: 69.8 us -> 64.3 us (0.921)
  starting transfers between devices: 30.8 us -> 24.9 us
  waiting for transfers between devices: 17 us -> 17.8 us
    ppermute x14 -> x12, starting transfers between devices: 19.3 us -> 13.5 us  [swap_chip(): return lax.ppermute(value, 'cell', pairs)]
    ppermute x14 -> x12, waiting for transfers between devices: 9.13 us -> 9.94 us  [swap_chip(): return lax.ppermute(value, 'cell', pairs)]
    pallas_call x20 -> x18, Pallas kernels: 20.3 us -> 20 us  [call(): pl.pallas_call(kernel, out_shape=out_shape, in_specs=specs, out_specs=[VM...]
  transfers between devices with their start and end apart: 21 -> 19, of which waited for: 11 -> 11; matrix products, arithmetic and copies ran while one was open for 1% -> 1% of each run, Pallas kernels for 20% -> 24%
where the time goes in v7:
time: 64.3 us; the launch traced here: 64.1 us
  starting transfers between devices  24.9 us (39%)
  Pallas kernels  20 us (31%)
  waiting for transfers between devices  17.8 us (28%)
  other arithmetic  1.11 us (2%)
    pallas_call x18, Pallas kernels, call(): pl.pallas_call(kernel, out_shape=out_shape, in_specs=specs, out_specs=[VM...  20 us
    ppermute x12, starting transfers between devices, swap_chip(): return lax.ppermute(value, 'cell', pairs)  13.5 us
    ppermute x4, starting transfers between devices, swap_plane(): return lax.ppermute(value, 'freq', [(i, i ^ 1 << j) for i in range(n_freq)])  10.6 us
    ppermute x12, waiting for transfers between devices, swap_chip(): return lax.ppermute(value, 'cell', pairs)  9.94 us
    ppermute x4, waiting for transfers between devices, swap_plane(): return lax.ppermute(value, 'freq', [(i, i ^ 1 << j) for i in range(n_freq)])  6.73 us
  transfers between devices with their start and end apart: 19, of which 11 were waited for; matrix products, arithmetic and copies ran while one was open for 1% of the time, Pallas kernels for 24%

profile of v7, /device:TPU:0, one launch (start us, length us, event | category | flops | bytes accessed | tf_op | source)
XLA Modules:
  0.0 64.1 jit_solution(8610603329916398170)
XLA Ops:
  0.0 1.6 %shard_map.55 = bf16[2,1024,512]{2,1,0:T(8,128)(2,1)S(1)} custom-call(s32[1]{0:T(128)} %bitcast.1.core_ref, bf16[2,2,1024,512]{3,2,1,0:T(8,128)(2,1)} %green_ref.3, s32[1]{0:T(128)} %bitcast.2.rest_0_.plane_ref, s32[1]{0:T(128)} %bitcast.3.rest_1_.piece_ref, s32[1]{0:T(128)} %bitcast.4.rest_2_.piece_ref, s32[1]{0:T(128)} %bitcast.5.rest_3_.piece_ref, ...), custom_call_target="tpu_custom_call" | custom-call | bytes 4194304 | tf_op jit(solution)/shard_map/pallas_call | solution.py:201
  1.6 0.6 collective-permute-start
  2.1 2.6 %collective-permute-start.1 = (f32[2,512]{1,0:T(2,128)S(1)}, f32[2,512]{1,0:T(2,128)S(1)}, u32[]{:S(2)}, u32[]{:S(2)}) collective-permute-start(f32[2,512]{1,0:T(2,128)S(1)} %copy-done.3), channel_id=1, source_target_pairs={{0,8},{8,0},{16,24},{24,16},{1,9},{9,1},{17,25},{25,17},{2,10},{10... | collective-permute-start | bytes 12296 | tf_op jit(solution)/shard_map/ppermute | solution.py:236
  4.8 1.6 %collective-permute-done.1 = f32[2,512]{1,0:T(2,128)S(1)} collective-permute-done((f32[2,512]{1,0:T(2,128)S(1)}, f32[2,512]{1,0:T(2,128)S(1)}, u32[]{:S(2)}, u32[]{:S(2)}) %collective-permute-start.1) | collective-permute-done | bytes 4128 | tf_op jit(solution)/shard_map/ppermute | solution.py:236
  6.4 3.1 %collective-permute-start.2 = (f32[4,512]{1,0:T(4,128)S(1)}, f32[4,512]{1,0:T(4,128)S(1)}, u32[]{:S(2)}, u32[]{:S(2)}) collective-permute-start(f32[4,512]{1,0:T(4,128)S(1)} %pad_maximum_fusion.2), channel_id=1, source_target_pairs={{0,16},{8,24},{16,0},{24,8},{1,17},{9,25},{17,1},{25,9},{2,18},{10... | collective-permute-start | bytes 24584 | tf_op jit(solution)/shard_map/ppermute | solution.py:236
  9.5 1.6 %collective-permute-done.2 = f32[4,512]{1,0:T(4,128)S(1)} collective-permute-done((f32[4,512]{1,0:T(4,128)S(1)}, f32[4,512]{1,0:T(4,128)S(1)}, u32[]{:S(2)}, u32[]{:S(2)}) %collective-permute-start.2) | collective-permute-done | bytes 8224 | tf_op jit(solution)/shard_map/ppermute | solution.py:236
  11.2 1.6 %shard_map.56.field_ref = bf16[1024,2048]{1,0:T(8,128)(2,1)S(1)} custom-call(s32[1]{0:T(128)} %bitcast.1.core_ref, bf16[2,2,1024,512]{3,2,1,0:T(8,128)(2,1)} %green_ref.3), custom_call_target="tpu_custom_call" | custom-call | bytes 4194304 | tf_op jit(solution)/shard_map/pallas_call | solution.py:201
  12.8 0.4 shard_map.62
  13.3 0.9 %shard_map.57 = (bf16[1024,2048]{1,0:T(8,128)(2,1)S(1)}, f32[8,128]{1,0:T(8,128)S(1)}) custom-call(s32[1]{0:T(128)} %bitcast.1.core_ref, s32[1]{0:T(128)} %bitcast.2.rest_0_.plane_ref, f32[2,8]{1,0:T(2,128)S(1)} %copy-done.2, bf16[2,1024,512]{2,1,0:T(8,128)(2,1)S(1)} %collective-permute-done.theirs_ref, ...), custom_call_target="tpu_custom_call", output_to_operand_aliasing={{0}: (4, {})} | custom-call | bytes 4194304 | tf_op jit(solution)/shard_map/pallas_call | solution.py:201
  14.2 1.0 %shard_map.61 = bf16[256,512]{1,0:T(8,128)(2,1)S(1)} custom-call(s32[1]{0:T(128)} %bitcast.rest_4_.piece_ref, f32[8,128]{1,0:T(8,128)S(1)} %get-tuple-element.15.column_ref, f32[8,1024]{1,0:T(8,128)S(1)} %pad_maximum_fusion.known_ref, bf16[1024,2048]{1,0:T(8,128)(2,1)S(1)} %get-tuple-element.16.green_ref), custom_call_target="tpu_custom_call" | custom-call | flops 536870912 | bytes 4718592 | tf_op jit(solution)/shard_map/pallas_call | solution.py:201
  15.3 1.9 %collective-permute-start.5 = (bf16[256,512]{1,0:T(8,128)(2,1)S(1)}, bf16[256,512]{1,0:T(8,128)(2,1)S(1)}, u32[]{:S(2)}, u32[]{:S(2)}) collective-permute-start(bf16[256,512]{1,0:T(8,128)(2,1)S(1)} %shard_map.61), channel_id=1, source_target_pairs={{0,2},{1,5},{2,0},{3,7},{4,6},{5,1},{6,4},{7,3},{8,10},{9,13},{10,... | collective-permute-start | bytes 786440 | tf_op jit(solution)/shard_map/ppermute | solution.py:233
  17.2 0.7 %shard_map.65 = bf16[256,512]{1,0:T(8,128)(2,1)S(1)} custom-call(s32[1]{0:T(128)} %bitcast.rest_4_.piece_ref, f32[8,128]{1,0:T(8,128)S(1)} %get-tuple-element.15.column_ref, f32[8,1024]{1,0:T(8,128)S(1)} %pad_maximum_fusion.known_ref, bf16[1024,2048]{1,0:T(8,128)(2,1)S(1)} %get-tuple-element.16.green_ref), custom_call_target="tpu_custom_call" | custom-call | flops 536870912 | bytes 4718592 | tf_op jit(solution)/shard_map/pallas_call | solution.py:201
  17.9 0.3 collective-permute-start.8
  18.2 1.0 %shard_map.59 = bf16[256,512]{1,0:T(8,128)(2,1)S(1)} custom-call(s32[1]{0:T(128)} %bitcast.4.rest_2_.piece_ref, f32[8,128]{1,0:T(8,128)S(1)} %get-tuple-element.15.column_ref, f32[8,1024]{1,0:T(8,128)S(1)} %pad_maximum_fusion.known_ref, bf16[1024,2048]{1,0:T(8,128)(2,1)S(1)} %get-tuple-element.16.green_ref), custom_call_target="tpu_custom_call" | custom-call | flops 536870912 | bytes 4718592 | tf_op jit(solution)/shard_map/pallas_call | solution.py:201
  19.3 1.9 %collective-permute-start.4 = (bf16[256,512]{1,0:T(8,128)(2,1)S(1)}, bf16[256,512]{1,0:T(8,128)(2,1)S(1)}, u32[]{:S(2)}, u32[]{:S(2)}) collective-permute-start(bf16[256,512]{1,0:T(8,128)(2,1)S(1)} %shard_map.59), channel_id=1, source_target_pairs={{0,2},{1,5},{2,0},{3,7},{4,6},{5,1},{6,4},{7,3},{8,10},{9,13},{10,... | collective-permute-start | bytes 786440 | tf_op jit(solution)/shard_map/ppermute | solution.py:233
  21.1 1.6 %shard_map.60 = (f32[256,512]{1,0:T(8,128)S(1)}, f32[256,512]{1,0:T(8,128)S(1)}) custom-call(s32[1]{0:T(128)} %bitcast.5.rest_3_.piece_ref, f32[8,128]{1,0:T(8,128)S(1)} %get-tuple-element.15.column_ref, f32[8,1024]{1,0:T(8,128)S(1)} %pad_maximum_fusion.known_ref, bf16[1024,2048]{1,0:T(8,128)(2,1)S(1)} %get-tuple-element.16.green_ref), custom_call_target="tpu_custom_call" | custom-call | flops 1073741824 | bytes 4718592 | tf_op jit(solution)/shard_map/pallas_call | solution.py:201
  22.7 1.6 %shard_map.58 = (f32[256,512]{1,0:T(8,128)S(1)}, f32[256,512]{1,0:T(8,128)S(1)}) custom-call(s32[1]{0:T(128)} %bitcast.3.rest_1_.piece_ref, f32[8,128]{1,0:T(8,128)S(1)} %get-tuple-element.15.column_ref, f32[8,1024]{1,0:T(8,128)S(1)} %pad_maximum_fusion.known_ref, bf16[1024,2048]{1,0:T(8,128)(2,1)S(1)} %get-tuple-element.16.green_ref), custom_call_target="tpu_custom_call" | custom-call | flops 1073741824 | bytes 4718592 | tf_op jit(solution)/shard_map/pallas_call | solution.py:201
  24.4 1.6 %collective-permute-start.6 = (bf16[256,512]{1,0:T(8,128)(2,1)S(1)}, bf16[256,512]{1,0:T(8,128)(2,1)S(1)}, u32[]{:S(2)}, u32[]{:S(2)}) collective-permute-start(bf16[256,512]{1,0:T(8,128)(2,1)S(1)} %add_convert_fusion.1), channel_id=1, source_target_pairs={{0,4},{1,3},{2,6},{3,1},{4,0},{5,7},{6,2},{7,5},{8,12},{9,11},{10,... | collective-permute-start | bytes 786440 | tf_op jit(solution)/shard_map/ppermute | solution.py:233
  26.0 0.8 %shard_map.64 = bf16[256,512]{1,0:T(8,128)(2,1)S(1)} custom-call(s32[1]{0:T(128)} %bitcast.4.rest_2_.piece_ref, f32[8,128]{1,0:T(8,128)S(1)} %get-tuple-element.15.column_ref, f32[8,1024]{1,0:T(8,128)S(1)} %pad_maximum_fusion.known_ref, bf16[1024,2048]{1,0:T(8,128)(2,1)S(1)} %get-tuple-element.16.green_ref), custom_call_target="tpu_custom_call" | custom-call | flops 536870912 | bytes 4718592 | tf_op jit(solution)/shard_map/pallas_call | solution.py:201
  26.7 0.6 collective-permute-start.7
  27.4 0.2 collective-permute-start.9
  27.7 0.3 collective-permute-done.4
  28.0 4.9 %collective-permute-done.6 = bf16[256,512]{1,0:T(8,128)(2,1)S(1)} collective-permute-done((bf16[256,512]{1,0:T(8,128)(2,1)S(1)}, bf16[256,512]{1,0:T(8,128)(2,1)S(1)}, u32[]{:S(2)}, u32[]{:S(2)}) %collective-permute-start.6) | collective-permute-done | bytes 262176 | tf_op jit(solution)/shard_map/ppermute | solution.py:233
  32.9 0.2 multiply_convert_fusion.1.resid_ref
  33.0 2.1 %collective-permute-start.10 = (bf16[256,512]{1,0:T(8,128)(2,1)S(1)}, bf16[256,512]{1,0:T(8,128)(2,1)S(1)}, u32[]{:S(2)}, u32[]{:S(2)}) collective-permute-start(bf16[256,512]{1,0:T(8,128)(2,1)S(1)} %multiply_convert_fusion.1.resid_ref), channel_id=1, source_target_pairs={{0,4},{1,3},{2,6},{3,1},{4,0},{5,7},{6,2},{7,5},{8,12},{9,11},{10,... | collective-permute-start | bytes 786440 | tf_op jit(solution)/shard_map/ppermute | solution.py:233
  35.1 0.9 %collective-permute-done.7 = bf16[256,512]{1,0:T(8,128)(2,1)S(1)} collective-permute-done((bf16[256,512]{1,0:T(8,128)(2,1)S(1)}, bf16[256,512]{1,0:T(8,128)(2,1)S(1)}, u32[]{:S(2)}, u32[]{:S(2)}) %collective-permute-start.7) | collective-permute-done | bytes 262176 | tf_op jit(solution)/shard_map/ppermute | solution.py:233
  36.0 0.5 collective-permute-done.9
  36.6 1.3 %collective-permute-start.11 = (bf16[256,512]{1,0:T(8,128)(2,1)S(1)}, bf16[256,512]{1,0:T(8,128)(2,1)S(1)}, u32[]{:S(2)}, u32[]{:S(2)}) collective-permute-start(bf16[256,512]{1,0:T(8,128)(2,1)S(1)} %multiply_convert_fusion.resid_ref), channel_id=1, source_target_pairs={{0,4},{1,3},{2,6},{3,1},{4,0},{5,7},{6,2},{7,5},{8,12},{9,11},{10,... | collective-permute-start | bytes 786440 | tf_op jit(solution)/shard_map/ppermute | solution.py:233
  37.9 0.9 %collective-permute-start.12 = (bf16[256,512]{1,0:T(8,128)(2,1)S(1)}, bf16[256,512]{1,0:T(8,128)(2,1)S(1)}, u32[]{:S(2)}, u32[]{:S(2)}) collective-permute-start(bf16[256,512]{1,0:T(8,128)(2,1)S(1)} %multiply_convert_fusion.1.resid_ref), channel_id=1, source_target_pairs={{0,2},{1,5},{2,0},{3,7},{4,6},{5,1},{6,4},{7,3},{8,10},{9,13},{10,... | collective-permute-start | bytes 786440 | tf_op jit(solution)/shard_map/ppermute | solution.py:233
  38.9 1.1 %collective-permute-start.13 = (bf16[256,512]{1,0:T(8,128)(2,1)S(1)}, bf16[256,512]{1,0:T(8,128)(2,1)S(1)}, u32[]{:S(2)}, u32[]{:S(2)}) collective-permute-start(bf16[256,512]{1,0:T(8,128)(2,1)S(1)} %multiply_convert_fusion.resid_ref), channel_id=1, source_target_pairs={{0,2},{1,5},{2,0},{3,7},{4,6},{5,1},{6,4},{7,3},{8,10},{9,13},{10,... | collective-permute-start | bytes 786440 | tf_op jit(solution)/shard_map/ppermute | solution.py:233
  40.0 0.9 %collective-permute-start.14 = (bf16[256,512]{1,0:T(8,128)(2,1)S(1)}, bf16[256,512]{1,0:T(8,128)(2,1)S(1)}, u32[]{:S(2)}, u32[]{:S(2)}) collective-permute-start(bf16[256,512]{1,0:T(8,128)(2,1)S(1)} %collective-permute-done.10.resid_ref), channel_id=1, source_target_pairs={{0,2},{1,5},{2,0},{3,7},{4,6},{5,1},{6,4},{7,3},{8,10},{9,13},{10,... | collective-permute-start | bytes 786440 | tf_op jit(solution)/shard_map/ppermute | solution.py:233
  40.9 1.0 %shard_map.66 = f32[1,1024]{1,0:T(1,128)S(1)} custom-call(s32[1]{0:T(128)} %bitcast.3.rest_1_.piece_ref, bf16[256,512]{1,0:T(8,128)(2,1)S(1)} %multiply_convert_fusion.resid_ref, bf16[1024,2048]{1,0:T(8,128)(2,1)S(1)} %get-tuple-element.16.green_ref), custom_call_target="tpu_custom_call" | custom-call | flops 536870912 | bytes 4718592 | tf_op jit(solution)/shard_map/pallas_call | solution.py:201
  41.9 1.1 %shard_map.63 = f32[1,1024]{1,0:T(1,128)S(1)} custom-call(s32[1]{0:T(128)} %bitcast.3.rest_1_.piece_ref, bf16[256,512]{1,0:T(8,128)(2,1)S(1)} %multiply_convert_fusion.1.resid_ref, bf16[1024,2048]{1,0:T(8,128)(2,1)S(1)} %get-tuple-element.16.green_ref), custom_call_target="tpu_custom_call" | custom-call | flops 536870912 | bytes 4718592 | tf_op jit(solution)/shard_map/pallas_call | solution.py:201
  43.0 2.8 %collective-permute-done.11.resid_ref = bf16[256,512]{1,0:T(8,128)(2,1)S(1)} collective-permute-done((bf16[256,512]{1,0:T(8,128)(2,1)S(1)}, bf16[256,512]{1,0:T(8,128)(2,1)S(1)}, u32[]{:S(2)}, u32[]{:S(2)}) %collective-permute-start.11) | collective-permute-done | bytes 262176 | tf_op jit(solution)/shard_map/ppermute | solution.py:233
  45.8 0.7 %collective-permute-start.15 = (bf16[256,512]{1,0:T(8,128)(2,1)S(1)}, bf16[256,512]{1,0:T(8,128)(2,1)S(1)}, u32[]{:S(2)}, u32[]{:S(2)}) collective-permute-start(bf16[256,512]{1,0:T(8,128)(2,1)S(1)} %collective-permute-done.11.resid_ref), channel_id=1, source_target_pairs={{0,2},{1,5},{2,0},{3,7},{4,6},{5,1},{6,4},{7,3},{8,10},{9,13},{10,... | collective-permute-start | bytes 786440 | tf_op jit(solution)/shard_map/ppermute | solution.py:233
  46.5 1.1 %shard_map.67 = f32[1,1024]{1,0:T(1,128)S(1)} custom-call(s32[1]{0:T(128)} %bitcast.5.rest_3_.piece_ref, bf16[256,512]{1,0:T(8,128)(2,1)S(1)} %collective-permute-done.10.resid_ref, bf16[1024,2048]{1,0:T(8,128)(2,1)S(1)} %get-tuple-element.16.green_ref), custom_call_target="tpu_custom_call" | custom-call | flops 536870912 | bytes 4718592 | tf_op jit(solution)/shard_map/pallas_call | solution.py:201
  47.7 1.0 %shard_map.68 = f32[1,1024]{1,0:T(1,128)S(1)} custom-call(s32[1]{0:T(128)} %bitcast.5.rest_3_.piece_ref, bf16[256,512]{1,0:T(8,128)(2,1)S(1)} %collective-permute-done.11.resid_ref, bf16[1024,2048]{1,0:T(8,128)(2,1)S(1)} %get-tuple-element.16.green_ref), custom_call_target="tpu_custom_call" | custom-call | flops 536870912 | bytes 4718592 | tf_op jit(solution)/shard_map/pallas_call | solution.py:201
  48.7 1.1 %shard_map.69 = f32[1,1024]{1,0:T(1,128)S(1)} custom-call(s32[1]{0:T(128)} %bitcast.4.rest_2_.piece_ref, bf16[256,512]{1,0:T(8,128)(2,1)S(1)} %collective-permute-done.12.resid_ref, bf16[1024,2048]{1,0:T(8,128)(2,1)S(1)} %get-tuple-element.16.green_ref), custom_call_target="tpu_custom_call" | custom-call | flops 536870912 | bytes 4718592 | tf_op jit(solution)/shard_map/pallas_call | solution.py:201
  49.8 1.2 %shard_map.70 = f32[1,1024]{1,0:T(1,128)S(1)} custom-call(s32[1]{0:T(128)} %bitcast.4.rest_2_.piece_ref, bf16[256,512]{1,0:T(8,128)(2,1)S(1)} %collective-permute-done.13.resid_ref, bf16[1024,2048]{1,0:T(8,128)(2,1)S(1)} %get-tuple-element.16.green_ref), custom_call_target="tpu_custom_call" | custom-call | flops 536870912 | bytes 4718592 | tf_op jit(solution)/shard_map/pallas_call | solution.py:201
  51.1 1.1 %shard_map.71 = f32[1,1024]{1,0:T(1,128)S(1)} custom-call(s32[1]{0:T(128)} %bitcast.rest_4_.piece_ref, bf16[256,512]{1,0:T(8,128)(2,1)S(1)} %collective-permute-done.14.resid_ref, bf16[1024,2048]{1,0:T(8,128)(2,1)S(1)} %get-tuple-element.16.green_ref), custom_call_target="tpu_custom_call" | custom-call | flops 536870912 | bytes 4718592 | tf_op jit(solution)/shard_map/pallas_call | solution.py:201
  52.2 0.6 collective-permute-done.15.resid_ref
  52.8 1.0 %shard_map.72 = (f32[4,1024]{1,0:T(4,128)S(1)}, f32[4,1024]{1,0:T(4,128)S(1)}) custom-call(s32[1]{0:T(128)} %bitcast.rest_4_.piece_ref, f32[8,128]{1,0:T(8,128)S(1)} %get-tuple-element.15.column_ref, f32[1,1024]{1,0:T(1,128)S(1)} %add_add_fusion.before_ref, bf16[256,512]{1,0:T(8,128)(2,1)S(1)} %collective-permute-done.15.resid_ref, ...), custom_call_target="tpu_custom_call" | custom-call | flops 536870912 | bytes 4718592 | tf_op jit(solution)/shard_map/pallas_call | solution.py:201
  53.8 2.9 %collective-permute-start.16 = (f32[4,1024]{1,0:T(4,128)S(1)}, f32[4,1024]{1,0:T(4,128)S(1)}, u32[]{:S(2)}, u32[]{:S(2)}) collective-permute-start(f32[4,1024]{1,0:T(4,128)S(1)} %get-tuple-element.24), channel_id=1, source_target_pairs={{0,16},{8,24},{16,0},{24,8},{1,17},{9,25},{17,1},{25,9},{2,18},{10... | collective-permute-start | bytes 49160 | tf_op jit(solution)/shard_map/ppermute | solution.py:236
  56.7 1.8 %collective-permute-done.16 = f32[4,1024]{1,0:T(4,128)S(1)} collective-permute-done((f32[4,1024]{1,0:T(4,128)S(1)}, f32[4,1024]{1,0:T(4,128)S(1)}, u32[]{:S(2)}, u32[]{:S(2)}) %collective-permute-start.16) | collective-permute-done | bytes 16416 | tf_op jit(solution)/shard_map/ppermute | solution.py:236
  58.6 2.0 %collective-permute-start.17 = (f32[2,1024]{1,0:T(2,128)S(1)}, f32[2,1024]{1,0:T(2,128)S(1)}, u32[]{:S(2)}, u32[]{:S(2)}) collective-permute-start(f32[2,1024]{1,0:T(2,128)S(1)} %slice.17), channel_id=1, source_target_pairs={{0,8},{8,0},{16,24},{24,16},{1,9},{9,1},{17,25},{25,17},{2,10},{10... | collective-permute-start | bytes 24584 | tf_op jit(solution)/shard_map/ppermute | solution.py:236
  60.6 1.7 %collective-permute-done.17 = f32[2,1024]{1,0:T(2,128)S(1)} collective-permute-done((f32[2,1024]{1,0:T(2,128)S(1)}, f32[2,1024]{1,0:T(2,128)S(1)}, u32[]{:S(2)}, u32[]{:S(2)}) %collective-permute-start.17) | collective-permute-done | bytes 8224 | tf_op jit(solution)/shard_map/ppermute | solution.py:236
  62.4 1.2 %collective-permute-done.18 = f32[2,512]{1,0:T(2,128)S(1)} collective-permute-done((f32[2,512]{1,0:T(2,128)S(1)}, f32[2,512]{1,0:T(2,128)S(1)}, u32[]{:S(2)}, u32[]{:S(2)}) %collective-permute-start.18) | collective-permute-done | bytes 4128 | tf_op jit(solution)/shard_map/ppermute | solution.py:320
  63.5 0.6 slice_add_fusion.1
  (29 shorter events, 0.6 us)
Async XLA Ops:
  0.0 2.1 %copy-start.3 = (f32[2,512]{1,0:T(2,128)S(1)}, f32[2,512]{1,0:T(2,128)}, u32[]{:S(2)}) copy-start(f32[2,512]{1,0:T(2,128)} %param.6) | copy-start | bytes 12292
  1.6 11.7 %collective-permute-start = (bf16[2,1024,512]{2,1,0:T(8,128)(2,1)S(1)}, bf16[2,1024,512]{2,1,0:T(8,128)(2,1)S(1)}, u32[]{:S(2)}, u32[]{:S(2)}) collective-permute-start(bf16[2,1024,512]{2,1,0:T(8,128)(2,1)S(1)} %shard_map.55), channel_id=1, source_target_pairs={{0,1},{1,0},{2,3},{3,2},{4,5},{5,4},{6,7},{7,6},{8,9},{9,8},{10,11... | collective-permute-start | bytes 6291464 | tf_op jit(solution)/shard_map/ppermute | solution.py:250
  2.1 4.2 %collective-permute-start.1 = (f32[2,512]{1,0:T(2,128)S(1)}, f32[2,512]{1,0:T(2,128)S(1)}, u32[]{:S(2)}, u32[]{:S(2)}) collective-permute-start(f32[2,512]{1,0:T(2,128)S(1)} %copy-done.3), channel_id=1, source_target_pairs={{0,8},{8,0},{16,24},{24,16},{1,9},{9,1},{17,25},{25,17},{2,10},{10... | collective-permute-start | bytes 12296 | tf_op jit(solution)/shard_map/ppermute | solution.py:236
  6.4 4.7 %collective-permute-start.2 = (f32[4,512]{1,0:T(4,128)S(1)}, f32[4,512]{1,0:T(4,128)S(1)}, u32[]{:S(2)}, u32[]{:S(2)}) collective-permute-start(f32[4,512]{1,0:T(4,128)S(1)} %pad_maximum_fusion.2), channel_id=1, source_target_pairs={{0,16},{8,24},{16,0},{24,8},{1,17},{9,25},{17,1},{25,9},{2,18},{10... | collective-permute-start | bytes 24584 | tf_op jit(solution)/shard_map/ppermute | solution.py:236
  11.1 1.7 %copy-start = (f32[2,1024]{1,0:T(2,128)S(1)}, f32[2,1024]{1,0:T(2,128)}, u32[]{:S(2)}) copy-start(f32[2,1024]{1,0:T(2,128)} %amp_ref.1) | copy-start | bytes 24580
  11.1 1.7 %copy-start.1 = (s32[16,16]{1,0:T(8,128)S(1)}, s32[16,16]{1,0:T(8,128)}, u32[]{:S(2)}) copy-start(s32[16,16]{1,0:T(8,128)} %mask_ref.1) | copy-start | bytes 3076
  11.2 2.2 %copy-start.2 = (f32[2,8]{1,0:T(2,128)S(1)}, f32[2,8]{1,0:T(2,128)}, u32[]{:S(2)}) copy-start(f32[2,8]{1,0:T(2,128)} %basis_ref.1) | copy-start | bytes 196
  11.2 2.1 %collective-permute-start.3 = (f32[8,512]{1,0:T(8,128)S(1)}, f32[8,512]{1,0:T(8,128)S(1)}, u32[]{:S(2)}, u32[]{:S(2)}) collective-permute-start(f32[8,512]{1,0:T(8,128)S(1)} %pad_maximum_fusion.1), channel_id=1, source_target_pairs={{0,1},{1,0},{2,3},{3,2},{4,5},{5,4},{6,7},{7,6},{8,9},{9,8},{10,11... | collective-permute-start | bytes 49160 | tf_op jit(solution)/shard_map/ppermute | solution.py:255
  15.3 9.0 %collective-permute-start.5 = (bf16[256,512]{1,0:T(8,128)(2,1)S(1)}, bf16[256,512]{1,0:T(8,128)(2,1)S(1)}, u32[]{:S(2)}, u32[]{:S(2)}) collective-permute-start(bf16[256,512]{1,0:T(8,128)(2,1)S(1)} %shard_map.61), channel_id=1, source_target_pairs={{0,2},{1,5},{2,0},{3,7},{4,6},{5,1},{6,4},{7,3},{8,10},{9,13},{10,... | collective-permute-start | bytes 786440 | tf_op jit(solution)/shard_map/ppermute | solution.py:233
  17.9 9.4 %collective-permute-start.8 = (bf16[256,512]{1,0:T(8,128)(2,1)S(1)}, bf16[256,512]{1,0:T(8,128)(2,1)S(1)}, u32[]{:S(2)}, u32[]{:S(2)}) collective-permute-start(bf16[256,512]{1,0:T(8,128)(2,1)S(1)} %shard_map.65), channel_id=1, source_target_pairs={{0,2},{1,5},{2,0},{3,7},{4,6},{5,1},{6,4},{7,3},{8,10},{9,13},{10,... | collective-permute-start | bytes 786440 | tf_op jit(solution)/shard_map/ppermute | solution.py:233
  19.3 8.7 %collective-permute-start.4 = (bf16[256,512]{1,0:T(8,128)(2,1)S(1)}, bf16[256,512]{1,0:T(8,128)(2,1)S(1)}, u32[]{:S(2)}, u32[]{:S(2)}) collective-permute-start(bf16[256,512]{1,0:T(8,128)(2,1)S(1)} %shard_map.59), channel_id=1, source_target_pairs={{0,2},{1,5},{2,0},{3,7},{4,6},{5,1},{6,4},{7,3},{8,10},{9,13},{10,... | collective-permute-start | bytes 786440 | tf_op jit(solution)/shard_map/ppermute | solution.py:233
  24.4 8.5 %collective-permute-start.6 = (bf16[256,512]{1,0:T(8,128)(2,1)S(1)}, bf16[256,512]{1,0:T(8,128)(2,1)S(1)}, u32[]{:S(2)}, u32[]{:S(2)}) collective-permute-start(bf16[256,512]{1,0:T(8,128)(2,1)S(1)} %add_convert_fusion.1), channel_id=1, source_target_pairs={{0,4},{1,3},{2,6},{3,1},{4,0},{5,7},{6,2},{7,5},{8,12},{9,11},{10,... | collective-permute-start | bytes 786440 | tf_op jit(solution)/shard_map/ppermute | solution.py:233
  26.7 9.2 %collective-permute-start.7 = (bf16[256,512]{1,0:T(8,128)(2,1)S(1)}, bf16[256,512]{1,0:T(8,128)(2,1)S(1)}, u32[]{:S(2)}, u32[]{:S(2)}) collective-permute-start(bf16[256,512]{1,0:T(8,128)(2,1)S(1)} %shard_map.64), channel_id=1, source_target_pairs={{0,2},{1,5},{2,0},{3,7},{4,6},{5,1},{6,4},{7,3},{8,10},{9,13},{10,... | collective-permute-start | bytes 786440 | tf_op jit(solution)/shard_map/ppermute | solution.py:233
  27.4 9.0 %collective-permute-start.9 = (bf16[256,512]{1,0:T(8,128)(2,1)S(1)}, bf16[256,512]{1,0:T(8,128)(2,1)S(1)}, u32[]{:S(2)}, u32[]{:S(2)}) collective-permute-start(bf16[256,512]{1,0:T(8,128)(2,1)S(1)} %add_convert_fusion), channel_id=1, source_target_pairs={{0,4},{1,3},{2,6},{3,1},{4,0},{5,7},{6,2},{7,5},{8,12},{9,11},{10,... | collective-permute-start | bytes 786440 | tf_op jit(solution)/shard_map/ppermute | solution.py:233
  33.0 6.9 %collective-permute-start.10 = (bf16[256,512]{1,0:T(8,128)(2,1)S(1)}, bf16[256,512]{1,0:T(8,128)(2,1)S(1)}, u32[]{:S(2)}, u32[]{:S(2)}) collective-permute-start(bf16[256,512]{1,0:T(8,128)(2,1)S(1)} %multiply_convert_fusion.1.resid_ref), channel_id=1, source_target_pairs={{0,4},{1,3},{2,6},{3,1},{4,0},{5,7},{6,2},{7,5},{8,12},{9,11},{10,... | collective-permute-start | bytes 786440 | tf_op jit(solution)/shard_map/ppermute | solution.py:233
  36.6 9.2 %collective-permute-start.11 = (bf16[256,512]{1,0:T(8,128)(2,1)S(1)}, bf16[256,512]{1,0:T(8,128)(2,1)S(1)}, u32[]{:S(2)}, u32[]{:S(2)}) collective-permute-start(bf16[256,512]{1,0:T(8,128)(2,1)S(1)} %multiply_convert_fusion.resid_ref), channel_id=1, source_target_pairs={{0,4},{1,3},{2,6},{3,1},{4,0},{5,7},{6,2},{7,5},{8,12},{9,11},{10,... | collective-permute-start | bytes 786440 | tf_op jit(solution)/shard_map/ppermute | solution.py:233
  37.9 10.7 %collective-permute-start.12 = (bf16[256,512]{1,0:T(8,128)(2,1)S(1)}, bf16[256,512]{1,0:T(8,128)(2,1)S(1)}, u32[]{:S(2)}, u32[]{:S(2)}) collective-permute-start(bf16[256,512]{1,0:T(8,128)(2,1)S(1)} %multiply_convert_fusion.1.resid_ref), channel_id=1, source_target_pairs={{0,2},{1,5},{2,0},{3,7},{4,6},{5,1},{6,4},{7,3},{8,10},{9,13},{10,... | collective-permute-start | bytes 786440 | tf_op jit(solution)/shard_map/ppermute | solution.py:233
  38.9 11.0 %collective-permute-start.13 = (bf16[256,512]{1,0:T(8,128)(2,1)S(1)}, bf16[256,512]{1,0:T(8,128)(2,1)S(1)}, u32[]{:S(2)}, u32[]{:S(2)}) collective-permute-start(bf16[256,512]{1,0:T(8,128)(2,1)S(1)} %multiply_convert_fusion.resid_ref), channel_id=1, source_target_pairs={{0,2},{1,5},{2,0},{3,7},{4,6},{5,1},{6,4},{7,3},{8,10},{9,13},{10,... | collective-permute-start | bytes 786440 | tf_op jit(solution)/shard_map/ppermute | solution.py:233
  40.0 11.1 %collective-permute-start.14 = (bf16[256,512]{1,0:T(8,128)(2,1)S(1)}, bf16[256,512]{1,0:T(8,128)(2,1)S(1)}, u32[]{:S(2)}, u32[]{:S(2)}) collective-permute-start(bf16[256,512]{1,0:T(8,128)(2,1)S(1)} %collective-permute-done.10.resid_ref), channel_id=1, source_target_pairs={{0,2},{1,5},{2,0},{3,7},{4,6},{5,1},{6,4},{7,3},{8,10},{9,13},{10,... | collective-permute-start | bytes 786440 | tf_op jit(solution)/shard_map/ppermute | solution.py:233
  45.8 7.0 %collective-permute-start.15 = (bf16[256,512]{1,0:T(8,128)(2,1)S(1)}, bf16[256,512]{1,0:T(8,128)(2,1)S(1)}, u32[]{:S(2)}, u32[]{:S(2)}) collective-permute-start(bf16[256,512]{1,0:T(8,128)(2,1)S(1)} %collective-permute-done.11.resid_ref), channel_id=1, source_target_pairs={{0,2},{1,5},{2,0},{3,7},{4,6},{5,1},{6,4},{7,3},{8,10},{9,13},{10,... | collective-permute-start | bytes 786440 | tf_op jit(solution)/shard_map/ppermute | solution.py:233
  53.8 4.7 %collective-permute-start.16 = (f32[4,1024]{1,0:T(4,128)S(1)}, f32[4,1024]{1,0:T(4,128)S(1)}, u32[]{:S(2)}, u32[]{:S(2)}) collective-permute-start(f32[4,1024]{1,0:T(4,128)S(1)} %get-tuple-element.24), channel_id=1, source_target_pairs={{0,16},{8,24},{16,0},{24,8},{1,17},{9,25},{17,1},{25,9},{2,18},{10... | collective-permute-start | bytes 49160 | tf_op jit(solution)/shard_map/ppermute | solution.py:236
  58.6 3.7 %collective-permute-start.17 = (f32[2,1024]{1,0:T(2,128)S(1)}, f32[2,1024]{1,0:T(2,128)S(1)}, u32[]{:S(2)}, u32[]{:S(2)}) collective-permute-start(f32[2,1024]{1,0:T(2,128)S(1)} %slice.17), channel_id=1, source_target_pairs={{0,8},{8,0},{16,24},{24,16},{1,9},{9,1},{17,25},{25,17},{2,10},{10... | collective-permute-start | bytes 24584 | tf_op jit(solution)/shard_map/ppermute | solution.py:236
  62.3 1.2 %collective-permute-start.18 = (f32[2,512]{1,0:T(2,128)S(1)}, f32[2,512]{1,0:T(2,128)S(1)}, u32[]{:S(2)}, u32[]{:S(2)}) collective-permute-start(f32[2,512]{1,0:T(2,128)S(1)} %slice.19), channel_id=1, source_target_pairs={{0,1},{1,0},{2,3},{3,2},{4,5},{5,4},{6,7},{7,6},{8,9},{9,8},{10,11... | collective-permute-start | bytes 12296 | tf_op jit(solution)/shard_map/ppermute | solution.py:320
